TPU v7x, 32 devices: a whole 2x2x4 slice. The times are simulated.
32 devices in a mesh: dp: 16 (over z, y, core), mp: 2 (over x).
Axes of the slice: x: 2, y: 2, z: 4, core: 2. Of those that a mesh axis runs over, the one named last changes fastest.
Arguments:
- hidden_in: bfloat16 [8192, 2048], P('dp', 'mp'), may hold values from -6 to 6
- doc_starts: int32 [16, 2], replicated, may hold values from 1 to 511, as said below
- attn_gain: bfloat16 [2048], P('dp'), may hold values from 0.25 to 1.75
- w_query: bfloat16 [2048, 2048], P('dp', 'mp'), may hold values from -0.125 to 0.125
- w_key: bfloat16 [2048, 512], P('dp', 'mp'), may hold values from -0.125 to 0.125
- w_value: bfloat16 [2048, 512], P('dp', 'mp'), may hold values from -0.125 to 0.125
- query_gain: bfloat16 [64], replicated, may hold values from 0.25 to 1.75
- key_gain: bfloat16 [64], replicated, may hold values from 0.25 to 1.75
- w_out: bfloat16 [2048, 2048], P('mp', 'dp'), may hold values from -0.5 to 0.5
- mlp_gain: bfloat16 [2048], P('dp'), may hold values from 0.25 to 1.75
- w_gate: bfloat16 [2048, 8192], P('dp', 'mp'), may hold values from -0.125 to 0.125
- w_up: bfloat16 [2048, 8192], P('dp', 'mp'), may hold values from -0.125 to 0.125
- w_down: bfloat16 [8192, 2048], P('mp', 'dp'), may hold values from -0.125 to 0.125
- cotangent: bfloat16 [8192, 2048], P('dp', 'mp'), may hold values from -12 to 12
Outputs:
- block_out: bfloat16 [8192, 2048], P('dp', 'mp')
- d_input: float32 [8192, 2048], P('dp', 'mp')
- d_attn_gain: float32 [2048], P('dp')
- d_query: float32 [2048, 2048], P('dp', 'mp')
- d_key: float32 [2048, 512], P('dp', 'mp')
- d_value: float32 [2048, 512], P('dp', 'mp')
- d_query_gain: float32 [64], replicated
- d_key_gain: float32 [64], replicated
- d_out_proj: float32 [2048, 2048], P('mp', 'dp')
- d_mlp_gain: float32 [2048], P('dp')
- d_gate: float32 [2048, 8192], P('dp', 'mp')
- d_up: float32 [2048, 8192], P('dp', 'mp')
- d_down: float32 [8192, 2048], P('mp', 'dp')
Inputs may be any that keep to these rules, and one draw needn't show every extreme that they name: `doc_starts`: in each row the first number is at most the second; documents may be empty.
All inputs are finite; a program needn't handle non-finite values.
Results may differ from a plain program's by a relative error of at most 0.017.
Values may be sent and summed in bfloat16 or wider, within the bound.
A program may use at most 256 MiB of HBM per device.

v0:
```python
from functools import partial
import math

import jax
import jax.numpy as jnp
from jax import lax
from jax.sharding import PartitionSpec as P


def rms_rows(v, gain):
    return v * lax.rsqrt(jnp.mean(v * v, axis=-1, keepdims=True) + 1e-05) * gain


def document_of(position, cut_row):
    return (position >= cut_row[0]).astype(jnp.int32) + (position >= cut_row[1]).astype(jnp.int32)


def tables(cut_row, length, head_dim):
    position = jnp.arange(length, dtype=jnp.int32)
    doc = document_of(position, cut_row)
    starts = jnp.where(doc == 0, 0, jnp.where(doc == 1, cut_row[0], cut_row[1]))
    places = (position - starts).astype(jnp.float32)
    freqs = jnp.exp(
        -math.log(1000000.0) * 2.0 * jnp.arange(head_dim // 2, dtype=jnp.float32) / head_dim
    )
    angles = places[:, None] * freqs[None, :]
    angles = jnp.concatenate([angles, angles], axis=-1)
    allowed = (doc[:, None] == doc[None, :]) & (position[None, :] <= position[:, None])
    return (jnp.cos(angles)[:, None, :], jnp.sin(angles)[:, None, :], allowed)


def rotate(v, cosine, sine_table):
    halfway = v.shape[-1] // 2
    turned = jnp.concatenate([-v[..., halfway:], v[..., :halfway]], axis=-1)
    return v * cosine + turned * sine_table


def head_piece(pre, gain, cosine, sine_table):
    shaped = pre.reshape(pre.shape[0], pre.shape[1] // gain.shape[0], gain.shape[0])
    return rotate(rms_rows(shaped, gain), cosine, sine_table)


def transpose_dot(left, right):
    return lax.dot_general(
        left, right, (((1,), (1,)), ((), ())), preferred_element_type=jnp.float32
    )


def rows_dot(left, right):
    return lax.dot_general(
        left, right, (((0,), (0,)), ((), ())), preferred_element_type=jnp.float32
    )


def attend_head(inputs, allowed, scale):
    queries, keys, values = inputs
    scores = jnp.einsum("qgd,td->gqt", queries, keys, preferred_element_type=jnp.float32) * scale
    scores = jnp.where(allowed[None], scores, -1e30)
    highest = jnp.max(scores, axis=-1, keepdims=True)
    weights_exp = jnp.exp(scores - highest)
    totals = jnp.sum(weights_exp, axis=-1, keepdims=True)
    probs = weights_exp / totals
    log_norm = highest[..., 0] + jnp.log(totals[..., 0])
    outputs = jnp.einsum(
        "gqt,td->qgd", probs.astype(jnp.bfloat16), values, preferred_element_type=jnp.float32
    )
    return (outputs.astype(jnp.bfloat16), log_norm)


def grad_head(inputs, allowed, scale):
    queries, keys, values, d_outputs, log_norm = inputs
    scores = jnp.einsum("qgd,td->gqt", queries, keys, preferred_element_type=jnp.float32) * scale
    scores = jnp.where(allowed[None], scores, -1e30)
    probs = jnp.exp(scores - log_norm[..., None])
    d_probs = jnp.einsum("qgd,td->gqt", d_outputs, values, preferred_element_type=jnp.float32)
    inner_sum = jnp.sum(probs * d_probs, axis=-1, keepdims=True)
    d_scores = (probs * (d_probs - inner_sum)).astype(jnp.bfloat16)
    d_queries = (
        jnp.einsum("gqt,td->qgd", d_scores, keys, preferred_element_type=jnp.float32) * scale
    )
    d_keys = (
        jnp.einsum("gqt,qgd->td", d_scores, queries, preferred_element_type=jnp.float32) * scale
    )
    d_values = jnp.einsum(
        "gqt,qgd->td", probs.astype(jnp.bfloat16), d_outputs, preferred_element_type=jnp.float32
    )
    return (d_queries, d_keys, d_values)


def body(
    hidden_in,
    doc_starts,
    attn_gain,
    w_query,
    w_key,
    w_value,
    query_gain,
    key_gain,
    w_out,
    mlp_gain,
    w_gate,
    w_up,
    w_down,
    cotangent,
):
    length = hidden_in.shape[0]
    width_part = hidden_in.shape[1]
    offset = lax.axis_index("mp") * width_part
    head_dim = query_gain.shape[0]
    scale = head_dim ** (-0.5)
    dp_index = lax.axis_index("dp")
    cut_row = lax.dynamic_slice_in_dim(doc_starts, dp_index, 1, 0)[0]
    cosine, sine_table, allowed = tables(cut_row, length, head_dim)
    q_gain = query_gain.astype(jnp.float32)
    k_gain = key_gain.astype(jnp.float32)
    full_in, grad_full = (
        lax.all_gather(hidden_in, "mp", axis=1, tiled=True),
        lax.all_gather(cotangent, "mp", axis=1, tiled=True),
    )
    resid = full_in.astype(jnp.float32)
    gain_one, query_cols, key_cols, value_cols, out_rows = (
        lax.all_gather(attn_gain, "dp", axis=0, tiled=True),
        lax.all_gather(w_query, "dp", axis=0, tiled=True),
        lax.all_gather(w_key, "dp", axis=0, tiled=True),
        lax.all_gather(w_value, "dp", axis=0, tiled=True),
        lax.all_gather(w_out, "dp", axis=1, tiled=True),
    )
    normed_one = rms_rows(resid, gain_one.astype(jnp.float32)).astype(jnp.bfloat16)
    query_pre = jnp.dot(normed_one, query_cols, preferred_element_type=jnp.float32)
    key_pre = jnp.dot(normed_one, key_cols, preferred_element_type=jnp.float32)
    value_low = jnp.dot(normed_one, value_cols, preferred_element_type=jnp.float32).astype(
        jnp.bfloat16
    )
    q_heads = query_cols.shape[1] // head_dim
    kv_heads = key_cols.shape[1] // head_dim
    group = q_heads // kv_heads
    query_rot = head_piece(query_pre, q_gain, cosine, sine_table).astype(jnp.bfloat16)
    key_rot = head_piece(key_pre, k_gain, cosine, sine_table).astype(jnp.bfloat16)
    query_stack = jnp.moveaxis(query_rot.reshape(length, kv_heads, group, head_dim), 1, 0)
    key_stack = jnp.moveaxis(key_rot, 1, 0)
    value_stack = jnp.moveaxis(value_low.reshape(length, kv_heads, head_dim), 1, 0)
    attended, log_norm = lax.map(
        partial(attend_head, allowed=allowed, scale=scale), (query_stack, key_stack, value_stack)
    )
    mixed = jnp.moveaxis(attended, 0, 1).reshape(length, q_heads * head_dim)
    attn_total = lax.psum(jnp.dot(mixed, out_rows, preferred_element_type=jnp.float32), "mp")
    middle = resid + attn_total
    gain_two, gate_cols, up_cols, down_rows = (
        lax.all_gather(mlp_gain, "dp", axis=0, tiled=True),
        lax.all_gather(w_gate, "dp", axis=0, tiled=True),
        lax.all_gather(w_up, "dp", axis=0, tiled=True),
        lax.all_gather(w_down, "dp", axis=1, tiled=True),
    )
    normed_two = rms_rows(middle, gain_two.astype(jnp.float32)).astype(jnp.bfloat16)
    gate_pre = jnp.dot(normed_two, gate_cols, preferred_element_type=jnp.float32)
    up_pre = jnp.dot(normed_two, up_cols, preferred_element_type=jnp.float32)
    inner_act = (jax.nn.silu(gate_pre) * up_pre).astype(jnp.bfloat16)
    mlp_half = lax.psum_scatter(
        jnp.dot(inner_act, down_rows, preferred_element_type=jnp.float32).astype(jnp.bfloat16),
        "mp",
        scatter_dimension=1,
        tiled=True,
    ).astype(jnp.float32)
    block_out = (lax.dynamic_slice_in_dim(middle, offset, width_part, 1) + mlp_half).astype(
        jnp.bfloat16
    )
    gain_two, gate_cols, up_cols, down_rows = (
        lax.all_gather(mlp_gain, "dp", axis=0, tiled=True),
        lax.all_gather(w_gate, "dp", axis=0, tiled=True),
        lax.all_gather(w_up, "dp", axis=0, tiled=True),
        lax.all_gather(w_down, "dp", axis=1, tiled=True),
    )
    d_inner = transpose_dot(grad_full, down_rows)
    d_down_part = rows_dot(inner_act, grad_full)
    sigmoid_gate = jax.nn.sigmoid(gate_pre)
    d_gate_pre = (d_inner * up_pre * sigmoid_gate * (1.0 + gate_pre * (1.0 - sigmoid_gate))).astype(
        jnp.bfloat16
    )
    d_up_pre = (d_inner * jax.nn.silu(gate_pre)).astype(jnp.bfloat16)
    d_normed_two = lax.psum(
        transpose_dot(d_gate_pre, gate_cols) + transpose_dot(d_up_pre, up_cols), "mp"
    )
    unused_two, middle_pull = jax.vjp(rms_rows, middle, gain_two.astype(jnp.float32))
    d_middle_norm, d_gain_two = middle_pull(d_normed_two)
    d_gate, d_up = (
        lax.psum_scatter(rows_dot(normed_two, d_gate_pre), "dp", scatter_dimension=0, tiled=True),
        lax.psum_scatter(rows_dot(normed_two, d_up_pre), "dp", scatter_dimension=0, tiled=True),
    )
    d_middle = grad_full.astype(jnp.float32) + d_middle_norm
    gain_one, query_cols, key_cols, value_cols, out_rows = (
        lax.all_gather(attn_gain, "dp", axis=0, tiled=True),
        lax.all_gather(w_query, "dp", axis=0, tiled=True),
        lax.all_gather(w_key, "dp", axis=0, tiled=True),
        lax.all_gather(w_value, "dp", axis=0, tiled=True),
        lax.all_gather(w_out, "dp", axis=1, tiled=True),
    )
    d_middle_low = d_middle.astype(jnp.bfloat16)
    d_mixed = transpose_dot(d_middle_low, out_rows).astype(jnp.bfloat16)
    d_out_part = rows_dot(mixed, d_middle_low)
    d_mixed_stack = jnp.moveaxis(d_mixed.reshape(length, kv_heads, group, head_dim), 1, 0)
    d_query_stack, d_key_stack, d_value_stack = lax.map(
        partial(grad_head, allowed=allowed, scale=scale),
        (query_stack, key_stack, value_stack, d_mixed_stack, log_norm),
    )
    d_query_rot = jnp.moveaxis(d_query_stack, 0, 1).reshape(length, q_heads, head_dim)
    d_key_rot = jnp.moveaxis(d_key_stack, 0, 1)
    d_value_low = (
        jnp.moveaxis(d_value_stack, 0, 1).reshape(length, kv_heads * head_dim).astype(jnp.bfloat16)
    )
    rotary_piece = partial(head_piece, cosine=cosine, sine_table=sine_table)
    unused_query, query_pull = jax.vjp(rotary_piece, query_pre, q_gain)
    d_query_pre, d_qgain_part = query_pull(d_query_rot)
    unused_key, key_pull = jax.vjp(rotary_piece, key_pre, k_gain)
    d_key_pre, d_kgain_part = key_pull(d_key_rot)
    d_query_pre = d_query_pre.astype(jnp.bfloat16)
    d_key_pre = d_key_pre.astype(jnp.bfloat16)
    d_query_part = rows_dot(normed_one, d_query_pre)
    d_key_part = rows_dot(normed_one, d_key_pre)
    d_value_part = rows_dot(normed_one, d_value_low)
    d_normed_one = lax.psum(
        (
            transpose_dot(d_query_pre, query_cols)
            + transpose_dot(d_key_pre, key_cols)
            + transpose_dot(d_value_low, value_cols)
        ).astype(jnp.bfloat16),
        "mp",
    ).astype(jnp.float32)
    unused_one, input_pull = jax.vjp(rms_rows, resid, gain_one.astype(jnp.float32))
    d_resid_norm, d_gain_one = input_pull(d_normed_one)
    d_total = d_middle + d_resid_norm
    d_input = lax.dynamic_slice_in_dim(d_total, offset, width_part, 1)
    d_attn_gain, d_mlp_gain, d_query, d_key, d_value, d_out_proj, d_down = (
        lax.psum_scatter(d_gain_one, "dp", scatter_dimension=0, tiled=True),
        lax.psum_scatter(d_gain_two, "dp", scatter_dimension=0, tiled=True),
        lax.psum_scatter(d_query_part, "dp", scatter_dimension=0, tiled=True),
        lax.psum_scatter(d_key_part, "dp", scatter_dimension=0, tiled=True),
        lax.psum_scatter(d_value_part, "dp", scatter_dimension=0, tiled=True),
        lax.psum_scatter(d_out_part, "dp", scatter_dimension=1, tiled=True),
        lax.psum_scatter(d_down_part, "dp", scatter_dimension=1, tiled=True),
    )
    d_query_gain, d_key_gain = lax.psum((d_qgain_part, d_kgain_part), ("dp", "mp"))
    return (
        block_out,
        d_input,
        d_attn_gain,
        d_query,
        d_key,
        d_value,
        d_query_gain,
        d_key_gain,
        d_out_proj,
        d_mlp_gain,
        d_gate,
        d_up,
        d_down,
    )


def solution(mesh):
    return jax.shard_map(
        body,
        mesh=mesh,
        in_specs=(
            P("dp", "mp"),
            P(),
            P("dp"),
            P("dp", "mp"),
            P("dp", "mp"),
            P("dp", "mp"),
            P(),
            P(),
            P("mp", "dp"),
            P("dp"),
            P("dp", "mp"),
            P("dp", "mp"),
            P("mp", "dp"),
            P("dp", "mp"),
        ),
        out_specs=(
            P("dp", "mp"),
            P("dp", "mp"),
            P("dp"),
            P("dp", "mp"),
            P("dp", "mp"),
            P("dp", "mp"),
            P(),
            P(),
            P("mp", "dp"),
            P("dp"),
            P("dp", "mp"),
            P("dp", "mp"),
            P("mp", "dp"),
        ),
        check_vma=False,
    )
```

profile of v0, /device:TPU:0, one launch (start us, length us, event | category | flops | bytes accessed | tf_op | source)
XLA Modules:
  0.0 2416.3 jit_solution(7327366560324740621)
XLA Ops:
  13.9 23.2 all-gather
  39.3 6.1 all-gather.12.cloned.1.call-done
  45.4 2.1 multiply_reduce_fusion.4
  47.5 38.0 %all-gather.16.cloned.1.call-done = bf16[2048,256]{1,0:T(8,128)(2,1)} async-done(((bf16[128,256]{1,0:T(8,128)(2,1)}), bf16[2048,256]{1,0:T(8,128)(2,1)}) %all-gather.16.cloned.1.call-update) | async-done | bytes 1048592 | tf_op jit(solution)/shard_map/all_gather | solution.py:124
  85.6 2.9 multiply_reduce_fusion.10
  89.5 35.1 %all-gather.14.cloned.1.call-done = bf16[2048,256]{1,0:T(8,128)(2,1)} async-done(((bf16[128,256]{1,0:T(8,128)(2,1)}), bf16[2048,256]{1,0:T(8,128)(2,1)}) %all-gather.14.cloned.1.call-update) | async-done | bytes 1048592 | tf_op jit(solution)/shard_map/all_gather | solution.py:125
  124.6 2.9 convolution_convert_fusion.2
  127.5 48.7 %all-gather.18.cloned.1.call-done = bf16[2048,1024]{1,0:T(8,128)(2,1)} async-done(((bf16[128,1024]{1,0:T(8,128)(2,1)}), bf16[2048,1024]{1,0:T(8,128)(2,1)}) %all-gather.18.cloned.1.call-update) | async-done | bytes 4194320 | tf_op jit(solution)/shard_map/all_gather | solution.py:123
  176.1 5.3 multiply_reduce_fusion.7
  183.9 22.8 while.28
  187.1 2.9 fusion.169
  192.6 2.9 fusion.169
  198.2 2.9 fusion.169
  203.7 2.9 fusion.169
  206.7 23.2 all-gather.20.cloned.1.call-done
  229.9 6.9 fusion.100
  239.7 18.6 all-gather.1
  258.3 84.7 %all-reduce.12.cloned.1.call-done = f32[512,2048]{1,0:T(8,128)} async-done(((f32[512,2048]{1,0:T(8,128)}), f32[512,2048]{1,0:T(8,128)}) %all-reduce.12.cloned.1.call-update) | async-done | bytes 4194320 | tf_op jit(solution)/shard_map/psum | solution.py:146
  343.0 2.9 multiply_reduce_fusion.3
  345.9 2.0 copy-done.2
  348.3 124.0 %all-gather.22.cloned.1.call-done = bf16[2048,4096]{1,0:T(8,128)(2,1)} async-done(((bf16[128,4096]{1,0:T(8,128)(2,1)}), bf16[2048,4096]{1,0:T(8,128)(2,1)}) %all-gather.22.cloned.1.call-update) | async-done | bytes 16777232 | tf_op jit(solution)/shard_map/all_gather | solution.py:150
  472.3 14.7 fusion.101
  487.0 112.8 %all-gather.24.cloned.1.call-done = bf16[2048,4096]{1,0:T(8,128)(2,1)} async-done(((bf16[128,4096]{1,0:T(8,128)(2,1)}), bf16[2048,4096]{1,0:T(8,128)(2,1)}) %all-gather.24.cloned.1.call-update) | async-done | bytes 16777232 | tf_op jit(solution)/shard_map/all_gather | solution.py:151
  599.8 14.5 fusion.102
  614.3 18.4 all-gather.28.cloned.1.call-done
  632.8 132.6 %all-gather.26.cloned.1.call-done = bf16[4096,2048]{1,0:T(8,128)(2,1)} async-done(((bf16[4096,128]{1,0:T(8,128)(2,1)}), bf16[4096,2048]{1,0:T(8,128)(2,1)}) %all-gather.26.cloned.1.call-update) | async-done | bytes 16777232 | tf_op jit(solution)/shard_map/all_gather | solution.py:152
  765.4 20.4 multiply_convert_fusion
  785.8 16.6 fusion.103
  802.4 14.6 convolution_add_fusion
  817.1 15.3 convolution_convert_fusion
  832.8 90.4 %all-reduce.14.cloned.1.call-done = f32[512,2048]{1,0:T(8,128)} async-done(((f32[512,2048]{1,0:T(8,128)}), f32[512,2048]{1,0:T(8,128)}) %all-reduce.14.cloned.1.call-update) | async-done | bytes 4194320 | tf_op jit(solution)/shard_map/psum | solution.py:180
  923.2 5.2 multiply_reduce_fusion
  930.3 2.2 copy-done.9
  932.5 3.4 convolution_convert_fusion.1
  935.9 1.5 copy.53
  937.5 36.7 %while.29 = (s32[]{:T(128)}, f32[4,512,4,64]{1,3,2,0:T(8,128)}, f32[4,512,64]{1,2,0:T(8,128)}, bf16[4,512,64]{1,2,0:T(8,128)(2,1)S(1)}, bf16[4,512,64]{1,2,0:T(8...) while((s32[]{:T(128)}, f32[4,512,4,64]{1,3,2,0:T(8,128)}, ...), condition=%wide.region_14.15_spmd.clone, body=%wide.region_12.14_spmd.clone.sunk | while | flops 687765504 | bytes 34602096 | solution.py:201
  939.1 2.3 fusion.180
  944.0 1.4 fusion.183
  948.3 2.3 fusion.180
  953.1 1.4 fusion.183
  957.4 2.3 fusion.180
  962.2 1.4 fusion.183
  966.5 2.3 fusion.180
  971.4 1.4 fusion.183
  983.1 2.4 fusion.104
  985.6 2.1 add_convert_fusion
  987.8 2.4 fusion.91
  990.3 3.3 fusion.90
  993.7 5.9 fusion.92
  1000.8 7.9 fusion.76
  1008.8 18.7 fusion.106
  1027.6 18.0 fusion.107
  1045.9 18.4 fusion.108
  1066.2 2.5 convert_element_type.137
  1068.7 39.9 %all-reduce.6 = (f32[64]{0:T(128)}, f32[64]{0:T(128)}) all-reduce(f32[64]{0:T(128)S(1)} %get-tuple-element.154, f32[64]{0:T(128)S(1)} %get-tuple-element.156), channel_id=1, replica_groups=mesh['dp'=16,'mp'=2] {'dp','mp'}, use_global_device_ids=true, to_apply=%region_25.26 | all-reduce | flops 128 | bytes 1024 | tf_op jit(solution)/shard_map/psum | solution.py:241
  1108.6 3.3 add_convert_fusion.1
  1111.8 5.4 fusion.67
  1117.2 59.9 %all-reduce.7 = (f32[2048]{0:T(1024)S(1)}, f32[2048]{0:T(1024)S(1)}) all-reduce(f32[2048]{0:T(1024)S(1)} %get-tuple-element.152, f32[2048]{0:T(1024)S(1)} %copy-done.44), channel_id=3, replica_groups=mesh['dp'=16,'mp'=2] {'dp'}, use_global_device_ids=true, to_apply=%region_20.21.clone | all-reduce | flops 4096 | bytes 32768
  1178.3 4.6 fusion.70
  1182.9 107.0 %reduce-scatter.11.cloned.1.call-done = f32[128,1024]{1,0:T(8,128)} async-done(((f32[2048,1024]{1,0:T(8,128)}), f32[128,1024]{1,0:T(8,128)}) %reduce-scatter.11.cloned.1.call-update) | async-done | bytes 524304 | tf_op jit(solution)/shard_map/reduce_scatter | solution.py:235
  1289.9 109.1 %reduce-scatter.17.cloned.1.call-done = f32[1024,128]{1,0:T(8,128)} async-done(((f32[1024,2048]{1,0:T(8,128)}), f32[1024,128]{1,0:T(8,128)}) %reduce-scatter.17.cloned.1.call-update) | async-done | bytes 524304 | tf_op jit(solution)/shard_map/reduce_scatter | solution.py:238
  1399.0 337.0 %reduce-scatter.19.cloned.1.call-done = f32[128,4096]{1,0:T(8,128)} async-done(((f32[2048,4096]{1,0:T(8,128)}), f32[128,4096]{1,0:T(8,128)}) %reduce-scatter.19.cloned.1.call-update) | async-done | bytes 2097168 | tf_op jit(solution)/shard_map/reduce_scatter | solution.py:186
  1736.0 336.5 %reduce-scatter.21.cloned.1.call-done = f32[128,4096]{1,0:T(8,128)} async-done(((f32[2048,4096]{1,0:T(8,128)}), f32[128,4096]{1,0:T(8,128)}) %reduce-scatter.21.cloned.1.call-update) | async-done | bytes 2097168 | tf_op jit(solution)/shard_map/reduce_scatter | solution.py:187
  2072.5 336.5 %reduce-scatter.23.cloned.1.call-done = f32[4096,128]{1,0:T(8,128)} async-done(((f32[4096,2048]{1,0:T(8,128)}), f32[4096,128]{1,0:T(8,128)}) %reduce-scatter.23.cloned.1.call-update) | async-done | bytes 2097168 | tf_op jit(solution)/shard_map/reduce_scatter | solution.py:239
  (243 shorter events, 62.7 us)
Async XLA Ops:
  7.2 3.5 copy-start
  7.2 38.2 %all-gather.12.cloned.1.call-start = ((), (), s32[]{:S(2)}) async-start(), calls=%async_computation.8 | async-start | bytes 3145728 | tf_op jit(solution)/shard_map/all_gather | solution.py:117
  7.9 77.6 %all-gather.16.cloned.1.call-start = ((), (), s32[]{:S(2)}) async-start(), calls=%async_computation.10 | async-start | bytes 1114112 | tf_op jit(solution)/shard_map/all_gather | solution.py:124
  8.7 115.9 %all-gather.14.cloned.1.call-start = ((), (), s32[]{:S(2)}) async-start(), calls=%async_computation.9 | async-start | bytes 1114112 | tf_op jit(solution)/shard_map/all_gather | solution.py:125
  9.4 166.7 %all-gather.18.cloned.1.call-start = ((), (), s32[]{:S(2)}) async-start(), calls=%async_computation.11 | async-start | bytes 4456448 | tf_op jit(solution)/shard_map/all_gather | solution.py:123
  10.0 219.9 %all-gather.20.cloned.1.call-start = ((), (), s32[]{:S(2)}) async-start(), calls=%async_computation.12 | async-start | bytes 4456448 | tf_op jit(solution)/shard_map/all_gather | solution.py:126
  10.6 332.4 %all-reduce.12.cloned.1.call-start = ((), (), s32[]{:S(2)}) async-start(), calls=%async_computation.13 | async-start | bytes 8388608 | tf_op jit(solution)/shard_map/psum | solution.py:146
  37.1 139.1 %copy-start.42 = (f32[16,1,128]{2,1,0:T(1,128)}, f32[16,1,128]{2,1,0:T(1,128)S(1)}, u32[]{:S(2)}) copy-start(f32[16,1,128]{2,1,0:T(1,128)S(1)} %convert_element_type.168) | copy-start | bytes 24580
  38.6 50.2 %copy-start.22 = (f32[512,64]{0,1:T(8,128)}, f32[512,64]{0,1:T(8,128)S(1)}, u32[]{:S(2)}) copy-start(f32[512,64]{0,1:T(8,128)S(1)} %get-tuple-element.217) | copy-start | bytes 393220
  38.6 144.4 %copy-start.20 = (f32[512,64]{0,1:T(8,128)}, f32[512,64]{0,1:T(8,128)S(1)}, u32[]{:S(2)}) copy-start(f32[512,64]{0,1:T(8,128)S(1)} %get-tuple-element.216) | copy-start | bytes 393220
  39.3 49.5 %copy-start.49 = (f32[64]{0:T(128)}, f32[64]{0:T(128)S(1)}, u32[]{:S(2)}) copy-start(f32[64]{0:T(128)S(1)} %convert_element_type.143) | copy-start | bytes 772
  47.5 41.1 %copy-start.45 = (f32[512]{0:T(512)}, f32[512]{0:T(512)S(1)}, u32[]{:S(2)}) copy-start(f32[512]{0:T(512)S(1)} %multiply_reduce_fusion.4) | copy-start | bytes 6148
  47.5 128.6 %copy-start.47 = (f32[512]{0:T(512)}, f32[512]{0:T(512)S(1)}, u32[]{:S(2)}) copy-start(f32[512]{0:T(512)S(1)} %fusion.88) | copy-start | bytes 6148
  85.6 39.1 %copy-start.6 = (bf16[512,2048]{1,0:T(8,128)(2,1)S(1)}, bf16[512,2048]{1,0:T(8,128)(2,1)}, u32[]{:S(2)}) copy-start(bf16[512,2048]{1,0:T(8,128)(2,1)} %all-gather.12.cloned.1.call-done) | copy-start | bytes 6291460
  88.5 39.0 %copy-start.40 = (f32[512,4]{0,1:T(4,128)}, f32[512,4]{0,1:T(4,128)S(1)}, u32[]{:S(2)}) copy-start(f32[512,4]{0,1:T(4,128)S(1)} %get-tuple-element.220) | copy-start | bytes 24580
  88.6 38.9 %copy-start.35 = (f32[512,4]{0,1:T(4,128)}, f32[512,4]{0,1:T(4,128)S(1)}, u32[]{:S(2)}) copy-start(f32[512,4]{0,1:T(4,128)S(1)} %fusion.87) | copy-start | bytes 24580
  127.5 54.8 %copy-start.51 = (f32[64]{0:T(128)S(1)}, f32[64]{0:T(128)}, u32[]{:S(2)}) copy-start(f32[64]{0:T(128)} %convert_element_type.146) | copy-start | bytes 772
  206.7 30.1 %copy-start.10 = (bf16[4,512,4,64]{1,3,2,0:T(8,128)(2,1)}, bf16[4,512,4,64]{1,3,2,0:T(8,128)(2,1)S(1)}, u32[]{:S(2)}) copy-start(bf16[4,512,4,64]{1,3,2,0:T(8,128)(2,1)S(1)} %get-tuple-element.422) | copy-start | bytes 3145732
  206.7 30.1 %copy-start.18 = (bf16[4,512,64]{1,2,0:T(8,128)(2,1)}, bf16[4,512,64]{1,2,0:T(8,128)(2,1)S(1)}, u32[]{:S(2)}) copy-start(bf16[4,512,64]{1,2,0:T(8,128)(2,1)S(1)} %get-tuple-element.431) | copy-start | bytes 786436
  206.7 30.1 %copy-start.29 = (s32[512]{0:T(512)}, s32[512]{0:T(512)S(1)}, u32[]{:S(2)}) copy-start(s32[512]{0:T(512)S(1)} %get-tuple-element.456) | copy-start | bytes 6148
  236.8 2.9 copy-start.54
  236.8 106.2 %copy-start.7 = (bf16[512,2048]{1,0:T(8,128)(2,1)S(1)}, bf16[512,2048]{1,0:T(8,128)(2,1)}, u32[]{:S(2)}) copy-start(bf16[512,2048]{1,0:T(8,128)(2,1)} %all-gather.12.cloned.1.call-done) | copy-start | bytes 6291460
  236.8 235.5 %all-gather.22.cloned.1.call-start = ((), (), s32[]{:S(2)}) async-start(), calls=%async_computation.14 | async-start | bytes 17825792 | tf_op jit(solution)/shard_map/all_gather | solution.py:150
  237.6 362.2 %all-gather.24.cloned.1.call-start = ((), (), s32[]{:S(2)}) async-start(), calls=%async_computation.15 | async-start | bytes 17825792 | tf_op jit(solution)/shard_map/all_gather | solution.py:151
  238.3 394.4 %all-gather.28.cloned.1.call-start = ((), (), s32[]{:S(2)}) async-start(), calls=%async_computation.18 | async-start | bytes 3145728 | tf_op jit(solution)/shard_map/all_gather | solution.py:118
  239.0 526.3 %all-gather.26.cloned.1.call-start = ((), (), s32[]{:S(2)}) async-start(), calls=%async_computation.16 | async-start | bytes 17825792 | tf_op jit(solution)/shard_map/all_gather | solution.py:152
  239.6 683.6 %all-reduce.14.cloned.1.call-start = ((), (), s32[]{:S(2)}) async-start(), calls=%async_computation.19 | async-start | bytes 8388608 | tf_op jit(solution)/shard_map/psum | solution.py:180
  345.9 2.0 copy-start.2
  348.3 251.5 %copy-start.25 = (bf16[512,2048]{1,0:T(8,128)(2,1)}, bf16[512,2048]{1,0:T(8,128)(2,1)S(1)}, u32[]{:S(2)}) copy-start(bf16[512,2048]{1,0:T(8,128)(2,1)S(1)} %multiply_convert_fusion.3) | copy-start | bytes 6291460
  785.8 16.6 copy-start.57
  817.0 291.6 %reduce-scatter.9.cloned.1.call-start = ((), (), s32[]{:S(2)}) async-start(), calls=%async_computation.17 | async-start | bytes 3145728 | tf_op jit(solution)/shard_map/reduce_scatter | solution.py:158
  832.3 96.1 %copy-start.26 = (bf16[512,2048]{1,0:T(8,128)(2,1)S(1)}, bf16[512,2048]{1,0:T(8,128)(2,1)}, u32[]{:S(2)}) copy-start(bf16[512,2048]{1,0:T(8,128)(2,1)} %all-gather.28.cloned.1.call-done) | copy-start | bytes 6291460
  832.4 279.5 %all-reduce.16.cloned.1.call-start = ((), (), s32[]{:S(2)}) async-start(), calls=%async_computation.20 | async-start | bytes 4194304 | tf_op jit(solution)/shard_map/psum | solution.py:220
  923.2 5.3 copy-start.3
  923.2 5.9 copy-start.12
  929.1 3.4 copy-start.15
  930.3 2.2 copy-start.9
  932.5 4.9 copy-start.11
  932.5 4.9 copy-start.19
  932.5 4.9 copy-start.30
  937.4 36.8 %copy-start.24 = (f32[512,64]{0,1:T(8,128)S(1)}, f32[512,64]{0,1:T(8,128)}, u32[]{:S(2)}) copy-start(f32[512,64]{0,1:T(8,128)} %copy-done.22) | copy-start | bytes 393220
  937.4 38.1 %copy-start.14 = (f32[512,256]{0,1:T(8,128)S(1)}, f32[512,256]{0,1:T(8,128)}, u32[]{:S(2)}) copy-start(f32[512,256]{0,1:T(8,128)} %copy-done.13) | copy-start | bytes 1572868
  937.5 38.1 %copy-start.21 = (f32[512,64]{0,1:T(8,128)S(1)}, f32[512,64]{0,1:T(8,128)}, u32[]{:S(2)}) copy-start(f32[512,64]{0,1:T(8,128)} %copy-done.20) | copy-start | bytes 393220
  937.5 38.1 %copy-start.36 = (f32[512,4]{0,1:T(4,128)S(1)}, f32[512,4]{0,1:T(4,128)}, u32[]{:S(2)}) copy-start(f32[512,4]{0,1:T(4,128)} %copy-done.35) | copy-start | bytes 24580
  937.5 38.1 %copy-start.50 = (f32[64]{0:T(128)S(1)}, f32[64]{0:T(128)}, u32[]{:S(2)}) copy-start(f32[64]{0:T(128)} %copy-done.49) | copy-start | bytes 772
  974.2 3.2 copy-start.33
  974.2 2.8 copy-start.41
  974.2 2.8 copy-start.16
  980.9 2.3 copy-start.55
  983.1 2.4 copy-start.27
  983.1 2.4 copy-start.34
  985.5 2.2 copy-start.8
  985.5 2.2 copy-start.43
  985.6 2.2 copy-start.48
  987.7 195.2 %reduce-scatter.13.cloned.1.call-start = ((), (), s32[]{:S(2)}) async-start(), calls=%async_computation.22 | async-start | bytes 2228224 | tf_op jit(solution)/shard_map/reduce_scatter | solution.py:236
  990.3 192.7 %reduce-scatter.15.cloned.1.call-start = ((), (), s32[]{:S(2)}) async-start(), calls=%async_computation.23 | async-start | bytes 2228224 | tf_op jit(solution)/shard_map/reduce_scatter | solution.py:237
  993.7 296.2 %reduce-scatter.11.cloned.1.call-start = ((), (), s32[]{:S(2)}) async-start(), calls=%async_computation.21 | async-start | bytes 8912896 | tf_op jit(solution)/shard_map/reduce_scatter | solution.py:235
  999.6 399.4 %reduce-scatter.17.cloned.1.call-start = ((), (), s32[]{:S(2)}) async-start(), calls=%async_computation.24 | async-start | bytes 8912896 | tf_op jit(solution)/shard_map/reduce_scatter | solution.py:238
  1008.8 727.3 %reduce-scatter.19.cloned.1.call-start = ((), (), s32[]{:S(2)}) async-start(), calls=%async_computation.25 | async-start | bytes 35651584 | tf_op jit(solution)/shard_map/reduce_scatter | solution.py:186
  1027.5 1045.0 %reduce-scatter.21.cloned.1.call-start = ((), (), s32[]{:S(2)}) async-start(), calls=%async_computation.26 | async-start | bytes 35651584 | tf_op jit(solution)/shard_map/reduce_scatter | solution.py:187
  1045.6 1363.5 %reduce-scatter.23.cloned.1.call-start = ((), (), s32[]{:S(2)}) async-start(), calls=%async_computation.27 | async-start | bytes 35651584 | tf_op jit(solution)/shard_map/reduce_scatter | solution.py:239
  1111.8 5.4 copy-start.44
  1111.8 66.4 %copy-start.46 = (f32[512]{0:T(512)S(1)}, f32[512]{0:T(512)}, u32[]{:S(2)}) copy-start(f32[512]{0:T(512)} %copy-done.45) | copy-start | bytes 6148
  1178.3 1230.8 %copy-start.1 = (s32[16,2]{0,1:T(2,128)S(1)}, s32[16,2]{0,1:T(2,128)}, u32[]{:S(2)}) copy-start(s32[16,2]{0,1:T(2,128)} %param.19) | copy-start | bytes 388
  (14 other events, 17.2 us)
Sparse Core Ops, SparseCore 0:
  9.6 35.7 all-gather.11
  47.6 37.9 all-gather.15
  87.7 36.8 all-gather.13
  126.6 49.4 all-gather.17
  178.1 51.6 all-gather.19
  236.9 106.0 all-reduce.11
  345.4 126.8 all-gather.21
  474.7 125.0 all-gather.23
  601.4 31.2 all-gather.27
  635.0 130.3 all-gather.25
  817.1 106.0 all-reduce.13
  925.9 31.8 reduce-scatter.8
  987.8 62.7 all-reduce.15
  1054.8 61.6 reduce-scatter.12
  1121.1 60.6 reduce-scatter.14
  1186.3 103.5 reduce-scatter.10
  1294.4 104.5 reduce-scatter.16
  1403.7 332.2 reduce-scatter.18
  1740.8 331.6 reduce-scatter.20
  2077.2 331.7 reduce-scatter.22
where the time goes:
time: 2420 us
  waiting for transfers between devices  1950 us (81%)
  matrix products  240 us (10%)
  blocking collectives  141 us (6%)
  other arithmetic  52.3 us (2%)
    reduce_scatter x1, waiting for transfers between devices, body(): lax.psum_scatter(rows_dot(normed_two, d_gate_pre), 'dp', scatter_dimensio...  337 us
    reduce_scatter x1, waiting for transfers between devices, body(): lax.psum_scatter(rows_dot(normed_two, d_up_pre), 'dp', scatter_dimension=...  337 us
    reduce_scatter x1, waiting for transfers between devices, body(): lax.psum_scatter(d_down_part, 'dp', scatter_dimension=1, tiled=True)  336 us
    all_gather x1, waiting for transfers between devices, body(): lax.all_gather(w_down, 'dp', axis=1, tiled=True)  133 us
    all_gather x1, waiting for transfers between devices, body(): lax.all_gather(w_gate, 'dp', axis=0, tiled=True)  124 us
    all_gather x1, waiting for transfers between devices, body(): lax.all_gather(w_up, 'dp', axis=0, tiled=True)  113 us
    reduce_scatter x1, waiting for transfers between devices, body(): lax.psum_scatter(d_out_part, 'dp', scatter_dimension=1, tiled=True)  109 us
    reduce_scatter x1, waiting for transfers between devices, body(): lax.psum_scatter(d_query_part, 'dp', scatter_dimension=0, tiled=True)  107 us
  transfers between devices with their start and end apart: 20, of which 16 were waited for; matrix products, arithmetic and copies ran while one was open for 10% of the time, Pallas kernels for 0%

commit v1 on v0

v1 whole, which is shorter than its diff:
```python
from functools import partial
import math

import jax
import jax.numpy as jnp
from jax import lax
from jax.sharding import Mesh, PartitionSpec as P

BF = jnp.bfloat16
F32 = jnp.float32
EPS = 1e-05
TP = ("i", "m")
ALL = ("t", "i", "m")


def dot_f32(left, right, dims):
    return lax.dot_general(left, right, (dims, ((), ())), preferred_element_type=F32)


def nn(left, right):
    return dot_f32(left, right, ((1,), (0,)))


def nt(left, right):
    return dot_f32(left, right, ((1,), (1,)))


def tn(left, right):
    return dot_f32(left, right, ((0,), (0,)))


def rms_rows(v, gain):
    return v * lax.rsqrt(jnp.mean(v * v, axis=-1, keepdims=True) + EPS) * gain


def tables(cut_row, length, head_dim):
    position = jnp.arange(length, dtype=jnp.int32)
    doc = (position >= cut_row[0]).astype(jnp.int32) + (position >= cut_row[1]).astype(jnp.int32)
    starts = jnp.where(doc == 0, 0, jnp.where(doc == 1, cut_row[0], cut_row[1]))
    places = (position - starts).astype(F32)
    freqs = jnp.exp(-math.log(1000000.0) * 2.0 * jnp.arange(head_dim // 2, dtype=F32) / head_dim)
    angles = places[:, None] * freqs[None, :]
    angles = jnp.concatenate([angles, angles], axis=-1)
    allowed = (doc[:, None] == doc[None, :]) & (position[None, :] <= position[:, None])
    return jnp.cos(angles), jnp.sin(angles), allowed


def rotate(v, cosine, sine_table):
    halfway = v.shape[-1] // 2
    turned = jnp.concatenate([-v[..., halfway:], v[..., :halfway]], axis=-1)
    return v * cosine + turned * sine_table


def head_piece(pre, gain, cosine, sine_table):
    shaped = pre.reshape(pre.shape[0], -1, gain.shape[0])
    return rotate(rms_rows(shaped, gain), cosine, sine_table)


def attend(inputs, scale):
    queries, keys, values, allowed = inputs
    scores = jnp.einsum("qgd,td->gqt", queries, keys, preferred_element_type=F32) * scale
    scores = jnp.where(allowed[None], scores, -1e30)
    highest = jnp.max(scores, axis=-1, keepdims=True)
    weights_exp = jnp.exp(scores - highest)
    totals = jnp.sum(weights_exp, axis=-1, keepdims=True)
    probs = weights_exp / totals
    log_norm = highest[..., 0] + jnp.log(totals[..., 0])
    outputs = jnp.einsum("gqt,td->qgd", probs.astype(BF), values, preferred_element_type=F32)
    return outputs.astype(BF), log_norm


def attend_grad(inputs, scale):
    queries, keys, values, d_outputs, log_norm, allowed = inputs
    scores = jnp.einsum("qgd,td->gqt", queries, keys, preferred_element_type=F32) * scale
    scores = jnp.where(allowed[None], scores, -1e30)
    probs = jnp.exp(scores - log_norm[..., None])
    d_probs = jnp.einsum("qgd,td->gqt", d_outputs, values, preferred_element_type=F32)
    inner_sum = jnp.sum(probs * d_probs, axis=-1, keepdims=True)
    d_scores = (probs * (d_probs - inner_sum)).astype(BF)
    d_queries = jnp.einsum("gqt,td->qgd", d_scores, keys, preferred_element_type=F32) * scale
    d_keys = jnp.einsum("gqt,qgd->td", d_scores, queries, preferred_element_type=F32) * scale
    d_values = jnp.einsum("gqt,qgd->td", probs.astype(BF), d_outputs, preferred_element_type=F32)
    return d_queries, d_keys, d_values


def gather_pieces(piece, ranks):
    rows, cols = piece.shape
    parts = lax.all_gather(piece, TP, axis=0)
    parts = parts.reshape(ranks[0], ranks[1], rows, cols)
    return jnp.moveaxis(parts, 1, 2).reshape(ranks[0] * rows, ranks[1] * cols)


def scatter_pieces(partial_sum, ranks):
    rows, cols = partial_sum.shape
    parts = partial_sum.astype(BF).reshape(ranks[0], rows // ranks[0], ranks[1], cols // ranks[1])
    parts = jnp.moveaxis(parts, 2, 1).reshape(-1, rows // ranks[0], cols // ranks[1])
    mine = lax.psum_scatter(parts, TP, scatter_dimension=0, tiled=False)
    return mine.astype(F32)


def spread(local, inner):
    rows, cols = local.shape
    parts = jnp.moveaxis(local.reshape(rows, inner, cols // inner), 1, 0)
    parts = lax.all_to_all(parts, "i", 0, 0, tiled=False)
    return parts.reshape(inner * rows, cols // inner)


def collect(block, inner):
    rows, cols = block.shape
    parts = lax.all_to_all(block.reshape(inner, rows // inner, cols), "i", 0, 0, tiled=False)
    return jnp.moveaxis(parts, 0, 1).reshape(rows // inner, inner * cols)


def full_rows(local, inner):
    return lax.all_gather(spread(local, inner), "t", axis=0, tiled=True)


def grad_rows(part, inner):
    mine = lax.psum_scatter(part.astype(BF), "t", scatter_dimension=0, tiled=True)
    return collect(mine, inner).astype(F32)


def body(
    hidden_in, doc_starts, attn_gain, w_query, w_key, w_value, query_gain, key_gain,
    w_out, mlp_gain, w_gate, w_up, w_down, cotangent, *, groups, inner, halves,
):
    length, width_part = hidden_in.shape
    ranks = (inner, halves)
    width = width_part * halves
    head_dim = query_gain.shape[0]
    scale = head_dim ** (-0.5)
    t_index, m_index = lax.axis_index("t"), lax.axis_index("m")
    cuts = lax.dynamic_slice_in_dim(doc_starts, t_index * inner, inner, 0)
    cosine, sine_table, allowed = jax.vmap(partial(tables, length=length, head_dim=head_dim))(cuts)
    cosine = cosine.reshape(inner * length, 1, head_dim)
    sine_table = sine_table.reshape(inner * length, 1, head_dim)
    q_gain, k_gain = query_gain.astype(F32), key_gain.astype(F32)
    gains = lax.all_gather(jnp.stack([attn_gain, mlp_gain], 1), ("t", "i"), axis=0, tiled=True)
    gain_one, gain_two = gains[:, 0].astype(F32), gains[:, 1].astype(F32)

    full_in = gather_pieces(hidden_in, ranks)
    sizes = [w.shape[1] // inner for w in (w_query, w_key, w_value)] + [w_out.shape[0] // inner]
    edges = [sum(sizes[:n]) for n in range(5)]

    def by_rank(w):
        return w.reshape(w.shape[0], inner, w.shape[1] // inner)

    attn_local = jnp.concatenate([by_rank(w_query), by_rank(w_key), by_rank(w_value), by_rank(w_out.T)], 2)
    attn_cols = full_rows(attn_local.reshape(attn_local.shape[0], -1), inner)
    query_cols, key_cols, value_cols, out_t = [attn_cols[:, edges[n]:edges[n + 1]] for n in range(4)]
    resid = full_in.astype(F32)
    r_one = lax.rsqrt(jnp.mean(resid * resid, axis=-1, keepdims=True) + EPS)
    normed_one = (resid * r_one * gain_one).astype(BF)
    gate_cols = full_rows(w_gate, inner)
    up_cols = full_rows(w_up, inner)
    down_t = full_rows(w_down.T, inner)
    grad_full = gather_pieces(cotangent, ranks)

    query_pre = nn(normed_one, query_cols)
    key_pre = nn(normed_one, key_cols)
    value_low = nn(normed_one, value_cols).astype(BF)
    query_rot = head_piece(query_pre, q_gain, cosine, sine_table).astype(BF)
    key_rot = head_piece(key_pre, k_gain, cosine, sine_table).astype(BF)
    group = query_rot.shape[1]
    query_stack = query_rot.reshape(inner, length, group, head_dim)
    key_stack = key_rot.reshape(inner, length, head_dim)
    value_stack = value_low.reshape(inner, length, head_dim)
    attended, log_norm = lax.map(partial(attend, scale=scale), (query_stack, key_stack, value_stack, allowed))
    mixed = attended.reshape(inner * length, group * head_dim)
    middle = hidden_in.astype(F32) + scatter_pieces(nt(mixed, out_t), ranks)
    my_gain_one = lax.dynamic_slice_in_dim(gain_one, m_index * width_part, width_part, 0)
    my_gain_two = lax.dynamic_slice_in_dim(gain_two, m_index * width_part, width_part, 0)
    r_two = lax.rsqrt(lax.psum(jnp.sum(middle * middle, axis=-1, keepdims=True), "m") / width + EPS)
    normed_two = gather_pieces((middle * r_two * my_gain_two).astype(BF), ranks)

    gate_pre, up_pre = nn(normed_two, gate_cols), nn(normed_two, up_cols)
    d_inner = nn(grad_full, down_t)
    sigmoid_gate = jax.nn.sigmoid(gate_pre)
    inner_act = (gate_pre * sigmoid_gate * up_pre).astype(BF)
    d_gate_pre = (d_inner * up_pre * sigmoid_gate * (1.0 + gate_pre * (1.0 - sigmoid_gate))).astype(BF)
    d_up_pre = (d_inner * gate_pre * sigmoid_gate).astype(BF)
    d_normed_two = scatter_pieces(nt(d_gate_pre, gate_cols) + nt(d_up_pre, up_cols), ranks)
    mlp_out = scatter_pieces(nt(inner_act, down_t), ranks)
    block_out = (middle + mlp_out).astype(BF)

    scaled = d_normed_two * my_gain_two
    dot_two = lax.psum(jnp.sum(scaled * middle, axis=-1, keepdims=True), "m") / width
    d_gain_two = jnp.sum(d_normed_two * middle * r_two, axis=0)
    d_middle = cotangent.astype(F32) + r_two * scaled - middle * (r_two * r_two * r_two) * dot_two
    d_middle_low = gather_pieces(d_middle.astype(BF), ranks)
    d_gate = grad_rows(tn(normed_two, d_gate_pre), inner)
    d_up = grad_rows(tn(normed_two, d_up_pre), inner)
    d_down = grad_rows(tn(grad_full, inner_act), inner).T

    d_mixed = nn(d_middle_low, out_t).astype(BF)
    d_out_part = tn(d_middle_low, mixed)
    d_mixed_stack = d_mixed.reshape(inner, length, group, head_dim)
    d_query_stack, d_key_stack, d_value_stack = lax.map(
        partial(attend_grad, scale=scale),
        (query_stack, key_stack, value_stack, d_mixed_stack, log_norm, allowed),
    )
    rotary_piece = partial(head_piece, cosine=cosine, sine_table=sine_table)
    _, query_pull = jax.vjp(rotary_piece, query_pre, q_gain)
    d_query_pre, d_qgain_part = query_pull(d_query_stack.reshape(inner * length, group, head_dim))
    _, key_pull = jax.vjp(rotary_piece, key_pre, k_gain)
    d_key_pre, d_kgain_part = key_pull(d_key_stack.reshape(inner * length, 1, head_dim))
    d_heads = jnp.concatenate(
        [d_query_pre, d_key_pre, d_value_stack.reshape(inner * length, head_dim)], 1
    ).astype(BF)
    heads_cols = attn_cols[:, : edges[3]]
    d_normed_one = scatter_pieces(nt(d_heads, heads_cols), ranks)
    d_attn = jnp.concatenate([tn(normed_one, d_heads), d_out_part], 1)
    d_attn = grad_rows(d_attn, inner).reshape(-1, inner, edges[4])
    d_query, d_key, d_value, d_out_t = [
        d_attn[:, :, edges[n]:edges[n + 1]].reshape(d_attn.shape[0], -1) for n in range(4)
    ]
    mine = hidden_in.astype(F32)
    i_index = lax.axis_index("i")
    r_own = lax.dynamic_slice_in_dim(r_one, i_index * length, length, 0)
    scaled = d_normed_one * my_gain_one
    dot_one = lax.psum(jnp.sum(scaled * mine, axis=-1, keepdims=True), "m") / width
    d_gain_one = jnp.sum(d_normed_one * mine * r_own, axis=0)
    d_input = d_middle + r_own * scaled - mine * (r_own * r_own * r_own) * dot_one

    both = jnp.stack([d_gain_one, d_gain_two], 0)
    wide = lax.dynamic_update_slice(jnp.zeros((2, width), F32), both, (0, m_index * width_part))
    small = jnp.concatenate([wide.reshape(-1), d_qgain_part, d_kgain_part])
    small = lax.psum(small, ALL)
    wide = small[: 2 * width].reshape(2, width)
    shard = attn_gain.shape[0]
    own = lax.dynamic_slice(wide, (0, (t_index * inner + i_index) * shard), (2, shard))
    return (
        block_out, d_input, own[0], d_query, d_key, d_value,
        small[2 * width : 2 * width + head_dim], small[2 * width + head_dim :],
        d_out_t.T, own[1], d_gate, d_up, d_down,
    )


def solution(mesh):
    dp, halves = mesh.shape["dp"], mesh.shape["mp"]
    inner = 4
    groups = dp // inner
    fine = Mesh(mesh.devices.reshape(groups, inner, halves), ("t", "i", "m"))
    rows = P(("t", "i"))
    block = P(("t", "i"), "m")
    turned = P("m", ("t", "i"))
    return jax.shard_map(
        partial(body, groups=groups, inner=inner, halves=halves),
        mesh=fine,
        in_specs=(block, P(), rows, block, block, block, P(), P(), turned, rows, block, block, turned, block),
        out_specs=(block, block, rows, block, block, block, P(), P(), turned, rows, block, block, turned),
        check_vma=False,
    )
```

time: 2420 us -> 1430 us (0.59)
  waiting for transfers between devices: 1950 us -> 558 us
  local copies, waits for them, and re-layouts: 17.3 us -> 361 us
    reduce_scatter x8, waiting for transfers between devices: 1230 us -> 209 us  [the longest x4 207 us: scatter_pieces(): mine = lax.psum_scatter(parts, TP, scatter_dimension=0, tiled=False)]
    all_gather x9 -> x8, waiting for transfers between devices: 539 us -> 306 us  [the longest x4 221 us: full_rows(): return lax.all_gather(spread(local, inner), 't', axis=0, tiled=True)]
    psum x3 -> x0, waiting for transfers between devices: 175 us -> none  [the longest x1 90.4 us: body(): lax.psum(transpose_dot(d_gate_pre, gate_cols) + transpose_dot(d_up_pre, u...]
    reshape x0 -> x17, local copies, waits for them, and re-layouts: none -> 123 us  [the longest x4 57.9 us: scatter_pieces(): partial_sum.astype(BF)]
    all_to_all x0 -> x4, blocking collectives: none -> 86.1 us  [spread(): parts = lax.all_to_all(parts, 'i', 0, 0, tiled=False)]
    dynamic_update_slice x0 -> x16, local copies, waits for them, and re-layouts: none -> 61.7 us  [body(): lax.map(partial(attend_grad, scale=scale), (query_stack, key_stack, value...]
    unnamed x1 -> x0, blocking collectives: 59.9 us -> none
    unnamed x119 -> x163, local copies, waits for them, and re-layouts: 11.6 us -> 56.6 us
  transfers between devices with their start and end apart: 20 -> 20, of which waited for: 16 -> 16; matrix products, arithmetic and copies ran while one was open for 10% -> 29% of each run, Pallas kernels for 0% -> 0%
where the time goes in v1:
time: 1430 us; the launch traced here: 1420 us
  waiting for transfers between devices  558 us (39%)
  local copies, waits for them, and re-layouts  361 us (25%)
  matrix products  229 us (16%)
  blocking collectives  162 us (11%)
  other arithmetic  76.3 us (5%)
  starting transfers between devices  15.8 us (1%)
  between operations  15.6 us (1%)
    all_gather x4, waiting for transfers between devices, full_rows(): return lax.all_gather(spread(local, inner), 't', axis=0, tiled=True)  221 us
    reduce_scatter x4, waiting for transfers between devices, scatter_pieces(): mine = lax.psum_scatter(parts, TP, scatter_dimension=0, tiled=False)  207 us
    dot_general x17, matrix products, dot_f32(): lax.dot_general(left, right, (dims, ((), ())), preferred_element_type=F32)  176 us
    all_to_all x4, blocking collectives, spread(): parts = lax.all_to_all(parts, 'i', 0, 0, tiled=False)  86.1 us
    all_gather x4, waiting for transfers between devices, gather_pieces(): parts = lax.all_gather(piece, TP, axis=0)  84.7 us
    dynamic_update_slice x16, local copies, waits for them, and re-layouts, body(): lax.map(partial(attend_grad, scale=scale), (query_stack, key_stack, value...  61.7 us
    reshape x4, local copies, waits for them, and re-layouts, scatter_pieces(): partial_sum.astype(BF)  57.9 us
    unnamed x163, local copies, waits for them, and re-layouts  56.6 us
  transfers between devices with their start and end apart: 20, of which 16 were waited for; matrix products, arithmetic and copies ran while one was open for 29% of the time, Pallas kernels for 0%

profile of v1, /device:TPU:0, one launch (start us, length us, event | category | flops | bytes accessed | tf_op | source)
XLA Modules:
  0.0 1419.3 jit_solution(7471907104294036596)
XLA Ops:
  11.3 14.3 %all_to_all.40 = bf16[4,128,640]{1,2,0:T(8,128)(2,1)S(1)} all-to-all(bf16[4,128,640]{1,2,0:T(8,128)(2,1)S(1)} %maximum_bitcast_fusion), channel_id=1, replica_groups=mesh['t'=4,'i'=4,'m'=2] {'i'}, dimensions={0} | all-to-all | bytes 1310720 | tf_op jit(solution)/shard_map/all_to_all | solution.py:104
  27.7 20.5 %all_gather.41 = bf16[2048,2]{0,1:T(2,128)(2,1)S(1)} all-gather(bf16[128,2]{0,1:T(2,128)(2,1)S(1)} %pad_maximum_fusion.6), channel_id=1, replica_groups=mesh['t'=4,'i'=4,'m'=2] {'t','i'}, dimensions={0}, use_global_device_ids=true | all-gather | bytes 8704 | tf_op jit(solution)/shard_map/all_gather | solution.py:138
  50.1 31.7 %all-gather.13.cloned.1.call-done = bf16[2048,640]{0,1:T(8,128)(2,1)} async-done(((bf16[512,640]{0,1:T(8,128)(2,1)}), bf16[2048,640]{0,1:T(8,128)(2,1)}) %all-gather.13.cloned.1.call-update) | async-done | bytes 2621456 | tf_op jit(solution)/shard_map/all_gather | solution.py:115
  81.8 55.0 %all-gather.21.cloned.1.call-done = bf16[4096,1024]{1,0:T(8,128)(2,1)} async-done(((bf16[512,1024]{1,0:T(8,128)(2,1)}), bf16[4096,1024]{1,0:T(8,128)(2,1)}) %all-gather.21.cloned.1.call-update) | async-done | bytes 8388624 | tf_op jit(solution)/shard_map/all_gather | solution.py:88
  136.8 5.1 multiply_reduce_fusion
  142.5 11.3 bitcast_convert_fusion
  153.9 27.7 %copy.137 = f32[4,2,512,1024]{3,1,2,0:T(2,128)S(1)} copy(f32[4,2,512,1024]{3,2,1,0:T(8,128)} %bitcast_convert_fusion) | data formatting | bytes 33554432 | tf_op jit(solution)/shard_map/convert_element_type | solution.py:151
  181.6 6.1 copy.210
  194.9 8.7 fusion.58
  203.6 16.4 %copy.142 = bf16[4,512,2,1024]{3,2,1,0:T(2,128)(2,1)} copy(bf16[4,512,2,1024]{3,1,2,0:T(8,128)(2,1)} %fusion.58) | data formatting | bytes 16777216 | tf_op jit(solution)/shard_map/mul | solution.py:153
  220.1 14.8 %reshape.761 = bf16[2048,2048,1]{1,0,2:T(8,128)(2,1)} reshape(bf16[4,512,2,1024]{3,2,1,0:T(2,128)(2,1)} %copy.142) | data formatting | bytes 16777216 | tf_op jit(solution)/shard_map/convert_element_type | solution.py:153
  234.8 5.8 multiply_reduce_fusion.4
  250.3 18.6 %while.26 = (s32[]{:T(128)}, bf16[4,512,4,64]{1,3,2,0:T(8,128)(2,1)}, f32[4,4,512]{2,1,0:T(4,128)}, bf16[4,512,64]{1,2,0:T(8,128)(2,1)S(1)}, pred[4,512,512]{1,2...) while((s32[]{:T(128)}, ...), condition=%wide.region_6.7_spmd, body=%wide.region_3.6_spmd.sunk | while | flops 281147392 | bytes 14617177 | solution.py:168
  273.2 5.7 convolution_convert_fusion.2
  278.9 14.5 %reshape.696 = bf16[4,512,2,1024]{3,2,1,0:T(2,128)(2,1)} reshape(bf16[2048,2048]{1,0:T(8,128)(2,1)} %convolution_convert_fusion.2) | data formatting | bytes 16777216 | tf_op jit(solution)/shard_map/reshape | solution.py:95
  293.3 9.4 copy.147
  303.4 70.8 %reduce-scatter.9.cloned.1.call-done = bf16[1,512,1024]{2,1,0:T(8,128)(2,1)} async-done(((bf16[8,512,1024]{2,1,0:T(8,128)(2,1)}), bf16[1,512,1024]{2,1,0:T(8,128)(2,1)}) %reduce-scatter.9.cloned.1.call-update) | async-done | bytes 1048592 | tf_op jit(solution)/shard_map/reduce_scatter | solution.py:97
  375.8 4.9 psum.28
  384.2 25.4 %all_to_all.41 = bf16[4,128,1024]{1,2,0:T(8,128)(2,1)S(1)} all-to-all(bf16[4,128,1024]{1,2,0:T(8,128)(2,1)S(1)} %bitcast.453), channel_id=1, replica_groups=mesh['t'=4,'i'=4,'m'=2] {'i'}, dimensions={0} | all-to-all | bytes 2097152 | tf_op jit(solution)/shard_map/all_to_all | solution.py:104
  412.6 28.4 %all_to_all.42 = bf16[4,128,1024]{1,2,0:T(8,128)(2,1)S(1)} all-to-all(bf16[4,128,1024]{1,2,0:T(8,128)(2,1)S(1)} %bitcast.454), channel_id=1, replica_groups=mesh['t'=4,'i'=4,'m'=2] {'i'}, dimensions={0} | all-to-all | bytes 2097152 | tf_op jit(solution)/shard_map/all_to_all | solution.py:104
  442.4 18.0 %all_to_all.43 = bf16[4,128,1024]{1,2,0:T(8,128)(2,1)S(1)} all-to-all(bf16[4,128,1024]{1,2,0:T(8,128)(2,1)} %bitcast.462), channel_id=1, replica_groups=mesh['t'=4,'i'=4,'m'=2] {'i'}, dimensions={0} | all-to-all | bytes 2097152 | tf_op jit(solution)/shard_map/all_to_all | solution.py:104
  461.8 16.7 %copy.155 = bf16[4,2,512,1024]{3,1,2,0:T(2,128)(2,1)} copy(bf16[4,2,512,1024]{3,2,1,0:T(8,128)(2,1)} %bitcast.439) | data formatting | bytes 16777216 | tf_op jit(solution)/shard_map/reshape | solution.py:89
  478.5 10.9 copy.217
  489.4 18.2 %all-gather.23.cloned.1.call-done = bf16[4096,1024]{1,0:T(8,128)(2,1)} async-done(((bf16[512,1024]{1,0:T(8,128)(2,1)}), bf16[4096,1024]{1,0:T(8,128)(2,1)}) %all-gather.23.cloned.1.call-update) | async-done | bytes 8388624 | tf_op jit(solution)/shard_map/all_gather | solution.py:88
  507.5 16.4 %copy.148 = bf16[4,2,512,1024]{3,1,2,0:T(2,128)(2,1)} copy(bf16[4,2,512,1024]{3,2,1,0:T(8,128)(2,1)} %bitcast.444) | data formatting | bytes 16777216 | tf_op jit(solution)/shard_map/reshape | solution.py:89
  524.0 10.2 copy.216
  534.2 56.2 %all-gather.15.cloned.1.call-done = bf16[2048,1024]{1,0:T(8,128)(2,1)} async-done(((bf16[512,1024]{1,0:T(8,128)(2,1)}), bf16[2048,1024]{1,0:T(8,128)(2,1)}) %all-gather.15.cloned.1.call-update) | async-done | bytes 4194320 | tf_op jit(solution)/shard_map/all_gather | solution.py:115
  590.4 14.7 %fusion.116 = f32[2048,1024]{1,0:T(8,128)} fusion(bf16[2048,2048]{1,0:T(8,128)(2,1)} %bitcast.440, bf16[2048,1024]{1,0:T(8,128)(2,1)} %all-gather.15.cloned.1.call-done), kind=kOutput, calls=%fused_computation.219 | convolution fusion | flops 8589934592 | bytes 20971520 | tf_op jit(solution)/shard_map/dot_general | solution.py:17
  605.1 66.3 %all-gather.17.cloned.1.call-done = bf16[2048,1024]{1,0:T(8,128)(2,1)} async-done(((bf16[512,1024]{1,0:T(8,128)(2,1)}), bf16[2048,1024]{1,0:T(8,128)(2,1)}) %all-gather.17.cloned.1.call-update) | async-done | bytes 4194320 | tf_op jit(solution)/shard_map/all_gather | solution.py:115
  671.4 14.4 %fusion.117 = f32[2048,1024]{1,0:T(8,128)} fusion(bf16[2048,2048]{1,0:T(8,128)(2,1)} %bitcast.441, bf16[2048,1024]{1,0:T(8,128)(2,1)} %all-gather.17.cloned.1.call-done), kind=kOutput, calls=%fused_computation.220 | convolution fusion | flops 8589934592 | bytes 20971520 | tf_op jit(solution)/shard_map/dot_general | solution.py:17
  685.8 66.6 %all-gather.19.cloned.1.call-done = bf16[2048,1024]{1,0:T(8,128)(2,1)} async-done(((bf16[512,1024]{1,0:T(8,128)(2,1)}), bf16[2048,1024]{1,0:T(8,128)(2,1)}) %all-gather.19.cloned.1.call-update) | async-done | bytes 4194320 | tf_op jit(solution)/shard_map/all_gather | solution.py:115
  752.4 21.8 %multiply_convert_fusion.2 = (bf16[2048,1024]{1,0:T(8,128)(2,1)}, bf16[2048,1024]{1,0:T(8,128)(2,1)}, bf16[2048,1024]{1,0:T(8,128)(2,1)}) fusion(f32[2048,1024]{1,0:T(8,128)} %fusion.116, f32[2048,1024]{1,0:T(8,128)} %fusion.117, bf16[2048,2048]{1,0:T(8,128)(2,1)} %bitcast.437, bf16[2048,1024]{1,0:T(8,128)(2,1)} %all-gather.19.cloned.1.call-done), kind=kOutput, calls=%fused_computation.70 | convolution fusion | flops 8623489024 | bytes 41943040 | tf_op jit(solution)/shard_map/dot_general | solution.py:17
  774.2 14.4 %fusion.118 = f32[2048,2048]{1,0:T(8,128)} fusion(bf16[2048,1024]{1,0:T(8,128)(2,1)} %get-tuple-element.270, bf16[2048,1024]{1,0:T(8,128)(2,1)S(1)} %copy-done.62), kind=kOutput, calls=%fused_computation.221 | convolution fusion | flops 8589934592 | bytes 25165824 | tf_op jit(solution)/shard_map/dot_general | solution.py:17
  788.6 16.4 %add_convert_fusion = bf16[2048,2048]{1,0:T(8,128)(2,1)} fusion(f32[2048,2048]{1,0:T(8,128)} %fusion.118, bf16[2048,1024]{1,0:T(8,128)(2,1)} %get-tuple-element.269, bf16[2048,1024]{1,0:T(8,128)(2,1)} %all-gather.17.cloned.1.call-done), kind=kOutput, calls=%fused_computation.65 | convolution fusion | flops 8598323200 | bytes 33554432 | tf_op jit(solution)/shard_map/dot_general | solution.py:17
  805.0 14.5 %reshape.710 = bf16[4,512,2,1024]{3,2,1,0:T(2,128)(2,1)} reshape(bf16[2048,2048]{1,0:T(8,128)(2,1)} %add_convert_fusion) | data formatting | bytes 16777216 | tf_op jit(solution)/shard_map/reshape | solution.py:95
  819.5 9.4 copy.156
  828.9 69.9 %reduce-scatter.13.cloned.1.call-done = bf16[1,512,1024]{2,1,0:T(8,128)(2,1)} async-done(((bf16[8,512,1024]{2,1,0:T(8,128)(2,1)}), bf16[1,512,1024]{2,1,0:T(8,128)(2,1)}) %reduce-scatter.13.cloned.1.call-update) | async-done | bytes 1048592 | tf_op jit(solution)/shard_map/reduce_scatter | solution.py:97
  901.6 5.1 psum.29
  910.4 14.0 convolution_convert_fusion.3
  924.5 14.0 convolution_convert_fusion.4
  938.8 14.5 %convert_bitcast_fusion = bf16[2048,1024]{0,1:T(8,128)(2,1)} fusion(bf16[2048,1024]{1,0:T(8,128)(2,1)} %get-tuple-element.271, bf16[2048,2048]{1,0:T(8,128)(2,1)} %bitcast.438), kind=kOutput, calls=%fused_computation.77 | convolution fusion | flops 8592031744 | bytes 16777216 | tf_op jit(solution)/shard_map/dot_general | solution.py:17
  953.3 11.5 all-gather.27.cloned.1.call-done
  964.9 16.4 %copy.157 = bf16[4,2,512,1024]{3,1,2,0:T(2,128)(2,1)} copy(bf16[4,2,512,1024]{3,2,1,0:T(8,128)(2,1)} %bitcast.445) | data formatting | bytes 16777216 | tf_op jit(solution)/shard_map/reshape | solution.py:89
  981.3 10.5 copy.219
  991.8 6.8 convolution_convert_fusion.7
  1004.3 116.4 %while.27 = (s32[]{:T(128)}, f32[4,512,4,64]{1,0,3,2:T(4,128)}, f32[4,512,64]{1,0,2:T(4,128)}, bf16[4,512,64]{1,2,0:T(8,128)(2,1)}, bf16[4,512,64]{1,2,0:T(8,128...) while((s32[]{:T(128)}, f32[4,512,4,64]{1,0,3,2:T(4,128)}, ...), condition=%wide.region_16.17_spmd, body=%wide.region_14.16_spmd.sunk | while | flops 686979072 | bytes 54259364 | solution.py:198
  1013.1 11.1 dynamic_update_slice.35
  1042.1 11.1 dynamic_update_slice.35
  1071.0 11.1 dynamic_update_slice.35
  1100.0 11.1 dynamic_update_slice.35
  1146.4 8.1 convolution_convert_fusion
  1154.6 14.5 %reshape.721 = bf16[4,512,2,1024]{3,2,1,0:T(2,128)(2,1)} reshape(bf16[2048,2048]{1,0:T(8,128)(2,1)} %convolution_convert_fusion) | data formatting | bytes 16777216 | tf_op jit(solution)/shard_map/reshape | solution.py:95
  1169.1 9.4 copy.166
  1178.5 14.2 %convolution_convert_fusion.1 = bf16[2048,2048]{1,0:T(8,128)(2,1)} fusion(bf16[2048,1024]{1,0:T(8,128)(2,1)} %get-tuple-element.271, bf16[2048,1024]{1,0:T(8,128)(2,1)} %all-gather.19.cloned.1.call-done), kind=kOutput, calls=%fused_computation.75 | convolution fusion | flops 8594128896 | bytes 16777216 | tf_op jit(solution)/shard_map/dot_general | solution.py:17
  1192.8 14.5 %reshape.706 = bf16[4,512,2,1024]{3,2,1,0:T(2,128)(2,1)} reshape(bf16[2048,2048]{1,0:T(8,128)(2,1)} %convolution_convert_fusion.1) | data formatting | bytes 16777216 | tf_op jit(solution)/shard_map/reshape | solution.py:95
  1207.2 9.4 copy.154
  1220.4 14.4 %all-to-all-done.6 = bf16[4,128,1024]{2,1,0:T(8,128)(2,1)S(1)} async-done(((bf16[4,128,1024]{2,1,0:T(8,128)(2,1)}), bf16[4,128,1024]{2,1,0:T(8,128)(2,1)S(1)}, u32[]{:S(2)}, u32[]{:S(2)}) %all-to-all-start.6) | async-done | bytes 1048608 | tf_op jit(solution)/shard_map/all_to_all | solution.py:110
  1240.7 12.0 all-to-all-done.5
  1260.1 10.6 all-to-all-done.7
  1279.9 5.4 all-to-all-done.4
  1293.1 39.7 %reduce-scatter.15.cloned.1.call-done = bf16[1,512,1024]{2,1,0:T(8,128)(2,1)} async-done(((bf16[8,512,1024]{2,1,0:T(8,128)(2,1)}), bf16[1,512,1024]{2,1,0:T(8,128)(2,1)}) %reduce-scatter.15.cloned.1.call-update) | async-done | bytes 1048592 | tf_op jit(solution)/shard_map/reduce_scatter | solution.py:97
  1335.0 39.7 %psum.31 = f32[4224]{0:T(1024)S(1)} all-reduce(f32[4224]{0:T(1024)S(1)} %concatenate.65), channel_id=1, replica_groups=mesh['t'=4,'i'=4,'m'=2] {'t','i','m'}, use_global_device_ids=true, to_apply=%region_26.27 | all-reduce | flops 4224 | bytes 33792 | tf_op jit(solution)/shard_map/psum | solution.py:228
  1374.7 5.3 psum.30
  1381.1 26.9 %reduce-scatter.11.cloned.1.call-done = bf16[1,512,1024]{2,1,0:T(8,128)(2,1)} async-done(((bf16[8,512,1024]{2,1,0:T(8,128)(2,1)}), bf16[1,512,1024]{2,1,0:T(8,128)(2,1)}) %reduce-scatter.11.cloned.1.call-update) | async-done | bytes 1048592 | tf_op jit(solution)/shard_map/reduce_scatter | solution.py:97
  (365 shorter events, 209.8 us)
Async XLA Ops:
  7.2 20.2 %copy-start = (s32[16,2]{0,1:T(2,128)S(1)}, s32[16,2]{0,1:T(2,128)}, u32[]{:S(2)}) copy-start(s32[16,2]{0,1:T(2,128)} %param.19) | copy-start | bytes 388
  7.2 20.4 %copy-start.63 = (bf16[64]{0:T(256)(128)(2,1)S(1)}, bf16[64]{0:T(256)(128)(2,1)}, u32[]{:S(2)}) copy-start(bf16[64]{0:T(256)(128)(2,1)} %param.25) | copy-start | bytes 388
  7.2 20.4 %copy-start.65 = (bf16[128]{0:T(256)(128)(2,1)S(1)}, bf16[128]{0:T(256)(128)(2,1)}, u32[]{:S(2)}) copy-start(bf16[128]{0:T(256)(128)(2,1)} %param.20) | copy-start | bytes 772
  7.2 20.4 %copy-start.64 = (bf16[128]{0:T(256)(128)(2,1)S(1)}, bf16[128]{0:T(256)(128)(2,1)}, u32[]{:S(2)}) copy-start(bf16[128]{0:T(256)(128)(2,1)} %param.27) | copy-start | bytes 772
  7.2 40.9 %copy-start.66 = (bf16[64]{0:T(256)(128)(2,1)S(1)}, bf16[64]{0:T(256)(128)(2,1)}, u32[]{:S(2)}) copy-start(bf16[64]{0:T(256)(128)(2,1)} %param.24) | copy-start | bytes 388
  7.2 74.5 %all-gather.13.cloned.1.call-start = ((), (), s32[]{:S(2)}) async-start(), calls=%async_computation.16 | async-start | bytes 3276800 | tf_op jit(solution)/shard_map/all_gather | solution.py:115
  26.6 110.3 %all-gather.21.cloned.1.call-start = ((), (), s32[]{:S(2)}) async-start(), calls=%async_computation.28 | async-start | bytes 9437184 | tf_op jit(solution)/shard_map/all_gather | solution.py:88
  27.3 346.9 %reduce-scatter.9.cloned.1.call-start = ((), (), s32[]{:S(2)}) async-start(), calls=%async_computation.17 | async-start | bytes 9437184 | tf_op jit(solution)/shard_map/reduce_scatter | solution.py:97
  27.6 213.8 %copy-start.60 = (f32[64]{0:T(128)}, f32[64]{0:T(128)S(1)}, u32[]{:S(2)}) copy-start(f32[64]{0:T(128)S(1)} %convert_element_type.239) | copy-start | bytes 772
  48.2 196.1 %copy-start.58 = (f32[64]{0:T(128)}, f32[64]{0:T(128)S(1)}, u32[]{:S(2)}) copy-start(f32[64]{0:T(128)S(1)} %convert_element_type.247) | copy-start | bytes 772
  49.2 138.4 %copy-start.48 = (f32[2048,1]{0,1:T(1,128)}, f32[2048,1]{0,1:T(1,128)S(1)}, u32[]{:S(2)}) copy-start(f32[2048,1]{0,1:T(1,128)S(1)} %get-tuple-element.297) | copy-start | bytes 24580
  193.4 48.0 %copy-start.11 = (f32[2048,64]{0,1:T(8,128)}, f32[2048,64]{0,1:T(8,128)S(1)}, u32[]{:S(2)}) copy-start(f32[2048,64]{0,1:T(8,128)S(1)} %get-tuple-element.306) | copy-start | bytes 1572868
  194.0 47.4 %copy-start.40 = (f32[2048]{0:T(1024)}, f32[2048]{0:T(1024)S(1)}, u32[]{:S(2)}) copy-start(f32[2048]{0:T(1024)S(1)} %fusion.102) | copy-start | bytes 24580
  220.0 14.8 %slice-start.6 = ((bf16[2048,640]{0,1:T(8,128)(2,1)}), bf16[2048,256]{0,1:T(8,128)(2,1)S(1)}, s32[]{:S(2)}) async-start(bf16[2048,640]{0,1:T(8,128)(2,1)} %all-gather.13.cloned.1.call-done), calls=%async_computation.38 | async-start | bytes 2097152 | tf_op jit(solution)/shard_map/slice | solution.py:150
  268.9 10.0 copy-start.10
  268.9 10.0 copy-start.13
  268.9 10.0 copy-start.16
  268.9 9.9 copy-start.31
  302.7 71.5 %copy-start.4 = (bf16[512,1024]{1,0:T(8,128)(2,1)S(1)}, bf16[512,1024]{1,0:T(8,128)(2,1)}, u32[]{:S(2)}) copy-start(bf16[512,1024]{1,0:T(8,128)(2,1)} %param.18) | copy-start | bytes 3145732
  302.7 80.8 %copy-start.32 = (bf16[128,4096]{1,0:T(8,128)(2,1)S(1)}, bf16[128,4096]{1,0:T(8,128)(2,1)}, u32[]{:S(2)}) copy-start(bf16[128,4096]{1,0:T(8,128)(2,1)} %param.28) | copy-start | bytes 3145732
  302.7 159.0 %all-gather.25.cloned.1.call-start = ((), (), s32[]{:S(2)}) async-start(), calls=%async_computation.30 | async-start | bytes 9437184 | tf_op jit(solution)/shard_map/all_gather | solution.py:88
  303.3 204.2 %all-gather.23.cloned.1.call-start = ((), (), s32[]{:S(2)}) async-start(), calls=%async_computation.29 | async-start | bytes 9437184 | tf_op jit(solution)/shard_map/all_gather | solution.py:88
  303.4 603.3 %copy-start.44 = (f32[1024,1]{0,1:T(1,128)}, f32[1024,1]{0,1:T(1,128)S(1)}, u32[]{:S(2)}) copy-start(f32[1024,1]{0,1:T(1,128)S(1)} %dynamic-slice_convert_fusion) | copy-start | bytes 12292
  380.8 525.9 %copy-start.50 = (f32[512,1]{0,1:T(1,128)}, f32[512,1]{0,1:T(1,128)S(1)}, u32[]{:S(2)}) copy-start(f32[512,1]{0,1:T(1,128)S(1)} %get-tuple-element.264) | copy-start | bytes 6148
  380.8 525.9 %copy-start.53 = (f32[512,1]{0,1:T(1,128)}, f32[512,1]{0,1:T(1,128)S(1)}, u32[]{:S(2)}) copy-start(f32[512,1]{0,1:T(1,128)S(1)} %get-tuple-element.263) | copy-start | bytes 6148
  383.4 207.0 %all-gather.15.cloned.1.call-start = ((), (), s32[]{:S(2)}) async-start(), calls=%async_computation.18 | async-start | bytes 5242880 | tf_op jit(solution)/shard_map/all_gather | solution.py:115
  410.9 260.5 %all-gather.17.cloned.1.call-start = ((), (), s32[]{:S(2)}) async-start(), calls=%async_computation.19 | async-start | bytes 5242880 | tf_op jit(solution)/shard_map/all_gather | solution.py:115
  442.3 310.0 %all-gather.19.cloned.1.call-start = ((), (), s32[]{:S(2)}) async-start(), calls=%async_computation.20 | async-start | bytes 5242880 | tf_op jit(solution)/shard_map/all_gather | solution.py:115
  461.7 437.2 %reduce-scatter.13.cloned.1.call-start = ((), (), s32[]{:S(2)}) async-start(), calls=%async_computation.22 | async-start | bytes 9437184 | tf_op jit(solution)/shard_map/reduce_scatter | solution.py:97
  752.4 21.8 %copy-start.62 = (bf16[2048,1024]{1,0:T(8,128)(2,1)S(1)}, bf16[2048,1024]{1,0:T(8,128)(2,1)}, u32[]{:S(2)}) copy-start(bf16[2048,1024]{1,0:T(8,128)(2,1)} %all-gather.15.cloned.1.call-done) | copy-start | bytes 12582916
  828.8 70.0 %copy-start.8 = (bf16[1,512,1024]{2,1,0:T(8,128)(2,1)S(1)}, bf16[1,512,1024]{2,1,0:T(8,128)(2,1)}, u32[]{:S(2)}) copy-start(bf16[1,512,1024]{2,1,0:T(8,128)(2,1)} %reduce-scatter.9.cloned.1.call-done) | copy-start | bytes 3145732
  828.8 78.4 %copy-start.14 = (bf16[512,1024]{1,0:T(8,128)(2,1)S(1)}, bf16[512,1024]{1,0:T(8,128)(2,1)}, u32[]{:S(2)}) copy-start(bf16[512,1024]{1,0:T(8,128)(2,1)} %param.31) | copy-start | bytes 3145732
  828.9 136.0 %all-gather.27.cloned.1.call-start = ((), (), s32[]{:S(2)}) async-start(), calls=%async_computation.31 | async-start | bytes 9437184 | tf_op jit(solution)/shard_map/all_gather | solution.py:88
  910.3 306.3 %reduce-scatter.21.cloned.1.call-start = ((), (), s32[]{:S(2)}) async-start(), calls=%async_computation.26 | async-start | bytes 5242880 | tf_op jit(solution)/shard_map/reduce_scatter | solution.py:119
  924.5 295.9 %reduce-scatter.19.cloned.1.call-start = ((), (), s32[]{:S(2)}) async-start(), calls=%async_computation.25 | async-start | bytes 5242880 | tf_op jit(solution)/shard_map/reduce_scatter | solution.py:119
  938.5 299.8 %reduce-scatter.23.cloned.1.call-start = ((), (), s32[]{:S(2)}) async-start(), calls=%async_computation.27 | async-start | bytes 5242880 | tf_op jit(solution)/shard_map/reduce_scatter | solution.py:119
  953.3 304.8 %reduce-scatter.17.cloned.1.call-start = ((), (), s32[]{:S(2)}) async-start(), calls=%async_computation.24 | async-start | bytes 3276800 | tf_op jit(solution)/shard_map/reduce_scatter | solution.py:119
  981.3 10.5 copy-start.28
  998.6 5.7 copy-start.17
  1035.4 4.4 copy-start.2
  1093.3 4.4 copy-start.2
  1120.7 6.0 copy-start.30
  1120.7 8.9 copy-start.12
  1120.7 8.9 copy-start.41
  1120.7 8.9 copy-start.61
  1123.5 9.2 copy-start.47
  1123.5 9.2 copy-start.24
  1126.7 13.1 copy-start.38
  1145.6 187.2 %reduce-scatter.15.cloned.1.call-start = ((), (), s32[]{:S(2)}) async-start(), calls=%async_computation.23 | async-start | bytes 9437184 | tf_op jit(solution)/shard_map/reduce_scatter | solution.py:97
  1178.5 229.5 %reduce-scatter.11.cloned.1.call-start = ((), (), s32[]{:S(2)}) async-start(), calls=%async_computation.21 | async-start | bytes 9437184 | tf_op jit(solution)/shard_map/reduce_scatter | solution.py:97
  1216.7 39.6 %copy-start.49 = (f32[2048,1]{0,1:T(1,128)S(1)}, f32[2048,1]{0,1:T(1,128)}, u32[]{:S(2)}) copy-start(f32[2048,1]{0,1:T(1,128)} %copy-done.48) | copy-start | bytes 24580
  1216.7 39.6 %copy-start.52 = (f32[1,1,4,512]{3,2,1,0:T(4,128)S(1)}, f32[1,1,4,512]{3,2,1,0:T(4,128)}, u32[]{:S(2)}) copy-start(f32[1,1,4,512]{3,2,1,0:T(4,128)} %get-tuple-element.293) | copy-start | bytes 24580
  1216.7 18.1 %all-to-all-start.6 = ((bf16[4,128,1024]{2,1,0:T(8,128)(2,1)}), bf16[4,128,1024]{2,1,0:T(8,128)(2,1)S(1)}, u32[]{:S(2)}, u32[]{:S(2)}) async-start(bf16[4,128,1024]{2,1,0:T(8,128)(2,1)} %bitcast.464), calls=%async_computation.13 | async-start | bytes 2097152 | tf_op jit(solution)/shard_map/all_to_all | solution.py:110
  1234.8 18.0 %all-to-all-start.5 = ((bf16[4,128,1024]{2,1,0:T(8,128)(2,1)}), bf16[4,128,1024]{2,1,0:T(8,128)(2,1)S(1)}, u32[]{:S(2)}, u32[]{:S(2)}) async-start(bf16[4,128,1024]{2,1,0:T(8,128)(2,1)} %bitcast.463), calls=%async_computation.11 | async-start | bytes 2097152 | tf_op jit(solution)/shard_map/all_to_all | solution.py:110
  1252.7 18.0 %all-to-all-start.7 = ((bf16[4,128,1024]{1,2,0:T(8,128)(2,1)}), bf16[4,128,1024]{1,2,0:T(8,128)(2,1)S(1)}, u32[]{:S(2)}, u32[]{:S(2)}) async-start(bf16[4,128,1024]{1,2,0:T(8,128)(2,1)} %copy_bitcast_fusion), calls=%async_computation.15 | async-start | bytes 2097152 | tf_op jit(solution)/shard_map/all_to_all | solution.py:110
  1270.7 14.5 %all-to-all-start.4 = ((bf16[4,128,640]{1,2,0:T(8,128)(2,1)}), bf16[4,128,640]{1,2,0:T(8,128)(2,1)}, u32[]{:S(2)}, u32[]{:S(2)}) async-start(bf16[4,128,640]{1,2,0:T(8,128)(2,1)} %copy_bitcast_fusion.3), calls=%async_computation.9 | async-start | bytes 1310720 | tf_op jit(solution)/shard_map/all_to_all | solution.py:110
  1278.4 54.4 %copy-start.5 = (bf16[512,1024]{1,0:T(8,128)(2,1)S(1)}, bf16[512,1024]{1,0:T(8,128)(2,1)}, u32[]{:S(2)}) copy-start(bf16[512,1024]{1,0:T(8,128)(2,1)} %param.18) | copy-start | bytes 3145732
  1279.8 55.1 %copy-start.57 = (f32[1024]{0:T(1024)S(1)}, f32[1024]{0:T(1024)}, u32[]{:S(2)}) copy-start(f32[1024]{0:T(1024)} %get-tuple-element.219) | copy-start | bytes 12292
  1279.8 128.2 %copy-start.9 = (bf16[1,512,1024]{2,1,0:T(8,128)(2,1)S(1)}, bf16[1,512,1024]{2,1,0:T(8,128)(2,1)}, u32[]{:S(2)}) copy-start(bf16[1,512,1024]{2,1,0:T(8,128)(2,1)} %reduce-scatter.9.cloned.1.call-done) | copy-start | bytes 3145732
  1279.8 128.2 %copy-start.15 = (bf16[512,1024]{1,0:T(8,128)(2,1)S(1)}, bf16[512,1024]{1,0:T(8,128)(2,1)}, u32[]{:S(2)}) copy-start(bf16[512,1024]{1,0:T(8,128)(2,1)} %param.31) | copy-start | bytes 3145732
  1279.8 128.2 %copy-start.45 = (f32[1024,1]{0,1:T(1,128)S(1)}, f32[1024,1]{0,1:T(1,128)}, u32[]{:S(2)}) copy-start(f32[1024,1]{0,1:T(1,128)} %copy-done.44) | copy-start | bytes 12292
  1279.8 128.2 %copy-start.51 = (f32[512,1]{0,1:T(1,128)S(1)}, f32[512,1]{0,1:T(1,128)}, u32[]{:S(2)}) copy-start(f32[512,1]{0,1:T(1,128)} %copy-done.50) | copy-start | bytes 6148
  1279.8 128.2 %copy-start.54 = (f32[512,1]{0,1:T(1,128)S(1)}, f32[512,1]{0,1:T(1,128)}, u32[]{:S(2)}) copy-start(f32[512,1]{0,1:T(1,128)} %copy-done.53) | copy-start | bytes 6148
  1279.8 128.2 %copy-start.56 = (f32[512,1]{0,1:T(1,128)S(1)}, f32[512,1]{0,1:T(1,128)}, u32[]{:S(2)}) copy-start(f32[512,1]{0,1:T(1,128)} %copy-done.55) | copy-start | bytes 6148
  (33 other events, 79.0 us)
Sparse Core Ops, SparseCore 0:
  26.7 55.0 all-gather.12
  83.7 53.1 all-gather.20
  302.9 71.2 reduce-scatter.8
  376.1 74.5 all-gather.24
  453.1 54.3 all-gather.22
  509.6 80.7 all-gather.14
  592.1 79.2 all-gather.16
  673.0 79.2 all-gather.18
  829.0 69.8 reduce-scatter.12
  910.4 54.3 all-gather.26
  967.2 76.7 reduce-scatter.20
  1046.2 77.2 reduce-scatter.18
  1125.8 77.2 reduce-scatter.22
  1205.4 52.5 reduce-scatter.16
  1261.7 70.9 reduce-scatter.14
  1336.1 71.9 reduce-scatter.10

commit v2 on v1

--- a/solution.py
+++ b/solution.py
@@ -4,6 +4,8 @@
 import jax
 import jax.numpy as jnp
 from jax import lax
+from jax.experimental import pallas as pl
+from jax.experimental.pallas import tpu as pltpu
 from jax.sharding import Mesh, PartitionSpec as P
 
 BF = jnp.bfloat16
@@ -120,7 +122,7 @@
     return collect(mine, inner).astype(F32)
 
 
-def body(
+def plain_body(
     hidden_in, doc_starts, attn_gain, w_query, w_key, w_value, query_gain, key_gain,
     w_out, mlp_gain, w_gate, w_up, w_down, cotangent, *, groups, inner, halves,
 ):
@@ -236,6 +238,755 @@
     )
 
 
+MESH = pl.DeviceIdType.MESH
+ANY = pl.BlockSpec(memory_space=pl.ANY)
+VMEM = pl.BlockSpec(memory_space=pltpu.VMEM)
+SMEM = pl.BlockSpec(memory_space=pltpu.SMEM)
+DMA = pltpu.SemaphoreType.DMA
+LIMIT = 60 * 1024 * 1024
+
+
+def flip(index, mask):
+    if mask == 1:
+        return index + 1 - 2 * lax.rem(index, 2)
+    if mask == 2:
+        return lax.rem(index + 2, 4)
+    return 3 - index
+
+
+def meet(peers):
+    barrier = pltpu.get_barrier_semaphore()
+    for peer in peers:
+        pl.semaphore_signal(barrier, inc=1, device_id=peer, device_id_type=MESH)
+    pl.semaphore_wait(barrier, len(peers))
+
+
+def remote(src, dst, sems, k, peer):
+    return pltpu.make_async_remote_copy(
+        src_ref=src, dst_ref=dst, send_sem=sems[0].at[k], recv_sem=sems[1].at[k],
+        device_id=peer, device_id_type=MESH,
+    )
+
+
+def at(start, size):
+    return pl.ds(pl.multiple_of(start, size), size)
+
+
+def tp_peers(i, m):
+    return {"i": flip(i, 1)}, {"m": 1 - m}, {"i": flip(i, 2)}
+
+
+class TpGather:
+    def __init__(self, piece, full, sems, base, i, m):
+        rows, cols = piece.shape
+        half = rows // 2
+        core, across, along = tp_peers(i, m)
+
+        def slot(a, b, part=None):
+            if part is None:
+                return full.at[at(a * rows, rows), at(b * cols, cols)]
+            return full.at[at(a * rows + part * half, half), at(b * cols, cols)]
+
+        def go(src, dst, k, peer):
+            return remote(src, dst, sems, base + k, peer)
+
+        mine, far = slot(i, m), flip(i, 2)
+        self.local = pltpu.make_async_copy(piece, mine, sems[2].at[base // 8])
+        self.copies = [
+            go(piece, mine, 0, core),
+            go(piece, mine, 1, across),
+            go(piece, mine, 2, along),
+            go(slot(i, 1 - m, 0), slot(i, 1 - m, 0), 3, along),
+            go(slot(i, 1 - m), slot(i, 1 - m), 4, core),
+            go(slot(far, m, 1), slot(far, m, 1), 5, across),
+            go(slot(far, m), slot(far, m), 6, core),
+            go(slot(far, 1 - m), slot(far, 1 - m), 7, core),
+        ]
+
+    def start(self):
+        for k in (1, 2, 0):
+            self.copies[k].start()
+        self.local.start()
+
+    def relay(self):
+        self.copies[1].wait_recv()
+        self.copies[3].start()
+        self.copies[4].start()
+        self.copies[2].wait_recv()
+        self.copies[5].start()
+        self.copies[6].start()
+
+    def relay_far(self):
+        self.copies[3].wait_recv()
+        self.copies[5].wait_recv()
+        self.copies[7].start()
+
+    def finish(self):
+        for k in (0, 4, 6, 7):
+            self.copies[k].wait_recv()
+        for copy in self.copies:
+            copy.wait_send()
+        self.local.wait()
+
+
+def add_rows(target, first, second, step=64):
+    rows = target.shape[0]
+
+    @pl.loop(0, rows, step=step)
+    def _(r):
+        span = pl.ds(pl.multiple_of(r, step), step)
+        total = first[span, :].astype(F32) + second[span, :].astype(F32)
+        target[span, :] = total.astype(target.dtype)
+
+
+def tp_reduce_scratch(rows, cols, halves):
+    return [
+        pltpu.VMEM((2, rows, cols * halves), BF),
+        pltpu.VMEM((2, rows, cols * halves), BF),
+        pltpu.VMEM((2, rows // 2, cols), BF),
+        pltpu.VMEM((rows // 2, cols * halves), BF),
+        pltpu.VMEM((2, rows // 2, cols), BF),
+        DMA((7,)), DMA((7,)), DMA((2,)),
+    ]
+
+
+class TpReduce:
+    def __init__(self, parts, out, scratch, i, m):
+        own, mate, by_x, by_y, last, send, recv, load = scratch
+        rows, cols = out.shape
+        half = rows // 2
+        core, across, along = tp_peers(i, m)
+        sems = (send, recv)
+        self.args = (own, mate, by_x, by_y, last, out, m, rows, cols, half)
+
+        def seq(a):
+            return parts.at[at(a * rows, rows), :]
+
+        self.loads = [
+            pltpu.make_async_copy(seq(flip(i, 2)), own.at[1], load.at[1]),
+            pltpu.make_async_copy(seq(i), own.at[0], load.at[0]),
+        ]
+        theirs = at((1 - m) * cols, cols)
+        ours = at(m * cols, cols)
+        low, high = pl.ds(0, half), pl.ds(half, half)
+        self.copies = [
+            remote(seq(flip(i, 3)), mate.at[1], sems, 0, core),
+            remote(seq(flip(i, 1)), mate.at[0], sems, 1, core),
+            remote(own.at[1, low, theirs], by_x.at[1], sems, 2, across),
+            remote(own.at[0, low, theirs], by_x.at[0], sems, 3, across),
+            remote(own.at[1, high, :], by_y, sems, 4, along),
+            remote(own.at[1, low, ours], last.at[0], sems, 5, along),
+            remote(own.at[0, high, theirs], last.at[1], sems, 6, across),
+        ]
+        self.ours = ours
+
+    def start(self):
+        for k in (0, 1):
+            self.copies[k].start()
+            self.loads[k].start()
+
+    def run(self):
+        own, mate, by_x, by_y, last, out, m, rows, cols, half = self.args
+        copies, ours = self.copies, self.ours
+        low, high = pl.ds(0, half), pl.ds(half, half)
+        for side, k in ((1, 0), (0, 1)):
+            self.loads[k].wait()
+            copies[k].wait_recv()
+            add_rows(own.at[side], own.at[side], mate.at[side])
+            if side == 1:
+                copies[2].start()
+                copies[4].start()
+            else:
+                copies[3].start()
+        copies[2].wait_recv()
+        add_rows(own.at[1, low, ours], own.at[1, low, ours], by_x.at[1])
+        copies[5].start()
+        copies[4].wait_recv()
+        add_rows(own.at[0, high, :], own.at[0, high, :], by_y)
+        copies[6].start()
+        copies[3].wait_recv()
+        add_rows(own.at[0, low, ours], own.at[0, low, ours], by_x.at[0])
+        copies[5].wait_recv()
+        add_rows(out.at[low, :], own.at[0, low, ours], last.at[0])
+        copies[6].wait_recv()
+        add_rows(out.at[high, :], own.at[0, high, ours], last.at[1])
+        for copy in copies:
+            copy.wait_send()
+
+
+def line_gather(full, block_rows, groups, sems, t):
+    def go(block, k, step):
+        view = full.at[at(block * block_rows, block_rows), :]
+        side = 0 if step > 0 else 1
+        return remote(view, view, sems, side * groups + k, {"t": t + step})
+
+    up, down = t < groups - 1, t > 0
+    for k in range(groups - 1):
+        @pl.when(up & (t - k >= 0))
+        def _():
+            go(t - k, k, 1).start()
+
+        @pl.when(down & (t + k <= groups - 1))
+        def _():
+            go(t + k, k, -1).start()
+
+        @pl.when(t - k - 1 >= 0)
+        def _():
+            go(t - k - 1, k, 1).wait_recv()
+
+        @pl.when(t + k + 1 <= groups - 1)
+        def _():
+            go(t + k + 1, k, -1).wait_recv()
+
+    for k in range(groups - 1):
+        @pl.when(up & (t - k >= 0))
+        def _():
+            go(t - k, k, 1).wait_send()
+
+        @pl.when(down & (t + k <= groups - 1))
+        def _():
+            go(t + k, k, -1).wait_send()
+
+
+def spread_kernel(groups, pack, gate, up, down, attn, gate_out, up_out, down_out,
+                  send, recv, local, z_send, z_recv):
+    t, i, m = lax.axis_index("t"), lax.axis_index("i"), lax.axis_index("m")
+    rows = pack.shape[1]
+    width = gate_out.shape[1]
+    others = [{"i": flip(i, j)} for j in (1, 2, 3)]
+    meet(others + [{"t": flip(t, j)} for j in (1, 2, 3)])
+    mine = attn.at[at((t * 4 + i) * rows, rows), :]
+    first, rest = [], []
+    for j in (2, 3, 1):
+        first.append(remote(pack.at[flip(i, j)], mine, (send, recv), j - 1, others[j - 1]))
+    own = [pltpu.make_async_copy(pack.at[i], mine, local.at[0])]
+    place = at(i * rows, rows)
+    for n, (src, dst) in enumerate(((gate, gate_out), (up, up_out), (down, down_out))):
+        for j in (2, 3, 1):
+            view = src.at[:, at(flip(i, j) * width, width)]
+            rest.append(remote(view, dst.at[place, :], (send, recv), 3 * n + 2 + j, others[j - 1]))
+        own.append(pltpu.make_async_copy(src.at[:, at(i * width, width)], dst.at[place, :], local.at[n + 1]))
+    for copy in first + own + rest:
+        copy.start()
+    own[0].wait()
+    for copy in first:
+        copy.wait_recv()
+    line_gather(attn, 4 * rows, groups, (z_send, z_recv), t)
+    for copy in own[1:]:
+        copy.wait()
+    for copy in rest:
+        copy.wait_recv()
+    for copy in first + rest:
+        copy.wait_send()
+
+
+def tp_group(i, m):
+    return list(tp_peers(i, m))
+
+
+def gather_kernel(hidden, cot, full_in, grad_full, send, recv, local):
+    i, m = lax.axis_index("i"), lax.axis_index("m")
+    meet(tp_group(i, m))
+    one = TpGather(hidden, full_in, (send, recv, local), 0, i, m)
+    two = TpGather(cot, grad_full, (send, recv, local), 8, i, m)
+    one.start()
+    two.start()
+    one.relay()
+    one.relay_far()
+    two.relay()
+    two.relay_far()
+    one.finish()
+    two.finish()
+
+
+def row_loop(rows, step=64):
+    def wrap(f):
+        @pl.loop(0, rows, step=step)
+        def _(r):
+            f(pl.ds(pl.multiple_of(r, step), step))
+
+    return wrap
+
+
+def middle_kernel(parts, hidden, gain, middle, stat, full, *scratch):
+    reduce_scratch, (piece, other, send, recv, local, s_send, s_recv) = scratch[:8], scratch[8:]
+    i, m = lax.axis_index("i"), lax.axis_index("m")
+    meet(tp_group(i, m))
+    width = hidden.shape[1] * 2
+    reduce = TpReduce(parts, middle, reduce_scratch, i, m)
+    reduce.start()
+    reduce.run()
+
+    @row_loop(hidden.shape[0])
+    def _(span):
+        v = middle[span, :] + hidden[span, :].astype(F32)
+        middle[span, :] = v
+        stat[span, :] = jnp.broadcast_to(jnp.sum(v * v, axis=-1, keepdims=True), stat[span, :].shape)
+
+    swap = remote(stat, other, (s_send, s_recv), 0, {"m": 1 - m})
+    swap.start()
+    swap.wait()
+
+    @row_loop(hidden.shape[0])
+    def _(span):
+        r = lax.rsqrt((stat[span, :] + other[span, :]) / width + EPS)
+        stat[span, :] = r
+        piece[span, :] = (middle[span, :] * r[:, :1] * gain[...]).astype(BF)
+
+    gather = TpGather(piece, full, (send, recv, local), 0, i, m)
+    gather.start()
+    gather.relay()
+    gather.relay_far()
+    gather.finish()
+
+
+def back_kernel(parts, middle, stat, cot, gain, d_middle, d_gain, full, *scratch):
+    reduce_scratch, (piece, sums, other, send, recv, local, s_send, s_recv) = scratch[:8], scratch[8:]
+    i, m = lax.axis_index("i"), lax.axis_index("m")
+    meet(tp_group(i, m))
+    width = middle.shape[1] * 2
+    reduce = TpReduce(parts, d_middle, reduce_scratch, i, m)
+    reduce.start()
+    d_gain[...] = jnp.zeros_like(d_gain)
+    reduce.run()
+
+    @row_loop(middle.shape[0])
+    def _(span):
+        dn, v, r = d_middle[span, :], middle[span, :], stat[span, :]
+        scaled = dn * gain[...]
+        sums[span, :] = jnp.broadcast_to(jnp.sum(scaled * v, axis=-1, keepdims=True), r.shape)
+        d_gain[0:1, :] += jnp.sum(dn * v * r[:, :1], axis=0, keepdims=True)
+
+    swap = remote(sums, other, (s_send, s_recv), 0, {"m": 1 - m})
+    swap.start()
+    swap.wait()
+
+    @row_loop(middle.shape[0])
+    def _(span):
+        r = stat[span, :]
+        factor = (r * r * r * ((sums[span, :] + other[span, :]) / width))[:, :1]
+        d = cot[span, :].astype(F32) + r[:, :1] * (d_middle[span, :] * gain[...]) - middle[span, :] * factor
+        d_middle[span, :] = d
+        piece[span, :] = d.astype(BF)
+
+    gather = TpGather(piece, full, (send, recv, local), 0, i, m)
+    gather.start()
+    gather.relay()
+    gather.relay_far()
+    gather.finish()
+
+
+def final_kernel(groups, parts, out_parts, grads, hidden, stat, gain, d_middle, middle, gains_in,
+                 d_input, block_out, attn, gains, *scratch):
+    reduce_one, reduce_two = scratch[:8], scratch[8:16]
+    (res, up_in, down_in, total, sums, other, g_in, send, recv, z_send, z_recv, g_send, g_recv,
+     s_send, s_recv, local) = scratch[16:]
+    t, i, m = lax.axis_index("t"), lax.axis_index("i"), lax.axis_index("m")
+    others = [{"i": flip(i, j)} for j in (1, 2, 3)]
+    meet(others + [{"m": 1 - m}] + [{"t": flip(t, j)} for j in (1, 2, 3)])
+    width = hidden.shape[1] * 2
+    block = width // groups
+    one = TpReduce(parts, d_input, reduce_one, i, m)
+    two = TpReduce(out_parts, res, reduce_two, i, m)
+    one.start()
+    two.start()
+
+    def lanes(b):
+        return grads.at[:, at(b * block, block)]
+
+    def up(k, src):
+        return remote(src, up_in.at[k], (z_send, z_recv), k, {"t": t + 1})
+
+    def down(k, src):
+        return remote(src, down_in.at[k], (z_send, z_recv), groups + k, {"t": t - 1})
+
+    @pl.when(t == 0)
+    def _():
+        for k in range(groups - 1):
+            up(k, lanes(groups - 1 - k)).start()
+
+    @pl.when(t == groups - 1)
+    def _():
+        for k in range(groups - 1):
+            down(k, lanes(k)).start()
+
+    one.run()
+    for k in range(groups - 1):
+        b = groups - 1 - k
+
+        @pl.when((t > 0) & (b > t))
+        def _():
+            up(k, up_in.at[k]).wait_recv()
+            add_rows(up_in.at[k], up_in.at[k], lanes(b))
+            up(k, up_in.at[k]).start()
+
+        @pl.when((t < groups - 1) & (k < t))
+        def _():
+            down(k, down_in.at[k]).wait_recv()
+            add_rows(down_in.at[k], down_in.at[k], lanes(k))
+            down(k, down_in.at[k]).start()
+
+    rows = hidden.shape[0]
+    gains[...] = gains_in[...]
+
+    @row_loop(rows)
+    def _(span):
+        dn, v, r = d_input[span, :], hidden[span, :].astype(F32), stat[span, :]
+        sums[span, :] = jnp.broadcast_to(jnp.sum(dn * gain[...] * v, axis=-1, keepdims=True), r.shape)
+        gains[0:1, at(m * (width // 2), width // 2)] += jnp.sum(dn * v * r[:, :1], axis=0, keepdims=True)
+
+    swap = remote(sums, other, (s_send, s_recv), 0, {"m": 1 - m})
+    swap.start()
+    swap.wait()
+
+    @row_loop(rows)
+    def _(span):
+        r = stat[span, :]
+        factor = (r * r * r * ((sums[span, :] + other[span, :]) / width))[:, :1]
+        d = d_middle[span, :] + r[:, :1] * (d_input[span, :] * gain[...])
+        d_input[span, :] = d - hidden[span, :].astype(F32) * factor
+
+    ways = [{"i": flip(i, 1)}, {"m": 1 - m}, {"i": flip(i, 2)}, {"t": flip(t, 1)}, {"t": flip(t, 2)}]
+    for k, peer in enumerate(ways):
+        trade = remote(gains, g_in.at[k], (g_send, g_recv), k, peer)
+        trade.start()
+        trade.wait()
+        gains[...] += g_in[k]
+
+    for b in range(groups):
+        @pl.when(t == b)
+        def _():
+            own = lanes(b)
+            if b > 0:
+                up(groups - 1 - b, up_in.at[0]).wait_recv()
+                add_rows(total, own, up_in.at[groups - 1 - b])
+                own = total
+            if b < groups - 1:
+                down(b, down_in.at[0]).wait_recv()
+                add_rows(total, own, down_in.at[b])
+
+    sub = block // 4
+    moves = []
+    for j in (2, 3, 1):
+        view = total.at[:, at(flip(i, j) * sub, sub)]
+        moves.append(remote(view, attn.at[i], (send, recv), j, others[j - 1]))
+    keep = pltpu.make_async_copy(total.at[:, at(i * sub, sub)], attn.at[i], local.at[0])
+    for move in moves:
+        move.start()
+    keep.start()
+    two.run()
+
+    @row_loop(rows)
+    def _(span):
+        block_out[span, :] = (middle[span, :] + res[span, :]).astype(BF)
+
+    for k in range(groups - 1):
+        @pl.when(t < groups - 1 - k)
+        def _():
+            up(k, up_in.at[k]).wait_send()
+
+        @pl.when(t > k)
+        def _():
+            down(k, down_in.at[k]).wait_send()
+
+    keep.wait()
+    for move in moves:
+        move.wait()
+
+
+def collect_kernel(gate, up, down, gate_out, up_out, down_out, send, recv, local):
+    i = lax.axis_index("i")
+    others = [{"i": flip(i, j)} for j in (1, 2, 3)]
+    meet(others)
+    rows, width = gate_out.shape[0], gate.shape[1]
+    place = at(i * width, width)
+    moves, own = [], []
+    for n, (src, dst) in enumerate(((gate, gate_out), (up, up_out), (down, down_out))):
+        for j in (2, 3, 1):
+            view = src.at[at(flip(i, j) * rows, rows), :]
+            moves.append(remote(view, dst.at[:, place], (send, recv), 3 * n + j - 1, others[j - 1]))
+        own.append(pltpu.make_async_copy(src.at[at(i * rows, rows), :], dst.at[:, place], local.at[n]))
+    for copy in moves + own:
+        copy.start()
+    for copy in moves + own:
+        copy.wait()
+
+
+def shape(dims, dtype):
+    return jax.ShapeDtypeStruct(dims, dtype)
+
+
+def comm_call(kernel, ins, outs, scratch, number):
+    return pl.pallas_call(
+        kernel,
+        out_shape=[s for s, _ in outs],
+        in_specs=ins,
+        out_specs=[b for _, b in outs],
+        scratch_shapes=scratch,
+        compiler_params=pltpu.CompilerParams(
+            collective_id=number, has_side_effects=True, vmem_limit_bytes=LIMIT
+        ),
+    )
+
+
+def allow(cut, q0, qn, kn):
+    q = q0 + lax.broadcasted_iota(jnp.int32, (qn, kn), 0)
+    k = lax.broadcasted_iota(jnp.int32, (qn, kn), 1)
+    doc_q = (q >= cut[0]).astype(jnp.int32) + (q >= cut[1]).astype(jnp.int32)
+    doc_k = (k >= cut[0]).astype(jnp.int32) + (k >= cut[1]).astype(jnp.int32)
+    return (doc_q == doc_k) & (k <= q)
+
+
+def turn(v):
+    half = v.shape[1] // 2
+    return jnp.concatenate([-v[:, half:], v[:, :half]], axis=1)
+
+
+def turn_back(v):
+    half = v.shape[1] // 2
+    return jnp.concatenate([v[:, half:], -v[:, :half]], axis=1)
+
+
+def fore_kernel(heads, hd, cuts, x, weights, gain, qk_gain, cos, sin,
+                normed, pre, qkv, stats, mixed, parts):
+    s = pl.program_id(0)
+    cut = (cuts[s, 0], cuts[s, 1])
+    rows = x.shape[0]
+    nq, kv = heads * hd, (heads + 2) * hd
+
+    @row_loop(rows)
+    def _(span):
+        v = x[span, :].astype(F32)
+        r = lax.rsqrt(jnp.mean(v * v, axis=-1, keepdims=True) + EPS)
+        stats[span, :] = jnp.broadcast_to(r, (r.shape[0], stats.shape[1]))
+        normed[span, :] = (v * r * gain[...]).astype(BF)
+
+    heads_pre = nn(normed[...], weights[:, :kv])
+    pre[...] = heads_pre
+    for h in range(heads + 1):
+        lanes = slice(h * hd, (h + 1) * hd)
+        v = heads_pre[:, lanes]
+        g = qk_gain[0:1, :] if h < heads else qk_gain[1:2, :]
+        n = rms_rows(v, g)
+        qkv[:, lanes] = (n * cos[...] + turn(n) * sin[...]).astype(BF)
+    qkv[:, nq + hd:kv] = heads_pre[:, nq + hd:kv].astype(BF)
+    step = rows // 2
+    for b in range(2):
+        span, kn = slice(b * step, (b + 1) * step), (b + 1) * step
+        mask = allow(cut, b * step, step, kn)
+        keys, values = qkv[0:kn, nq:nq + hd], qkv[0:kn, nq + hd:kv]
+        for h in range(heads):
+            q = qkv[span, h * hd:(h + 1) * hd]
+            scores = jnp.where(mask, nt(q, keys) * (hd ** -0.5), -1e30)
+            top = jnp.max(scores, axis=-1, keepdims=True)
+            e = jnp.exp(scores - top)
+            total = jnp.sum(e, axis=-1, keepdims=True)
+            probs = (e * (1.0 / total)).astype(BF)
+            stats[span, h:h + 1] = top + jnp.log(total)
+            mixed[span, h * hd:(h + 1) * hd] = nn(probs, values).astype(BF)
+    wide = parts.shape[1]
+
+    @pl.loop(0, wide, step=512)
+    def _(c):
+        cols = pl.ds(pl.multiple_of(c, 512), 512)
+        parts[:, cols] = nt(mixed[...], weights[cols, kv:kv + nq]).astype(BF)
+
+
+def aft_kernel(heads, hd, cuts, dm, normed, pre, qkv, stats, mixed, weights, qk_gain, cos, sin,
+               parts, grads, gains, d_mix, d_pre, d_kv, acc):
+    s = pl.program_id(0)
+    cut = (cuts[s, 0], cuts[s, 1])
+    rows = dm.shape[0]
+    nq, kv = heads * hd, (heads + 2) * hd
+    scale = hd ** -0.5
+
+    @pl.when(s == 0)
+    def _():
+        acc[...] = jnp.zeros_like(acc)
+        gains[...] = jnp.zeros_like(gains)
+
+    d_mix[...] = nn(dm[...], weights[:, kv:kv + nq]).astype(BF)
+    d_kv[...] = jnp.zeros_like(d_kv)
+    step = rows // 2
+
+    def undo(h, grad):
+        lanes = slice(h * hd, (h + 1) * hd)
+        row = 0 if h < heads else 1
+        g = qk_gain[row:row + 1, :]
+        u = cos[...] * grad + turn_back(sin[...] * grad)
+        v = pre[:, lanes]
+        r = lax.rsqrt(jnp.mean(v * v, axis=-1, keepdims=True) + EPS)
+        gains[0:1, row * hd:(row + 1) * hd] += jnp.sum(u * v * r, axis=0, keepdims=True)
+        scaled = u * g
+        back = r * scaled - v * (r * r * r) * jnp.mean(scaled * v, axis=-1, keepdims=True)
+        d_pre[:, lanes] = back.astype(BF)
+
+    for h in range(heads):
+        lanes = slice(h * hd, (h + 1) * hd)
+        pieces = []
+        for b in range(2):
+            span, kn = slice(b * step, (b + 1) * step), (b + 1) * step
+            mask = allow(cut, b * step, step, kn)
+            keys, values = qkv[0:kn, nq:nq + hd], qkv[0:kn, nq + hd:kv]
+            q, go = qkv[span, lanes], d_mix[span, lanes]
+            scores = jnp.where(mask, nt(q, keys) * scale, -1e30)
+            probs = jnp.exp(scores - stats[span, h:h + 1])
+            d_probs = nt(go, values)
+            inner = jnp.sum(probs * d_probs, axis=-1, keepdims=True)
+            d_scores = (probs * (d_probs - inner)).astype(BF)
+            pieces.append(nn(d_scores, keys) * scale)
+            d_kv[0:kn, 0:hd] += tn(d_scores, q) * scale
+            d_kv[0:kn, hd:2 * hd] += tn(probs.astype(BF), go)
+        undo(h, jnp.concatenate(pieces, axis=0))
+    undo(heads, d_kv[:, 0:hd])
+    d_pre[:, nq + hd:kv] = d_kv[:, hd:2 * hd].astype(BF)
+    wide = parts.shape[1]
+
+    @pl.loop(0, wide, step=512)
+    def _(c):
+        cols = pl.ds(pl.multiple_of(c, 512), 512)
+        parts[:, cols] = nt(d_pre[...], weights[cols, 0:kv]).astype(BF)
+        acc[0:kv, cols] += tn(d_pre[...], normed[:, cols])
+        acc[kv:kv + nq, cols] += tn(mixed[...], dm[:, cols])
+
+    @pl.when(s == pl.num_programs(0) - 1)
+    def _():
+        grads[...] = acc[...].astype(BF)
+
+
+def fast_body(
+    hidden_in, doc_starts, attn_gain, w_query, w_key, w_value, query_gain, key_gain,
+    w_out, mlp_gain, w_gate, w_up, w_down, cotangent, *, groups, inner, halves,
+):
+    length, part = hidden_in.shape
+    shard = w_query.shape[0]
+    width, tokens = part * halves, length * inner
+    hd = query_gain.shape[0]
+    heads = w_query.shape[1] // inner // hd
+    nq, kv = heads * hd, (heads + 2) * hd
+    hidden_units = w_gate.shape[1] // inner
+    t_index, i_index, m_index = lax.axis_index("t"), lax.axis_index("i"), lax.axis_index("m")
+    cuts = lax.dynamic_slice_in_dim(doc_starts, t_index * inner, inner, 0)
+    cosine, sine_table, _ = jax.vmap(partial(tables, length=length, head_dim=hd))(cuts)
+    cosine, sine_table = cosine.reshape(tokens, hd), sine_table.reshape(tokens, hd)
+    qk_gain = jnp.zeros((8, hd), F32).at[0].set(query_gain.astype(F32)).at[1].set(key_gain.astype(F32))
+
+    def by_rank(w):
+        return jnp.moveaxis(w.reshape(shard, inner, w.shape[1] // inner), 1, 0)
+
+    gains = jnp.zeros((shard, 128), BF).at[:, 0].set(attn_gain).at[:, 1].set(mlp_gain)
+    pack = jnp.concatenate(
+        [by_rank(w_query), by_rank(w_key), by_rank(w_value), by_rank(w_out.T),
+         jnp.broadcast_to(gains[None], (inner, shard, 128))], 2)
+    cols = pack.shape[2]
+    tp_rows = inner * shard
+    attn_w, gate_w, up_w, down_w = comm_call(
+        partial(spread_kernel, groups), [ANY] * 4,
+        [(shape((groups * tp_rows, cols), BF), ANY)] + [(shape((tp_rows, hidden_units), BF), ANY)] * 3,
+        [DMA((12,)), DMA((12,)), DMA((4,)), DMA((2 * groups,)), DMA((2 * groups,))], 0,
+    )(pack, w_gate, w_up, w_down.T)
+    gate_cols, up_cols, down_t = [lax.all_gather(w, "t", axis=0, tiled=True) for w in (gate_w, up_w, down_w)]
+    full_in, grad_full = comm_call(
+        gather_kernel, [ANY] * 2, [(shape((tokens, width), BF), ANY)] * 2,
+        [DMA((16,)), DMA((16,)), DMA((2,))], 1,
+    )(hidden_in, cotangent)
+    both_gains = attn_w[:, nq + kv:nq + kv + 2].astype(F32).T
+    gain_one = both_gains[0:1]
+    own_gains = lax.dynamic_slice(both_gains, (0, m_index * part), (2, part))
+
+    def seq(lanes):
+        return pl.BlockSpec((length, lanes), lambda s: (s, 0))
+
+    def whole(*dims):
+        return pl.BlockSpec(dims, lambda s: (0,) * len(dims))
+
+    params = pltpu.CompilerParams(vmem_limit_bytes=LIMIT, dimension_semantics=("arbitrary",))
+    normed_one, pre, qkv, stats, mixed, parts = pl.pallas_call(
+        partial(fore_kernel, heads, hd),
+        grid=(inner,),
+        in_specs=[SMEM, seq(width), whole(width, cols), whole(1, width), whole(8, hd), seq(hd), seq(hd)],
+        out_shape=[shape((tokens, width), BF), shape((tokens, kv), F32), shape((tokens, kv), BF),
+                   shape((tokens, 128), F32), shape((tokens, nq), BF), shape((tokens, width), BF)],
+        out_specs=[seq(width), seq(kv), seq(kv), seq(128), seq(nq), seq(width)],
+        compiler_params=params,
+    )(cuts, full_in, attn_w, gain_one, qk_gain, cosine, sine_table)
+
+    half_scratch = tp_reduce_scratch(length, part, halves)
+    gather_sems = [DMA((8,)), DMA((8,)), DMA((1,)), DMA((1,)), DMA((1,))]
+    middle, r_two, normed_two = comm_call(
+        middle_kernel, [ANY, VMEM, VMEM],
+        [(shape((length, part), F32), VMEM), (shape((length, 128), F32), VMEM), (shape((tokens, width), BF), ANY)],
+        half_scratch + [pltpu.VMEM((length, part), BF), pltpu.VMEM((length, 128), F32)] + gather_sems, 2,
+    )(parts, hidden_in, own_gains[1:2])
+
+    gate_pre, up_pre = nn(normed_two, gate_cols), nn(normed_two, up_cols)
+    d_inner = nn(grad_full, down_t)
+    sigmoid_gate = jax.nn.sigmoid(gate_pre)
+    inner_act = (gate_pre * sigmoid_gate * up_pre).astype(BF)
+    d_gate_pre = (d_inner * up_pre * sigmoid_gate * (1.0 + gate_pre * (1.0 - sigmoid_gate))).astype(BF)
+    d_up_pre = (d_inner * gate_pre * sigmoid_gate).astype(BF)
+    d_two_parts = (nt(d_gate_pre, gate_cols) + nt(d_up_pre, up_cols)).astype(BF)
+    d_down, d_gate, d_up = [
+        lax.psum_scatter(tn(a, b).astype(BF), "t", scatter_dimension=0, tiled=True)
+        for a, b in ((grad_full, inner_act), (normed_two, d_gate_pre), (normed_two, d_up_pre))
+    ]
+    out_parts = nt(inner_act, down_t).astype(BF)
+
+    d_middle, d_gain_two, d_low = comm_call(
+        back_kernel, [ANY] + [VMEM] * 4,
+        [(shape((length, part), F32), VMEM), (shape((8, part), F32), VMEM), (shape((tokens, width), BF), ANY)],
+        half_scratch + [pltpu.VMEM((length, part), BF)] + [pltpu.VMEM((length, 128), F32)] * 2 + gather_sems, 3,
+    )(d_two_parts, middle, r_two, cotangent, own_gains[1:2])
+
+    d_one_parts, d_attn, qk_grad = pl.pallas_call(
+        partial(aft_kernel, heads, hd),
+        grid=(inner,),
+        in_specs=[SMEM, seq(width), seq(width), seq(kv), seq(kv), seq(128), seq(nq), whole(width, cols),
+                  whole(8, hd), seq(hd), seq(hd)],
+        out_shape=[shape((tokens, width), BF), shape((nq + kv, width), BF), shape((8, 2 * hd), F32)],
+        out_specs=[seq(width), whole(nq + kv, width), whole(8, 2 * hd)],
+        scratch_shapes=[pltpu.VMEM((length, nq), BF), pltpu.VMEM((length, kv), BF),
+                        pltpu.VMEM((length, 2 * hd), F32), pltpu.VMEM((nq + kv, width), F32)],
+        compiler_params=params,
+    )(cuts, d_low, normed_one, pre, qkv, stats, mixed, attn_w, qk_gain, cosine, sine_table)
+
+    gains_in = jnp.zeros((8, width), F32)
+    gains_in = lax.dynamic_update_slice(gains_in, d_gain_two[0:1], (1, m_index * part))
+    gains_in = gains_in.at[2].set(jnp.tile(qk_grad[0], width // (2 * hd)))
+    r_one = lax.dynamic_slice_in_dim(stats, i_index * length, length, 0)
+    r_one = jnp.broadcast_to(r_one[:, heads:heads + 1], (length, 128))
+    block = width // groups
+    d_input, block_out, attn_back, gains_out = comm_call(
+        partial(final_kernel, groups), [ANY, ANY] + [VMEM] * 7,
+        [(shape((length, part), F32), VMEM), (shape((length, part), BF), VMEM),
+         (shape((inner, nq + kv, block // inner), BF), ANY), (shape((8, width), F32), VMEM)],
+        half_scratch * 2 + [
+            pltpu.VMEM((length, part), F32),
+            pltpu.VMEM((groups, nq + kv, block), BF), pltpu.VMEM((groups, nq + kv, block), BF),
+            pltpu.VMEM((nq + kv, block), BF),
+            pltpu.VMEM((length, 128), F32), pltpu.VMEM((length, 128), F32),
+            pltpu.VMEM((5, 8, width), F32),
+            DMA((4,)), DMA((4,)), DMA((2 * groups,)), DMA((2 * groups,)), DMA((5,)), DMA((5,)),
+            DMA((1,)), DMA((1,)), DMA((1,))], 4,
+    )(d_one_parts, out_parts, d_attn, hidden_in, r_one, own_gains[0:1], d_middle, middle, gains_in)
+
+    d_gate, d_up, d_down = comm_call(
+        collect_kernel, [ANY] * 3, [(shape((shard, inner * hidden_units), BF), ANY)] * 3,
+        [DMA((9,)), DMA((9,)), DMA((3,))], 5,
+    )(d_gate, d_up, d_down)
+    own = lax.dynamic_slice(gains_out, (0, (t_index * inner + i_index) * shard), (2, shard))
+
+    def columns(first, last):
+        return jnp.moveaxis(attn_back[:, first:last, :], 2, 0).reshape(shard, -1).astype(F32)
+
+    return (
+        block_out, d_input, own[0], columns(0, nq), columns(nq, nq + hd), columns(nq + hd, kv),
+        gains_out[2, :hd], gains_out[2, hd:2 * hd],
+        attn_back[:, kv:kv + nq, :].reshape(inner * nq, shard).astype(F32), own[1],
+        d_gate.astype(F32), d_up.astype(F32), d_down.T.astype(F32),
+    )
+
+
 def solution(mesh):
     dp, halves = mesh.shape["dp"], mesh.shape["mp"]
     inner = 4
@@ -244,6 +995,7 @@
     rows = P(("t", "i"))
     block = P(("t", "i"), "m")
     turned = P("m", ("t", "i"))
+    body = fast_body if groups == 4 and halves == 2 else plain_body
     return jax.shard_map(
         partial(body, groups=groups, inner=inner, halves=halves),
         mesh=fine,

time: 1430 us -> 826 us (0.58)
  Pallas kernels: 0 us -> 623 us
  waiting for transfers between devices: 558 us -> 1.47 us
  local copies, waits for them, and re-layouts: 361 us -> 28.2 us
  blocking collectives: 162 us -> 0 us
  matrix products: 229 us -> 135 us
  other arithmetic: 76.3 us -> 18.5 us
  starting transfers between devices: 15.8 us -> 0.41 us
    pallas_call x0 -> x8, Pallas kernels: none -> 623 us  [the longest x1 144 us: fast_body(): comm_call(partial(final_kernel, groups), [ANY, ANY] + [VMEM] * 7, [(shape...]
    all_gather x8 -> x3, waiting for transfers between devices: 306 us -> 0.02 us  [fast_body(): lax.all_gather(w, 't', axis=0, tiled=True)]
    reduce_scatter x8 -> x3, waiting for transfers between devices: 209 us -> 0.01 us  [fast_body(): lax.psum_scatter(tn(a, b).astype(BF), 't', scatter_dimension=0, tiled=True)]
    reshape x17 -> x4, local copies, waits for them, and re-layouts: 123 us -> 1.51 us  [by_rank(): return jnp.moveaxis(w.reshape(shard, inner, w.shape[1] // inner), 1, 0)]
    all_to_all x4 -> x0, blocking collectives: 86.1 us -> none  [spread(): parts = lax.all_to_all(parts, 'i', 0, 0, tiled=False)]
    dynamic_update_slice x16 -> x1, local copies, waits for them, and re-layouts: 61.7 us -> 0.42 us  [fast_body(): lax.dynamic_update_slice(gains_in, d_gain_two[0:1], (1, m_index * part))]
    psum x4 -> x0, blocking collectives: 55 us -> none  [the longest x1 39.7 us: body(): small = lax.psum(small, ALL)]
    dot_general x28 -> x0, matrix products: 53.3 us -> none  [the longest x4 16.1 us: attend_grad(): jnp.einsum('gqt,qgd->td', probs.astype(BF), d_outputs, preferred_element_...]
  transfers between devices with their start and end apart: 20 -> 6, of which waited for: 16 -> 0; matrix products, arithmetic and copies ran while one was open for 29% -> 15% of each run, Pallas kernels for 0% -> 63%
where the time goes in v2:
time: 826 us; the launch traced here: 822 us
  Pallas kernels  623 us (75%)
  matrix products  135 us (16%)
  local copies, waits for them, and re-layouts  28.2 us (3%)
  other arithmetic  18.5 us (2%)
  between operations  14.9 us (2%)
    pallas_call x1, Pallas kernels, fast_body(): comm_call(partial(final_kernel, groups), [ANY, ANY] + [VMEM] * 7, [(shape...  144 us
    dot_general x9, matrix products, dot_f32(): lax.dot_general(left, right, (dims, ((), ())), preferred_element_type=F32)  135 us
    pallas_call x1, Pallas kernels, fast_body(): comm_call(back_kernel, [ANY] + [VMEM] * 4, [(shape((length, part), F32),...  93.7 us
    pallas_call x1, Pallas kernels, fast_body(): comm_call(middle_kernel, [ANY, VMEM, VMEM], [(shape((length, part), F32),...  92.3 us
    pallas_call x1, Pallas kernels, fast_body(): comm_call(gather_kernel, [ANY] * 2, [(shape((tokens, width), BF), ANY)] *...  75.7 us
    pallas_call x1, Pallas kernels, fast_body(): comm_call(partial(spread_kernel, groups), [ANY] * 4, [(shape((groups * tp...  72.4 us
    pallas_call x1, Pallas kernels, fast_body(): pl.pallas_call(partial(aft_kernel, heads, hd), grid=(inner,), in_specs=[S...  60.8 us
    pallas_call x1, Pallas kernels, fast_body(): pl.pallas_call(partial(fore_kernel, heads, hd), grid=(inner,), in_specs=[...  48.2 us
  transfers between devices with their start and end apart: 6, of which 0 were waited for; matrix products, arithmetic and copies ran while one was open for 15% of the time, Pallas kernels for 63%

profile of v2, /device:TPU:0, one launch (start us, length us, event | category | flops | bytes accessed | tf_op | source)
XLA Modules:
  0.0 822.1 jit_solution(12166287142920636365)
XLA Ops:
  7.2 0.6 compare_reduce_fusion.1
  7.9 0.6 compare_reduce_fusion
  8.5 1.1 copy.36
  9.6 0.2 copy.37
  9.8 1.1 copy.42
  10.9 1.3 fusion.4
  12.2 1.3 fusion.5
  13.6 0.1 copy.43
  13.7 1.0 copy.38
  14.6 0.1 copy.39
  14.8 1.0 copy.40
  15.7 0.1 copy.41
  15.9 2.3 copy.44
  18.2 1.1 concatenate.18.pack
  19.2 72.4 %shard_map.238 = (bf16[2048,768]{1,0:T(8,128)(2,1)}, bf16[512,1024]{1,0:T(8,128)(2,1)}, bf16[512,1024]{1,0:T(8,128)(2,1)}, bf16[512,1024]{1,0:T(8,128)(2,1)}) custom-call(bf16[4,128,768]{2,1,0:T(8,128)(2,1)} %concatenate.18.pack, bf16[128,4096]{1,0:T(8,128)(2,1)} %gate.1, bf16[128,4096]{1,0:T(8,128)(2,1)} %up.1, bf16[128,4096]{1,0:T(8,128)(2,1)} %bitcast.75), custom_call_target="tpu_custom_call" | custom-call | tf_op jit(solution)/shard_map/pallas_call | solution.py:883
  91.8 0.7 all-gather.4.cloned.1.call-update
  92.5 0.7 all-gather.6.cloned.1.call-update
  93.4 0.2 slice_reduce_fusion
  93.7 3.0 copy.45
  96.6 0.8 slice_convert_fusion.3
  97.5 0.6 slice.151.gain
  98.1 75.7 %shard_map.237 = (bf16[2048,2048]{1,0:T(8,128)(2,1)}, bf16[2048,2048]{1,0:T(8,128)(2,1)}) custom-call(bf16[512,1024]{1,0:T(8,128)(2,1)} %hidden.5, bf16[512,1024]{1,0:T(8,128)(2,1)} %cot.3), custom_call_target="tpu_custom_call" | custom-call | tf_op jit(solution)/shard_map/pallas_call | solution.py:889
  173.9 0.2 scatter.31.qk_gain
  174.2 0.3 broadcast_multiply_fusion
  174.5 4.8 fusion
  179.3 48.2 %shard_map.239 = (bf16[2048,2048]{1,0:T(8,128)(2,1)}, f32[2048,384]{1,0:T(8,128)}, bf16[2048,384]{1,0:T(8,128)(2,1)}, f32[2048,128]{1,0:T(8,128)}, bf16[2048,256...) custom-call(s32[4,2]{1,0:T(4,128)} %copy-done.7, bf16[2048,2048]{1,0:T(8,128)(2,1)} %get-tuple-element.103.x, ...), custom_call_target="tpu_custom_call" | custom-call | tf_op jit(solution)/shard_map/pallas_call | solution.py:904
  227.5 0.6 fusion.8
  228.1 92.3 %shard_map.240 = (f32[512,1024]{1,0:T(8,128)}, f32[512,128]{1,0:T(8,128)}, bf16[2048,2048]{1,0:T(8,128)(2,1)}) custom-call(bf16[2048,2048]{1,0:T(8,128)(2,1)} %get-tuple-element.105.parts, bf16[512,1024]{1,0:T(8,128)(2,1)} %hidden.5, f32[1,1024]{1,0:T(1,128)} %get-tuple-element.171.gain), custom_call_target="tpu_custom_call" | custom-call | tf_op jit(solution)/shard_map/pallas_call | solution.py:916
  320.5 14.4 %fusion.10 = f32[2048,1024]{1,0:T(8,128)} fusion(bf16[2048,2048]{1,0:T(8,128)(2,1)} %get-tuple-element.106, bf16[2048,1024]{1,0:T(8,128)(2,1)} %all-gather.8.cloned.1.call-done), kind=kOutput, calls=%fused_computation.51 | convolution fusion | flops 8589934592 | bytes 20971520 | tf_op jit(solution)/shard_map/dot_general | solution.py:19
  334.9 14.9 %fusion.9 = f32[2048,1024]{1,0:T(8,128)} fusion(bf16[2048,2048]{1,0:T(8,128)(2,1)} %get-tuple-element.101, bf16[2048,1024]{1,0:T(8,128)(2,1)} %all-gather.4.cloned.1.call-done), kind=kOutput, calls=%fused_computation.50 | convolution fusion | flops 8589934592 | bytes 20971520 | tf_op jit(solution)/shard_map/dot_general | solution.py:19
  349.8 21.1 %multiply_convert_fusion = (bf16[2048,1024]{1,0:T(8,128)(2,1)}, bf16[2048,1024]{1,0:T(8,128)(2,1)}, bf16[2048,1024]{1,0:T(8,128)(2,1)S(1)}) fusion(f32[2048,1024]{1,0:T(8,128)} %fusion.10, f32[2048,1024]{1,0:T(8,128)} %fusion.9, bf16[2048,2048]{1,0:T(8,128)(2,1)} %get-tuple-element.106, bf16[2048,1024]{1,0:T(8,128)(2,1)} %all-gather.6.cloned.1.call-done), kind=kOutput, calls=%fused_computation.1 | convolution fusion | flops 8623489024 | bytes 41943040 | tf_op jit(solution)/shard_map/dot_general | solution.py:19
  370.9 2.0 copy-done.12
  372.9 12.9 %convolution_convert_fusion.2 = bf16[2048,1024]{1,0:T(8,128)(2,1)} fusion(bf16[2048,2048]{1,0:T(8,128)(2,1)} %get-tuple-element.106, bf16[2048,1024]{1,0:T(8,128)(2,1)S(1)} %get-tuple-element.159), kind=kOutput, calls=%fused_computation.7 | convolution fusion | flops 8592031744 | bytes 16777216 | tf_op jit(solution)/shard_map/dot_general | solution.py:19
  385.8 0.2 reduce-scatter.4.cloned.1.call-start
  386.1 14.0 %convolution_convert_fusion.3 = bf16[2048,1024]{1,0:T(8,128)(2,1)} fusion(bf16[2048,2048]{1,0:T(8,128)(2,1)} %get-tuple-element.106, bf16[2048,1024]{1,0:T(8,128)(2,1)} %get-tuple-element.158), kind=kOutput, calls=%fused_computation.8 | convolution fusion | flops 8592031744 | bytes 16777216 | tf_op jit(solution)/shard_map/dot_general | solution.py:19
  400.2 14.0 %convolution_convert_fusion.1 = bf16[2048,1024]{1,0:T(8,128)(2,1)} fusion(bf16[2048,2048]{1,0:T(8,128)(2,1)} %get-tuple-element.101, bf16[2048,1024]{1,0:T(8,128)(2,1)} %get-tuple-element.157), kind=kOutput, calls=%fused_computation.6 | convolution fusion | flops 8592031744 | bytes 16777216 | tf_op jit(solution)/shard_map/dot_general | solution.py:19
  414.2 1.2 dynamic-slice_reduce_fusion
  415.4 15.4 %fusion.11 = f32[2048,2048]{1,0:T(8,128)} fusion(bf16[2048,1024]{1,0:T(8,128)(2,1)} %get-tuple-element.158, bf16[2048,1024]{1,0:T(8,128)(2,1)} %all-gather.8.cloned.1.call-done), kind=kOutput, calls=%fused_computation.52 | convolution fusion | flops 8589934592 | bytes 25165824 | tf_op jit(solution)/shard_map/dot_general | solution.py:19
  430.8 13.9 %add_convert_fusion.parts = bf16[2048,2048]{1,0:T(8,128)(2,1)} fusion(f32[2048,2048]{1,0:T(8,128)} %fusion.11, bf16[2048,1024]{1,0:T(8,128)(2,1)S(1)} %copy-done.13, bf16[2048,1024]{1,0:T(8,128)(2,1)S(1)} %copy-done.10), kind=kOutput, calls=%fused_computation | convolution fusion | flops 8598323200 | bytes 33554432 | tf_op jit(solution)/shard_map/dot_general | solution.py:19
  444.8 93.7 %shard_map.241 = (f32[512,1024]{1,0:T(8,128)}, f32[8,1024]{1,0:T(8,128)}, bf16[2048,2048]{1,0:T(8,128)(2,1)}) custom-call(bf16[2048,2048]{1,0:T(8,128)(2,1)} %add_convert_fusion.parts, f32[512,1024]{1,0:T(8,128)} %get-tuple-element.109.middle, f32[512,128]{1,0:T(8,128)} %get-tuple-element.110.stat, bf16[512,1024]{1,0:T(8,128)(2,1)} %cot.3, ...), custom_call_target="tpu_custom_call" | custom-call | tf_op jit(solution)/shard_map/pallas_call | solution.py:935
  538.5 0.8 slice.140
  539.3 0.4 dynamic_update_slice.3
  539.7 60.8 %shard_map.242 = (bf16[2048,2048]{1,0:T(8,128)(2,1)}, bf16[640,2048]{1,0:T(8,128)(2,1)}, f32[8,128]{1,0:T(8,128)}) custom-call(s32[4,2]{1,0:T(4,128)} %copy-done.7, bf16[2048,2048]{1,0:T(8,128)(2,1)} %get-tuple-element.111.dm, bf16[2048,2048]{1,0:T(8,128)(2,1)} %get-tuple-element.112.normed, f32[2048,384]{1,0:T(8,128)} %get-tuple-element.113.pre, ...), custom_call_target="tpu_custom_call" | custom-call | tf_op jit(solution)/shard_map/pallas_call | solution.py:941
  600.6 0.7 slice_bitcast_fusion.4
  601.3 0.2 scatter.32.gains_in
  601.5 14.4 %convolution_convert_fusion.out_parts = bf16[2048,2048]{1,0:T(8,128)(2,1)} fusion(bf16[2048,1024]{1,0:T(8,128)(2,1)} %get-tuple-element.157, bf16[2048,1024]{1,0:T(8,128)(2,1)} %all-gather.4.cloned.1.call-done), kind=kOutput, calls=%fused_computation.5 | convolution fusion | flops 8594128896 | bytes 16777216 | tf_op jit(solution)/shard_map/dot_general | solution.py:19
  615.8 0.8 broadcast_in_dim.37.stat
  616.7 143.5 %shard_map.243 = (f32[512,1024]{1,0:T(8,128)}, bf16[512,1024]{1,0:T(8,128)(2,1)}, bf16[4,640,128]{2,1,0:T(8,128)(2,1)}, f32[8,2048]{1,0:T(8,128)}) custom-call(bf16[2048,2048]{1,0:T(8,128)(2,1)} %get-tuple-element.117.parts, bf16[2048,2048]{1,0:T(8,128)(2,1)} %convolution_convert_fusion.out_parts, bf16[640,2048]{1,0:T(8,128)(2,1)} %get-tuple-element.118.grads, ...), custom_call_target="tpu_custom_call" | custom-call | tf_op jit(solution)/shard_map/pallas_call | solution.py:959
  760.2 1.1 fusion.7
  761.3 1.0 copy.46
  762.3 0.9 slice_convert_fusion.1
  763.2 0.8 copy.47
  763.9 0.8 copy.48
  764.7 0.7 constant_dynamic-slice_fusion
  765.4 0.5 slice_bitcast_fusion
  765.9 1.3 slice_bitcast_fusion.1
  767.2 0.8 bitcast_convert_fusion
  768.1 36.8 %shard_map.244 = (bf16[128,4096]{1,0:T(8,128)(2,1)}, bf16[128,4096]{1,0:T(8,128)(2,1)}, bf16[128,4096]{1,0:T(8,128)(2,1)}) custom-call(bf16[512,1024]{1,0:T(8,128)(2,1)} %reduce-scatter.4.cloned.1.call-done.gate, bf16[512,1024]{1,0:T(8,128)(2,1)} %reduce-scatter.6.cloned.1.call-done.up, bf16[512,1024]{1,0:T(8,128)(2,1)} %reduce-scatter.8.cloned.1.call-done.down), custom_call_target="tpu_custom_call" | custom-call | tf_op jit(solution)/shard_map/pallas_call | solution.py:973
  804.8 1.4 convert_bitcast_fusion
  806.3 1.8 copy.49
  808.1 2.9 convert_element_type.121
  811.0 1.5 convert_element_type.122
  812.5 1.0 copy.60
  813.5 1.3 copy.61
  (59 shorter events, 0.7 us)
Async XLA Ops:
  7.2 86.1 %copy-start = (s32[16,2]{0,1:T(2,128)S(1)}, s32[16,2]{0,1:T(2,128)}, u32[]{:S(2)}) copy-start(s32[16,2]{0,1:T(2,128)} %param.25) | copy-start | bytes 388
  7.2 313.3 %all-gather.8.cloned.1.call-start = ((), (), s32[]{:S(2)}) async-start(), calls=%async_computation.5 | async-start | bytes 5242880 | tf_op jit(solution)/shard_map/all_gather | solution.py:888
  91.7 1.9 copy-start.2
  91.7 243.2 %all-gather.4.cloned.1.call-start = ((), (), s32[]{:S(2)}) async-start(), calls=%async_computation.3 | async-start | bytes 5242880 | tf_op jit(solution)/shard_map/all_gather | solution.py:888
  92.5 257.3 %all-gather.6.cloned.1.call-start = ((), (), s32[]{:S(2)}) async-start(), calls=%async_computation.4 | async-start | bytes 5242880 | tf_op jit(solution)/shard_map/all_gather | solution.py:888
  93.2 674.9 %reduce-scatter.6.cloned.1.call-start = ((), (), s32[]{:S(2)}) async-start(), calls=%async_computation.7 | async-start | bytes 5242880 | tf_op jit(solution)/shard_map/reduce_scatter | solution.py:930
  93.4 80.4 %copy-start.7 = (s32[4,2]{1,0:T(4,128)}, s32[4,2]{1,0:T(4,128)S(1)}, u32[]{:S(2)}) copy-start(s32[4,2]{1,0:T(4,128)S(1)} %copy.50.cuts) | copy-start | bytes 100
  93.6 80.2 %copy-start.9 = (bf16[64]{0:T(256)(128)(2,1)S(1)}, bf16[64]{0:T(256)(128)(2,1)}, u32[]{:S(2)}) copy-start(bf16[64]{0:T(256)(128)(2,1)} %param.30) | copy-start | bytes 388
  93.6 80.2 %copy-start.11 = (bf16[64]{0:T(256)(128)(2,1)S(1)}, bf16[64]{0:T(256)(128)(2,1)}, u32[]{:S(2)}) copy-start(bf16[64]{0:T(256)(128)(2,1)} %param.31) | copy-start | bytes 388
  174.1 5.2 copy-start.8
  370.9 2.0 copy-start.12
  385.8 382.2 %reduce-scatter.4.cloned.1.call-start = ((), (), s32[]{:S(2)}) async-start(), calls=%async_computation.6 | async-start | bytes 5242880 | tf_op jit(solution)/shard_map/reduce_scatter | solution.py:930
  400.1 368.0 %reduce-scatter.8.cloned.1.call-start = ((), (), s32[]{:S(2)}) async-start(), calls=%async_computation.8 | async-start | bytes 5242880 | tf_op jit(solution)/shard_map/reduce_scatter | solution.py:930
  415.4 15.5 %copy-start.10 = (bf16[2048,1024]{1,0:T(8,128)(2,1)S(1)}, bf16[2048,1024]{1,0:T(8,128)(2,1)}, u32[]{:S(2)}) copy-start(bf16[2048,1024]{1,0:T(8,128)(2,1)} %all-gather.6.cloned.1.call-done) | copy-start | bytes 12582916
  415.4 15.4 %copy-start.13 = (bf16[2048,1024]{1,0:T(8,128)(2,1)S(1)}, bf16[2048,1024]{1,0:T(8,128)(2,1)}, u32[]{:S(2)}) copy-start(bf16[2048,1024]{1,0:T(8,128)(2,1)} %copy-done.12) | copy-start | bytes 12582916
  601.4 14.4 %copy-start.6 = (f32[8,2048]{1,0:T(8,128)}, f32[8,2048]{1,0:T(8,128)S(1)}, u32[]{:S(2)}) copy-start(f32[8,2048]{1,0:T(8,128)S(1)} %scatter.32.gains_in) | copy-start | bytes 196612
  806.3 4.7 copy-start.4
  808.1 4.4 copy-start.5
  808.1 5.4 copy-start.3
  811.0 3.8 copy-start.1
Sparse Core Ops, SparseCore 0:
  91.8 79.8 all-gather.7
  173.3 79.2 all-gather.3
  254.2 79.2 all-gather.5
  386.0 74.6 reduce-scatter.5
  462.9 77.2 reduce-scatter.3
  542.3 77.2 reduce-scatter.7

commit v3 on v1

--- a/solution.py
+++ b/solution.py
@@ -4,6 +4,8 @@
 import jax
 import jax.numpy as jnp
 from jax import lax
+from jax.experimental import pallas as pl
+from jax.experimental.pallas import tpu as pltpu
 from jax.sharding import Mesh, PartitionSpec as P
 
 BF = jnp.bfloat16
@@ -120,7 +122,7 @@
     return collect(mine, inner).astype(F32)
 
 
-def body(
+def plain_body(
     hidden_in, doc_starts, attn_gain, w_query, w_key, w_value, query_gain, key_gain,
     w_out, mlp_gain, w_gate, w_up, w_down, cotangent, *, groups, inner, halves,
 ):
@@ -236,6 +238,1191 @@
     )
 
 
+MESH = pl.DeviceIdType.MESH
+ANY = pl.BlockSpec(memory_space=pl.ANY)
+VMEM = pl.BlockSpec(memory_space=pltpu.VMEM)
+SMEM = pl.BlockSpec(memory_space=pltpu.SMEM)
+DMA = pltpu.SemaphoreType.DMA
+LIMIT = 62 * 1024 * 1024
+
+
+def flip(index, mask):
+    if mask == 1:
+        return index + 1 - 2 * lax.rem(index, 2)
+    if mask == 2:
+        return lax.rem(index + 2, 4)
+    return 3 - index
+
+
+def meet(peers):
+    barrier = pltpu.get_barrier_semaphore()
+    for peer in peers:
+        pl.semaphore_signal(barrier, inc=1, device_id=peer, device_id_type=MESH)
+    pl.semaphore_wait(barrier, len(peers))
+
+
+def remote(src, dst, sems, k, peer):
+    return pltpu.make_async_remote_copy(
+        src_ref=src, dst_ref=dst, send_sem=sems[0].at[k], recv_sem=sems[1].at[k],
+        device_id=peer, device_id_type=MESH,
+    )
+
+
+def at(start, size):
+    return pl.ds(pl.multiple_of(start, size), size)
+
+
+def tp_peers(i, m):
+    return {"i": flip(i, 1)}, {"m": 1 - m}, {"i": flip(i, 2)}
+
+
+class TpGather:
+    def __init__(self, piece, full, sems, base, i, m):
+        rows, cols = piece.shape
+        half = rows // 2
+        core, across, along = tp_peers(i, m)
+
+        def slot(a, b, part=None):
+            if part is None:
+                return full.at[at(a * rows, rows), at(b * cols, cols)]
+            return full.at[at(a * rows + part * half, half), at(b * cols, cols)]
+
+        def go(src, dst, k, peer):
+            return remote(src, dst, sems, base + k, peer)
+
+        mine, far = slot(i, m), flip(i, 2)
+        self.local = pltpu.make_async_copy(piece, mine, sems[2].at[base // 8])
+        self.copies = [
+            go(piece, mine, 0, core),
+            go(piece, mine, 1, across),
+            go(piece, mine, 2, along),
+            go(slot(i, 1 - m, 0), slot(i, 1 - m, 0), 3, along),
+            go(slot(i, 1 - m), slot(i, 1 - m), 4, core),
+            go(slot(far, m, 1), slot(far, m, 1), 5, across),
+            go(slot(far, m), slot(far, m), 6, core),
+            go(slot(far, 1 - m), slot(far, 1 - m), 7, core),
+        ]
+
+    def start(self):
+        for k in (1, 2, 0):
+            self.copies[k].start()
+        self.local.start()
+
+    def relay(self):
+        self.copies[1].wait_recv()
+        self.copies[3].start()
+        self.copies[4].start()
+        self.copies[2].wait_recv()
+        self.copies[5].start()
+        self.copies[6].start()
+
+    def relay_far(self):
+        self.copies[3].wait_recv()
+        self.copies[5].wait_recv()
+        self.copies[7].start()
+
+    def finish(self):
+        for k in (0, 4, 6, 7):
+            self.copies[k].wait_recv()
+        for copy in self.copies:
+            copy.wait_send()
+        self.local.wait()
+
+
+def add_rows(target, first, second, step=64):
+    rows = target.shape[0]
+
+    @pl.loop(0, rows, step=step)
+    def _(r):
+        span = pl.ds(pl.multiple_of(r, step), step)
+        total = first[span, :].astype(F32) + second[span, :].astype(F32)
+        target[span, :] = total.astype(target.dtype)
+
+
+def tp_reduce_scratch(rows, cols, halves):
+    return [
+        pltpu.VMEM((2, rows, cols * halves), BF),
+        pltpu.VMEM((2, rows, cols * halves), BF),
+        pltpu.VMEM((2, rows // 2, cols), BF),
+        pltpu.VMEM((rows // 2, cols * halves), BF),
+        pltpu.VMEM((2, rows // 2, cols), BF),
+        DMA((7,)), DMA((7,)), DMA((2,)),
+    ]
+
+
+class TpReduce:
+    def __init__(self, parts, out, scratch, i, m):
+        own, mate, by_x, by_y, last, send, recv, load = scratch
+        rows, cols = out.shape
+        half = rows // 2
+        core, across, along = tp_peers(i, m)
+        sems = (send, recv)
+        self.args = (own, mate, by_x, by_y, last, out, m, rows, cols, half)
+
+        def seq(a):
+            return parts.at[at(a * rows, rows), :]
+
+        self.loads = [
+            pltpu.make_async_copy(seq(flip(i, 2)), own.at[1], load.at[1]),
+            pltpu.make_async_copy(seq(i), own.at[0], load.at[0]),
+        ]
+        theirs = at((1 - m) * cols, cols)
+        ours = at(m * cols, cols)
+        low, high = pl.ds(0, half), pl.ds(half, half)
+        self.copies = [
+            remote(seq(flip(i, 3)), mate.at[1], sems, 0, core),
+            remote(seq(flip(i, 1)), mate.at[0], sems, 1, core),
+            remote(own.at[1, low, theirs], by_x.at[1], sems, 2, across),
+            remote(own.at[0, low, theirs], by_x.at[0], sems, 3, across),
+            remote(own.at[1, high, :], by_y, sems, 4, along),
+            remote(own.at[1, low, ours], last.at[0], sems, 5, along),
+            remote(own.at[0, high, theirs], last.at[1], sems, 6, across),
+        ]
+        self.ours = ours
+
+    def start(self):
+        for k in (0, 1):
+            self.copies[k].start()
+            self.loads[k].start()
+
+    def run(self):
+        own, mate, by_x, by_y, last, out, m, rows, cols, half = self.args
+        copies, ours = self.copies, self.ours
+        low, high = pl.ds(0, half), pl.ds(half, half)
+        for side, k in ((1, 0), (0, 1)):
+            self.loads[k].wait()
+            copies[k].wait_recv()
+            add_rows(own.at[side], own.at[side], mate.at[side])
+            if side == 1:
+                copies[2].start()
+                copies[4].start()
+            else:
+                copies[3].start()
+        copies[2].wait_recv()
+        add_rows(own.at[1, low, ours], own.at[1, low, ours], by_x.at[1])
+        copies[5].start()
+        copies[4].wait_recv()
+        add_rows(own.at[0, high, :], own.at[0, high, :], by_y)
+        copies[6].start()
+        copies[3].wait_recv()
+        add_rows(own.at[0, low, ours], own.at[0, low, ours], by_x.at[0])
+        copies[5].wait_recv()
+        add_rows(out.at[low, :], own.at[0, low, ours], last.at[0])
+        copies[6].wait_recv()
+        add_rows(out.at[high, :], own.at[0, high, ours], last.at[1])
+        for copy in copies:
+            copy.wait_send()
+
+
+def tp_fold_scratch(rows, cols, halves):
+    return [
+        pltpu.VMEM((2, rows, cols * halves), BF),
+        pltpu.VMEM((2, rows // 2, cols), BF),
+        pltpu.VMEM((rows // 2, cols * halves), BF),
+        pltpu.VMEM((2, rows // 2, cols), BF),
+        DMA((7,)), DMA((7,)),
+    ]
+
+
+class TpFold:
+    def __init__(self, parts, out, scratch, i, m):
+        mate, by_x, by_y, last, send, recv = scratch
+        rows, cols = out.shape
+        half = rows // 2
+        core, across, along = tp_peers(i, m)
+        sems = (send, recv)
+        mate, by_x, last = [[v[k] if isinstance(v, list) else v.at[k] for k in range(2)] for v in (mate, by_x, last)]
+
+        def seq(a):
+            return parts.at[at(a * rows, rows), :]
+
+        def piece(a, part, b):
+            return parts.at[at(a * rows + part * half, half), at(b * cols, cols)]
+
+        far = flip(i, 2)
+        self.mine = [seq(i), seq(far)]
+        self.copies = [
+            remote(seq(flip(i, 3)), mate[1], sems, 0, core),
+            remote(seq(flip(i, 1)), mate[0], sems, 1, core),
+            remote(piece(far, 0, 1 - m), by_x[1], sems, 2, across),
+            remote(piece(i, 0, 1 - m), by_x[0], sems, 3, across),
+            remote(parts.at[at(far * rows + half, half), :], by_y, sems, 4, along),
+            remote(piece(far, 0, m), last[0], sems, 5, along),
+            remote(piece(i, 1, 1 - m), last[1], sems, 6, across),
+        ]
+        self.low_far, self.low, self.high = piece(far, 0, m), piece(i, 0, m), piece(i, 1, m)
+        self.high_all = parts.at[at(i * rows + half, half), :]
+        self.mate, self.by_x, self.by_y, self.last, self.out, self.half = mate, by_x, by_y, last, out, half
+
+    def send(self, k):
+        self.copies[k].start()
+
+    def side(self, k):
+        self.copies[1 - k].wait_recv()
+        add_rows(self.mine[k], self.mine[k], self.mate[k])
+        for n in ((2, 4) if k == 1 else (3,)):
+            self.copies[n].start()
+
+    def finish(self, meanwhile=None):
+        copies, half = self.copies, self.half
+        copies[2].wait_recv()
+        add_rows(self.low_far, self.low_far, self.by_x[1])
+        copies[5].start()
+        copies[4].wait_recv()
+        add_rows(self.high_all, self.high_all, self.by_y)
+        copies[6].start()
+        if meanwhile is not None:
+            meanwhile()
+        copies[3].wait_recv()
+        add_rows(self.low, self.low, self.by_x[0])
+        copies[5].wait_recv()
+        add_rows(self.out.at[pl.ds(0, half), :], self.low, self.last[0])
+        copies[6].wait_recv()
+        add_rows(self.out.at[pl.ds(half, half), :], self.high, self.last[1])
+
+    def wait_sends(self):
+        for copy in self.copies:
+            copy.wait_send()
+
+
+def pick(step, i):
+    return jnp.where(step == 0, flip(i, 3), jnp.where(step == 1, flip(i, 1), jnp.where(step == 2, flip(i, 2), i)))
+
+
+class LineGather:
+    def __init__(self, own, full, sems, base, groups, t):
+        self.own, self.full, self.sems, self.base, self.groups, self.t = own, full, sems, base, groups, t
+        self.rows = full.shape[0] // groups
+
+    def block(self, b):
+        return self.full.at[at(b * self.rows, self.rows), :]
+
+    def go(self, b, k, step, own=False):
+        n = self.base + (0 if step > 0 else self.groups - 1) + k
+        src = self.own if own else self.block(b)
+        return remote(src, self.block(b), self.sems, n, {"t": self.t + step})
+
+    def send(self, k):
+        t, last = self.t, self.groups - 1
+
+        @pl.when((t < last) & (t - k >= 0))
+        def _():
+            self.go(t - k, k, 1, k == 0).start()
+
+        @pl.when((t > 0) & (t + k <= last))
+        def _():
+            self.go(t + k, k, -1, k == 0).start()
+
+    def arrive(self, k):
+        t, last = self.t, self.groups - 1
+
+        @pl.when(t - k - 1 >= 0)
+        def _():
+            self.go(t - k - 1, k, 1).wait_recv()
+
+        @pl.when(t + k + 1 <= last)
+        def _():
+            self.go(t + k + 1, k, -1).wait_recv()
+
+    def pass_on(self, k):
+        self.arrive(k - 1)
+        if k < self.groups - 1:
+            self.send(k)
+
+    def wait_sends(self):
+        t, last = self.t, self.groups - 1
+        for k in range(self.groups - 1):
+            @pl.when((t < last) & (t - k >= 0))
+            def _():
+                self.go(t - k, k, 1, k == 0).wait_send()
+
+            @pl.when((t > 0) & (t + k <= last))
+            def _():
+                self.go(t + k, k, -1, k == 0).wait_send()
+
+
+class LineReduce:
+    def __init__(self, grads, ups, downs, back, stage, spare, load, sems, base, move_sems, t, i, before):
+        self.grads, self.ups, self.downs, self.back, self.stage, self.spare = grads, ups, downs, back, stage, spare
+        self.load, self.sems, self.base, self.move_sems = load, sems, base, move_sems
+        self.t, self.i, self.before = t, i, before
+
+    def up(self, k, src):
+        return remote(src, self.ups.at[k], self.sems, self.base + k, {"t": self.t + 1})
+
+    def down(self, k, src):
+        return remote(src, self.downs.at[k], self.sems, self.base + 3 + k, {"t": self.t - 1})
+
+    def first(self, b):
+        if b > 0:
+            @pl.when(self.t == 0)
+            def _():
+                self.up(3 - b, self.grads.at[b]).start()
+        if b < 3:
+            @pl.when(self.t == 3)
+            def _():
+                self.down(b, self.grads.at[b]).start()
+
+    def total(self, place, sources):
+        loads = [pltpu.make_async_copy(sources[0], self.stage.at[place], self.load.at[0])]
+        loads += [pltpu.make_async_copy(v, self.spare, self.load.at[1]) for v in sources[1:]]
+        loads[0].start()
+        loads[1].start()
+        loads[0].wait()
+        for n, copy in enumerate(loads[1:]):
+            if n > 0:
+                copy.start()
+            copy.wait()
+            add_rows(self.stage.at[place], self.stage.at[place], self.spare)
+
+    def relay(self, place, way, k):
+        make = self.up if way == "up" else self.down
+        slots = self.ups if way == "up" else self.downs
+        make(k, slots.at[k]).wait_recv()
+        self.total(place, [slots.at[k], self.grads.at[3 - k if way == "up" else k]])
+        make(k, self.stage.at[place]).start()
+
+    def relayed(self, place, way, k):
+        (self.up if way == "up" else self.down)(k, self.stage.at[place]).wait_send()
+
+    PLAN = {1: ((0, "up", 0), (1, "up", 1), (2, "down", 0)), 2: ((0, "down", 0), (1, "up", 0), (2, "down", 1))}
+
+    def hop(self, places):
+        for t, plan in self.PLAN.items():
+            @pl.when(self.t == t)
+            def _():
+                for place, way, k in plan:
+                    if place in places:
+                        if self.before is not None:
+                            self.before.relayed(place, way, k)
+                        self.relay(place, way, k)
+
+    def moves(self):
+        lanes = self.stage.shape[2] // 4
+        found = []
+        for j in (2, 3, 1):
+            p = flip(self.i, j)
+            view = self.stage.at[3, :, at(p * lanes, lanes)]
+            found.append(remote(view, self.back.at[self.i], self.move_sems, self.base // 6 * 4 + j, {"i": p}))
+        view = self.stage.at[3, :, at(self.i * lanes, lanes)]
+        return found, pltpu.make_async_copy(view, self.back.at[self.i], self.load.at[2])
+
+    def close(self):
+        if self.before is not None:
+            self.before.closed()
+        for t in range(4):
+            @pl.when(self.t == t)
+            def _():
+                sources = [self.grads.at[t]]
+                if t > 0:
+                    self.up(3 - t, self.ups.at[3 - t]).wait_recv()
+                    sources.append(self.ups.at[3 - t])
+                if t < 3:
+                    self.down(t, self.downs.at[t]).wait_recv()
+                    sources.append(self.downs.at[t])
+                self.total(3, sources)
+
+        found, keep = self.moves()
+        for move in found:
+            move.start()
+        keep.start()
+
+    def closed(self):
+        found, keep = self.moves()
+        for move in found:
+            move.wait()
+        keep.wait()
+
+    def wait_firsts(self):
+        @pl.when(self.t == 0)
+        def _():
+            for k in range(3):
+                self.up(k, self.grads.at[3 - k]).wait_send()
+
+        @pl.when(self.t == 3)
+        def _():
+            for k in range(3):
+                self.down(k, self.grads.at[k]).wait_send()
+
+    def wait_relays(self):
+        for t, plan in self.PLAN.items():
+            @pl.when(self.t == t)
+            def _():
+                for place, way, k in plan:
+                    self.relayed(place, way, k)
+
+
+def tp_group(i, m):
+    return list(tp_peers(i, m))
+
+
+def row_loop(rows, step=64):
+    def wrap(f):
+        @pl.loop(0, rows, step=step)
+        def _(r):
+            f(pl.ds(pl.multiple_of(r, step), step))
+
+    return wrap
+
+
+def mlp_kernel(groups, piece_in, grad_full, first_w, other_w, middle, stat, cot, gain,
+               rest_w, grads, ups, downs, back, out_parts, d_middle, d_gain, piece, *scratch):
+    (x, g, w, act, act_t, fresh, stage, spare, sums, other, load, g_send, g_recv, g_local, z_send, z_recv,
+     r_send, r_recv, m_send, m_recv, f_send, f_recv, s_send, s_recv, free) = scratch
+    t, i, m = lax.axis_index("t"), lax.axis_index("i"), lax.axis_index("m")
+    others = [{"i": flip(i, j)} for j in (1, 2, 3)]
+    meet(others + [{"m": 1 - m}] + [{"t": flip(t, j)} for j in (1, 2, 3)])
+    tokens, wide = x.shape
+    rows, part = middle.shape
+    unit = w.shape[2] // 3
+    two, three = 2 * unit, 3 * unit
+    block = wide // groups
+    gather = TpGather(piece_in, x, (g_send, g_recv, g_local), 0, i, m)
+    gather.start()
+    lines = [LineGather(other_w.at[c], rest_w.at[c], (z_send, z_recv), 6 * c, groups, t) for c in range(2)]
+    lines[0].send(0)
+    take_g = pltpu.make_async_copy(grad_full, g, load.at[3])
+    take_w = [pltpu.make_async_copy(first_w.at[c], w.at[c], load.at[4 + c]) for c in range(2)]
+    own = [
+        pltpu.make_async_copy(other_w.at[c], rest_w.at[c, at(t * block, block), :], load.at[6 + c]) for c in range(2)
+    ]
+    rest = [pltpu.make_async_copy(rest_w.at[c], w.at[2 + c], load.at[8 + c]) for c in range(2)]
+    for copy in [take_w[0], take_g, take_w[1]] + own:
+        copy.start()
+    gather.relay()
+    lines[0].pass_on(1)
+    gather.relay_far()
+    lines[0].pass_on(2)
+    lines[1].send(0)
+    for copy in [take_w[0], take_g, take_w[1]] + own:
+        copy.wait()
+    gather.finish()
+    reds = []
+    for c in range(3):
+        reds.append(LineReduce(
+            grads.at[c], ups.at[c], downs.at[c], back.at[c], stage, spare, load, (r_send, r_recv), 6 * c,
+            (m_send, m_recv), t, i, reds[-1] if reds else None))
+    order = (3, 0, 2, 1)
+    events = {
+        (0, 3): lambda: (lines[0].pass_on(3), rest[0].start()),
+        (1, 0): lambda: lines[1].pass_on(1),
+        (1, 3): lambda: reds[0].hop((0,)),
+        (1, 5): lambda: lines[1].pass_on(2),
+        (2, 0): lambda: reds[0].hop((1, 2)),
+        (2, 1): lambda: (lines[1].pass_on(3), rest[1].start()),
+        (2, 5): lambda: reds[0].close(),
+        (3, 0): lambda: reds[1].hop((0,)),
+        (3, 5): lambda: reds[1].hop((1, 2)),
+    }
+
+    def hook(c, slot):
+        for (when_c, when_slot), run in events.items():
+            if when_slot == slot:
+                @pl.when(c == when_c)
+                def _():
+                    run()
+
+    def stored(c, n):
+        return pltpu.make_async_copy(fresh.at[n % 2], grads.at[c, order[n]], load.at[10 + n % 2])
+
+    @pl.loop(0, 4)
+    def _(c):
+        for n in range(2):
+            @pl.when(c == 2 + n)
+            def _():
+                rest[n].wait()
+
+        for n in range(4):
+            span = pl.ds(n * rows, rows)
+            d_inner = nn(g[span, :], w[c, :, two:three])
+            both = nn(x[span, :], w[c, :, 0:two])
+            gate, up = both[:, :unit], both[:, unit:]
+            sig = jax.nn.sigmoid(gate)
+            silu = gate * sig
+            d_gate = (d_inner * up * sig * (1.0 + gate * (1.0 - sig))).astype(BF)
+            d_up = (d_inner * silu).astype(BF)
+            inner = (silu * up).astype(BF)
+            for k, v in enumerate((d_gate, d_up, inner)):
+                act[c, span, k * unit:(k + 1) * unit] = v
+                act_t[k * unit:(k + 1) * unit, span] = v.T
+            hook(c, n)
+        for n in range(4):
+            cols = pl.ds(order[n] * block, block)
+            fresh[n % 2, 0:two, :] = nn(act_t[0:two, :], x[:, cols]).astype(BF)
+            fresh[n % 2, two:three, :] = nn(act_t[two:three, :], g[:, cols]).astype(BF)
+            stored(c, n).start()
+            for done in ((n - 1,) if n < 3 else (2, 3)):
+                if done >= 0:
+                    stored(c, done).wait()
+                    for q in range(3):
+                        @pl.when(c == q)
+                        def _():
+                            reds[q].first(order[done])
+            hook(c, 4 + n)
+
+    for peer in tp_group(i, m):
+        pl.semaphore_signal(free, inc=1, device_id=peer, device_id_type=MESH)
+    quarter, half = rows // 2, part
+    base = 2 * rows
+    lists = [
+        [g.at[pl.ds(0, rows), :], g.at[pl.ds(rows, rows), :]],
+        [g.at[pl.ds(base, quarter), pl.ds(k * half, half)] for k in range(2)],
+        g.at[pl.ds(base + quarter, quarter), :],
+        [g.at[pl.ds(base + 2 * quarter, quarter), pl.ds(k * half, half)] for k in range(2)],
+    ]
+    fold = TpFold(x, d_middle, lists + [f_send, f_recv], i, m)
+
+    def product(span, cols, low, high):
+        total = nt(act[0, span, low:high], w[0, cols, low:high])
+        for c in range(1, 4):
+            total += nt(act[c, span, low:high], w[c, cols, low:high])
+        return total.astype(BF)
+
+    def tiles(f):
+        @pl.loop(0, wide, step=512)
+        def _(col):
+            f(pl.ds(pl.multiple_of(col, 512), 512))
+
+    @pl.loop(0, 4)
+    def _(step):
+        span = at(pick(step, i) * rows, rows)
+
+        @tiles
+        def _(cols):
+            x[span, cols] = product(span, cols, 0, two)
+
+        @pl.when(step == 0)
+        def _():
+            pl.semaphore_wait(free, 3)
+            fold.send(0)
+
+        @pl.when(step == 1)
+        def _():
+            fold.send(1)
+            reds[1].close()
+
+        @pl.when(step == 2)
+        def _():
+            fold.side(1)
+
+    fold.side(0)
+    reds[2].hop((0,))
+
+    def project(first):
+        @pl.loop(first, first + 2)
+        def _(s):
+            span = at(s * rows, rows)
+
+            @tiles
+            def _(cols):
+                act_t[0:rows, cols] = product(span, cols, two, three)
+
+            put = pltpu.make_async_copy(act_t.at[pl.ds(0, rows), :], out_parts.at[span, :], load.at[10])
+            put.start()
+            put.wait()
+
+    project(0)
+    fold.finish(lambda: project(2))
+    d_gain[...] = jnp.zeros_like(d_gain)
+    reds[2].hop((1, 2))
+
+    @row_loop(rows)
+    def _(span):
+        dn, v, r = d_middle[span, :], middle[span, :], stat[span, :]
+        sums[span, :] = jnp.broadcast_to(jnp.sum(dn * gain[...] * v, axis=-1, keepdims=True), r.shape)
+        d_gain[0:1, :] += jnp.sum(dn * v * r[:, :1], axis=0, keepdims=True)
+
+    swap = remote(sums, other, (s_send, s_recv), 0, {"m": 1 - m})
+    swap.start()
+    swap.wait()
+
+    @row_loop(rows)
+    def _(span):
+        r = stat[span, :]
+        factor = (r * r * r * ((sums[span, :] + other[span, :]) / wide))[:, :1]
+        d = cot[span, :].astype(F32) + r[:, :1] * (d_middle[span, :] * gain[...]) - middle[span, :] * factor
+        d_middle[span, :] = d
+        piece[span, :] = d.astype(BF)
+
+    fold.wait_sends()
+    for line in lines:
+        line.wait_sends()
+    reds[2].close()
+    for red in reds:
+        red.wait_firsts()
+    reds[2].wait_relays()
+    reds[2].closed()
+
+
+def shape(dims, dtype):
+    return jax.ShapeDtypeStruct(dims, dtype)
+
+
+def comm_call(kernel, ins, outs, scratch, number):
+    return pl.pallas_call(
+        kernel,
+        out_shape=[s for s, _ in outs],
+        in_specs=ins,
+        out_specs=[b for _, b in outs],
+        scratch_shapes=scratch,
+        compiler_params=pltpu.CompilerParams(
+            collective_id=number, has_side_effects=True, vmem_limit_bytes=LIMIT
+        ),
+    )
+
+
+def allow(cut, q0, qn, kn):
+    q = q0 + lax.broadcasted_iota(jnp.int32, (qn, kn), 0)
+    k = lax.broadcasted_iota(jnp.int32, (qn, kn), 1)
+    doc_q = (q >= cut[0]).astype(jnp.int32) + (q >= cut[1]).astype(jnp.int32)
+    doc_k = (k >= cut[0]).astype(jnp.int32) + (k >= cut[1]).astype(jnp.int32)
+    return (doc_q == doc_k) & (k <= q)
+
+
+def turn(v):
+    half = v.shape[1] // 2
+    return jnp.concatenate([-v[:, half:], v[:, :half]], axis=1)
+
+
+def turn_back(v):
+    half = v.shape[1] // 2
+    return jnp.concatenate([v[:, half:], -v[:, :half]], axis=1)
+
+
+def fore_kernel(groups, heads, hd, cuts, pack, gate, up, down, hidden, cot, qk_gain, table,
+                attn, first_w, other_w, normed_out, pre, qkv, stats, mixed, middle, stat, piece, grad_full, gain_rows,
+                *scratch):
+    fold_scratch, (full, weights, other, load, w_send, w_recv, w_local, z_send, z_recv,
+                   g_send, g_recv, g_local, s_send, s_recv) = scratch[:6], scratch[6:]
+    x = full
+    t, i, m = lax.axis_index("t"), lax.axis_index("i"), lax.axis_index("m")
+    rows, wide = hidden.shape[0], x.shape[1]
+    nq, kv = heads * hd, (heads + 2) * hd
+    shard = pack.shape[1]
+    unit = first_w.shape[2] // 3
+    others = [{"i": flip(i, j)} for j in (1, 2, 3)]
+    meet(others + [{"m": 1 - m}] + [{"t": flip(t, j)} for j in (1, 2, 3)])
+    mine = attn.at[at((t * 4 + i) * shard, shard), :]
+    spread = [remote(pack.at[flip(i, j)], mine, (w_send, w_recv), j - 1, others[j - 1]) for j in (2, 3, 1)]
+    own = pltpu.make_async_copy(pack.at[i], mine, w_local.at[0])
+    for copy in spread:
+        copy.start()
+    own.start()
+    gather_h = TpGather(hidden, full, (g_send, g_recv, g_local), 0, i, m)
+    gather_g = TpGather(cot, grad_full, (g_send, g_recv, g_local), 8, i, m)
+    gather_h.start()
+
+    def chunk(c):
+        if c < 2:
+            place = first_w.at[c, at((t * 4 + i) * shard, shard), :]
+        else:
+            place = other_w.at[c - 2, at(i * shard, shard), :]
+        found, kept = [], []
+        for n, src in enumerate((gate, up, down)):
+            dst = place.at[:, pl.ds(n * unit, unit)]
+
+            def view(p):
+                return src.at[:, at(p * 4 * unit + c * unit, unit)]
+
+            for j in (2, 3, 1):
+                found.append(remote(view(flip(i, j)), dst, (w_send, w_recv), 3 + 9 * c + 3 * n + j - 1, others[j - 1]))
+            kept.append(pltpu.make_async_copy(view(i), dst, w_local.at[1 + 3 * c + n]))
+        return found, kept
+
+    chunks = [chunk(c) for c in range(4)]
+
+    def begin(c):
+        for copy in chunks[c][0] + chunks[c][1]:
+            copy.start()
+
+    def landed(c):
+        for copy in chunks[c][0]:
+            copy.wait_recv()
+        for copy in chunks[c][1]:
+            copy.wait()
+
+    sems = (z_send, z_recv)
+    block = 4 * shard
+    line = LineGather(attn.at[at(t * block, block), :], attn, sems, 0, groups, t)
+    lines = [
+        LineGather(first_w.at[c, at(t * block, block), :], first_w.at[c], sems, 6 * c + 6, groups, t) for c in range(2)
+    ]
+    own.wait()
+    for copy in spread:
+        copy.wait_recv()
+    line.send(0)
+    begin(0)
+    line.pass_on(1)
+    gather_h.relay()
+    begin(1)
+    line.pass_on(2)
+    gather_h.relay_far()
+    gather_g.start()
+    begin(2)
+    begin(3)
+    landed(0)
+    lines[0].send(0)
+    line.pass_on(3)
+    landed(1)
+    lines[1].send(0)
+    fill = pltpu.make_async_copy(attn, weights, load.at[0])
+    fill.start()
+    gather_h.finish()
+    fill.wait()
+    gain_rows[...] = jnp.transpose(weights[:, kv + nq:kv + nq + 128].astype(F32))[0:8, :]
+    gain = gain_rows[0:1, :]
+    gain_two = gain_rows[1:2, at(m * (wide // 2), wide // 2)]
+    parts = full
+    fold = TpFold(parts, middle, fold_scratch, i, m)
+
+    @pl.loop(0, 4)
+    def _(step):
+        s = pick(step, i)
+        start = s * rows
+        def sub(r, size):
+            return pl.ds(pl.multiple_of(start + r, size), size)
+
+        cut = (cuts[s, 0], cuts[s, 1])
+
+        @pl.loop(0, rows, step=64)
+        def _(r):
+            span = sub(r, 64)
+            v = x[span, :].astype(F32)
+            scale = lax.rsqrt(jnp.mean(v * v, axis=-1, keepdims=True) + EPS)
+            stats[span, :] = jnp.broadcast_to(scale, (64, stats.shape[1]))
+            x[span, :] = (v * scale * gain_rows[0:1, :]).astype(BF)
+
+        everything = sub(0, rows)
+        keep = pltpu.make_async_copy(x.at[everything, :], normed_out.at[everything, :], load.at[1])
+        keep.start()
+        heads_pre = nn(x[everything, :], weights[:, :kv])
+        pre[everything, :] = heads_pre
+        c, sn = table[everything, 0:hd], table[everything, hd:2 * hd]
+        for h in range(heads + 1):
+            lanes = slice(h * hd, (h + 1) * hd)
+            n = rms_rows(heads_pre[:, lanes], qk_gain[0:1, :] if h < heads else qk_gain[1:2, :])
+            qkv[everything, lanes] = (n * c + turn(n) * sn).astype(BF)
+        qkv[everything, nq + hd:kv] = heads_pre[:, nq + hd:kv].astype(BF)
+        half = rows // 2
+        for b in range(2):
+            kn = (b + 1) * half
+            span = sub(b * half, half)
+            mask = allow(cut, b * half, half, kn)
+            keys, values = qkv[pl.ds(start, kn), nq:nq + hd], qkv[pl.ds(start, kn), nq + hd:kv]
+            for h in range(heads):
+                q = qkv[span, h * hd:(h + 1) * hd]
+                scores = jnp.where(mask, nt(q, keys) * (hd ** -0.5), -1e30)
+                top = jnp.max(scores, axis=-1, keepdims=True)
+                e = jnp.exp(scores - top)
+                total = jnp.sum(e, axis=-1, keepdims=True)
+                probs = (e * (1.0 / total)).astype(BF)
+                stats[span, h:h + 1] = top + jnp.log(total)
+                mixed[span, h * hd:(h + 1) * hd] = nn(probs, values).astype(BF)
+
+        keep.wait()
+
+        @pl.loop(0, wide, step=512)
+        def _(col):
+            cols = pl.ds(pl.multiple_of(col, 512), 512)
+            parts[everything, cols] = nt(mixed[everything, :], weights[cols, kv:kv + nq]).astype(BF)
+
+        @pl.when(step == 0)
+        def _():
+            fold.send(0)
+            gather_g.relay()
+
+        @pl.when(step == 1)
+        def _():
+            fold.send(1)
+            gather_g.relay_far()
+            lines[0].pass_on(1)
+
+        @pl.when(step == 2)
+        def _():
+            fold.side(1)
+            lines[1].pass_on(1)
+
+    fold.side(0)
+    lines[0].pass_on(2)
+    fold.finish(lambda: lines[1].pass_on(2))
+
+    @row_loop(rows)
+    def _(span):
+        v = middle[span, :] + hidden[span, :].astype(F32)
+        middle[span, :] = v
+        stat[span, :] = jnp.broadcast_to(jnp.sum(v * v, axis=-1, keepdims=True), stat[span, :].shape)
+
+    swap = remote(stat, other, (s_send, s_recv), 0, {"m": 1 - m})
+    swap.start()
+    swap.wait()
+
+    @row_loop(rows)
+    def _(span):
+        r = lax.rsqrt((stat[span, :] + other[span, :]) / wide + EPS)
+        stat[span, :] = r
+        piece[span, :] = (middle[span, :] * r[:, :1] * gain_two).astype(BF)
+
+    gather_g.finish()
+    fold.wait_sends()
+    for c in range(4):
+        if c >= 2:
+            landed(c)
+        for copy in chunks[c][0]:
+            copy.wait_send()
+    for copy in spread:
+        copy.wait_send()
+    for one in lines:
+        one.pass_on(3)
+    for one in [line] + lines:
+        one.wait_sends()
+
+
+def aft_kernel(groups, heads, hd, cuts, piece, normed, out_parts, attn, pre_in, middle, d_middle, qkv_in, stats_in,
+               mixed_in, table_in, mlp_grads, qk_gain, hidden, gain, d_gain_two,
+               d_input, block_out, back, gains, ups, downs, mlp_back, *scratch):
+    fold_scratch, out_scratch = scratch[:6], scratch[6:14]
+    (dm, nrm, pre, qkv, stats, mixed, table, weights, res, acc, grads, up_in, down_in, total, d_mix, d_pre, d_kv, qk_sum, sums, other,
+     g_in, load, a_send, a_recv, a_local, send, recv, z_send, z_recv, g_send, g_recv, s_send, s_recv,
+     local, stage, spare, line_load, r_send, r_recv, m_send, m_recv) = scratch[14:]
+    t, i, m = lax.axis_index("t"), lax.axis_index("i"), lax.axis_index("m")
+    others = [{"i": flip(i, j)} for j in (1, 2, 3)]
+    meet(others + [{"m": 1 - m}] + [{"t": flip(t, j)} for j in (1, 2, 3)])
+    rows, wide = hidden.shape[0], dm.shape[1]
+    nq, kv = heads * hd, (heads + 2) * hd
+    scale = hd ** -0.5
+    gather = TpGather(piece, dm, (a_send, a_recv, a_local), 0, i, m)
+    gather.start()
+    red = LineReduce(mlp_grads.at[3], ups, downs, mlp_back, stage, spare, line_load, (r_send, r_recv), 0,
+                     (m_send, m_recv), t, i, None)
+    for b in (3, 0, 2, 1):
+        red.first(b)
+    fill = pltpu.make_async_copy(attn.at[:, pl.ds(0, kv + nq)], weights, load.at[2])
+    fill.start()
+
+    def fetch(step):
+        span = at(pick(step, i) * rows, rows)
+        return (pltpu.make_async_copy(normed.at[span, :], nrm, load.at[0]),
+                *[pltpu.make_async_copy(src.at[span, :], dst, load.at[n]) for n, src, dst in (
+                    (1, pre_in, pre), (4, qkv_in, qkv), (5, stats_in, stats), (6, mixed_in, mixed),
+                    (7, table_in, table))])
+
+    take = pltpu.make_async_copy(middle, d_input, load.at[3])
+    take.start()
+    two = TpReduce(out_parts, res, out_scratch, i, m)
+    acc[...] = jnp.zeros_like(acc)
+    qk_sum[...] = jnp.zeros_like(qk_sum)
+    fold = TpFold(dm, d_input, fold_scratch, i, m)
+    fill.wait()
+    gather.relay()
+    red.hop((0,))
+    gather.relay_far()
+    two.start()
+    red.hop((1, 2))
+    gather.finish()
+
+    @pl.loop(0, 4)
+    def _(step):
+        s = pick(step, i)
+        start = s * rows
+        for copy in fetch(step):
+            copy.start()
+
+        def sub(r, size):
+            return pl.ds(pl.multiple_of(start + r, size), size)
+
+        cut = (cuts[s, 0], cuts[s, 1])
+        everything = sub(0, rows)
+        d_mix[...] = nn(dm[everything, :], weights[:, kv:kv + nq]).astype(BF)
+        d_kv[...] = jnp.zeros_like(d_kv)
+        half = rows // 2
+
+        def undo(h, grad):
+            lanes = slice(h * hd, (h + 1) * hd)
+            row = 0 if h < heads else 1
+            c, sn = table[:, 0:hd], table[:, hd:2 * hd]
+            u = c * grad + turn_back(sn * grad)
+            v = pre[:, lanes]
+            r = lax.rsqrt(jnp.mean(v * v, axis=-1, keepdims=True) + EPS)
+            qk_sum[0:1, row * hd:(row + 1) * hd] += jnp.sum(u * v * r, axis=0, keepdims=True)
+            scaled = u * qk_gain[row:row + 1, :]
+            undone = r * scaled - v * (r * r * r) * jnp.mean(scaled * v, axis=-1, keepdims=True)
+            d_pre[:, lanes] = undone.astype(BF)
+
+        for copy in fetch(step)[1:]:
+            copy.wait()
+        for h in range(heads):
+            lanes = slice(h * hd, (h + 1) * hd)
+            found = []
+            for b in range(2):
+                kn = (b + 1) * half
+                span = slice(b * half, kn)
+                mask = allow(cut, b * half, half, kn)
+                keys, values = qkv[0:kn, nq:nq + hd], qkv[0:kn, nq + hd:kv]
+                q, go = qkv[span, lanes], d_mix[span, lanes]
+                scores = jnp.where(mask, nt(q, keys) * scale, -1e30)
+                probs = jnp.exp(scores - stats[span, h:h + 1])
+                d_probs = nt(go, values)
+                inner = jnp.sum(probs * d_probs, axis=-1, keepdims=True)
+                d_scores = (probs * (d_probs - inner)).astype(BF)
+                found.append(nn(d_scores, keys) * scale)
+                d_kv[0:kn, 0:hd] += tn(d_scores, q) * scale
+                d_kv[0:kn, hd:2 * hd] += tn(probs.astype(BF), go)
+            undo(h, jnp.concatenate(found, axis=0))
+        undo(heads, d_kv[:, 0:hd])
+        d_pre[:, nq + hd:kv] = d_kv[:, hd:2 * hd].astype(BF)
+        fetch(step)[0].wait()
+
+        @pl.loop(0, wide, step=512)
+        def _(col):
+            cols = pl.ds(pl.multiple_of(col, 512), 512)
+            acc[0:kv, cols] += tn(d_pre[...], nrm[:, cols])
+            acc[kv:kv + nq, cols] += tn(mixed[...], dm[everything, cols])
+            dm[everything, cols] = nt(d_pre[...], weights[cols, 0:kv]).astype(BF)
+
+        @pl.when(step < 2)
+        def _():
+            @pl.when(step == 0)
+            def _():
+                fold.send(0)
+
+            @pl.when(step == 1)
+            def _():
+                fold.send(1)
+
+        @pl.when(step == 2)
+        def _():
+            fold.side(1)
+
+        @pl.when(step == 3)
+        def _():
+            fold.side(0)
+
+        @pl.when(step == 0)
+        def _():
+            two.run()
+            take.wait()
+
+            @row_loop(rows)
+            def _(span):
+                block_out[span, :] = (d_input[span, :] + res[span, :]).astype(BF)
+
+            pltpu.make_async_copy(d_middle, res, load.at[3]).start()
+            red.close()
+
+    block = wide // groups
+
+    @pl.loop(0, groups)
+    def _(b):
+        cols = at(b * block, block)
+        grads[b] = acc[:, cols].astype(BF)
+
+    def up(k, src):
+        return remote(src, up_in.at[k], (z_send, z_recv), k, {"t": t + 1})
+
+    def down(k, src):
+        return remote(src, down_in.at[k], (z_send, z_recv), groups + k, {"t": t - 1})
+
+    @pl.when(t == 0)
+    def _():
+        for k in range(groups - 1):
+            up(k, grads.at[groups - 1 - k]).start()
+
+    @pl.when(t == groups - 1)
+    def _():
+        for k in range(groups - 1):
+            down(k, grads.at[k]).start()
+
+    def hop(k):
+        b = groups - 1 - k
+
+        @pl.when((t > 0) & (b > t))
+        def _():
+            up(k, up_in.at[k]).wait_recv()
+            add_rows(up_in.at[k], up_in.at[k], grads.at[b])
+            up(k, up_in.at[k]).start()
+
+        @pl.when((t < groups - 1) & (k < t))
+        def _():
+            down(k, down_in.at[k]).wait_recv()
+            add_rows(down_in.at[k], down_in.at[k], grads.at[k])
+            down(k, down_in.at[k]).start()
+
+    hop(0)
+    pltpu.make_async_copy(d_middle, res, load.at[3]).wait()
+    fold.finish(lambda: hop(1))
+    gains[...] = jnp.zeros_like(gains)
+    own_half = at(m * (wide // 2), wide // 2)
+    gains[1:2, own_half] = d_gain_two[0:1, :]
+    gains[2:3, :] = jnp.concatenate([qk_sum[0:1, :]] * (wide // (2 * hd)), axis=1)
+
+    @row_loop(rows)
+    def _(span):
+        dn, v = d_input[span, :], hidden[span, :].astype(F32)
+        r = stats[span, heads:heads + 1]
+        sums[span, :] = jnp.broadcast_to(jnp.sum(dn * gain[...] * v, axis=-1, keepdims=True), sums[span, :].shape)
+        gains[0:1, own_half] += jnp.sum(dn * v * r, axis=0, keepdims=True)
+
+    swap = remote(sums, other, (s_send, s_recv), 0, {"m": 1 - m})
+    swap.start()
+    ways = [{"i": flip(i, 1)}, {"m": 1 - m}, {"i": flip(i, 2)}, {"t": flip(t, 1)}, {"t": flip(t, 2)}]
+
+    def trade(k):
+        return remote(gains, g_in.at[k], (g_send, g_recv), k, ways[k])
+
+    trade(0).start()
+    swap.wait()
+
+    @row_loop(rows)
+    def _(span):
+        r = stats[span, heads:heads + 1]
+        factor = r * r * r * ((sums[span, :] + other[span, :]) / wide)[:, :1]
+        d = res[span, :] + r * (d_input[span, :] * gain[...])
+        d_input[span, :] = d - hidden[span, :].astype(F32) * factor
+
+    hop(2)
+    for b in range(groups):
+        @pl.when(t == b)
+        def _():
+            own = grads.at[b]
+            if b > 0:
+                up(groups - 1 - b, up_in.at[0]).wait_recv()
+                add_rows(total, own, up_in.at[groups - 1 - b])
+                own = total
+            if b < groups - 1:
+                down(b, down_in.at[0]).wait_recv()
+                add_rows(total, own, down_in.at[b])
+
+    sub_cols = block // 4
+    moves = []
+    for j in (2, 3, 1):
+        view = total.at[:, at(flip(i, j) * sub_cols, sub_cols)]
+        moves.append(remote(view, back.at[i], (send, recv), j, others[j - 1]))
+    keep = pltpu.make_async_copy(total.at[:, at(i * sub_cols, sub_cols)], back.at[i], local.at[0])
+    for move in moves:
+        move.start()
+    keep.start()
+    for k in range(5):
+        if k > 0:
+            trade(k).start()
+        trade(k).wait()
+        gains[...] += g_in[k]
+    for k in range(groups - 1):
+        @pl.when(t < groups - 1 - k)
+        def _():
+            up(k, up_in.at[k]).wait_send()
+
+        @pl.when(t > k)
+        def _():
+            down(k, down_in.at[k]).wait_send()
+
+    fold.wait_sends()
+    red.wait_firsts()
+    red.wait_relays()
+    red.closed()
+    keep.wait()
+    for move in moves:
+        move.wait()
+
+
+def fast_body(
+    hidden_in, doc_starts, attn_gain, w_query, w_key, w_value, query_gain, key_gain,
+    w_out, mlp_gain, w_gate, w_up, w_down, cotangent, *, groups, inner, halves,
+):
+    length, part = hidden_in.shape
+    shard = w_query.shape[0]
+    width, tokens = part * halves, length * inner
+    hd = query_gain.shape[0]
+    heads = w_query.shape[1] // inner // hd
+    nq, kv = heads * hd, (heads + 2) * hd
+    hidden_units = w_gate.shape[1] // inner
+    t_index, i_index, m_index = lax.axis_index("t"), lax.axis_index("i"), lax.axis_index("m")
+    cuts = lax.dynamic_slice_in_dim(doc_starts, t_index * inner, inner, 0)
+    cosine, sine_table, _ = jax.vmap(partial(tables, length=length, head_dim=hd))(cuts)
+    table = jnp.concatenate([cosine.reshape(tokens, hd), sine_table.reshape(tokens, hd)], axis=1)
+    qk_gain = jnp.zeros((8, hd), F32).at[0].set(query_gain.astype(F32)).at[1].set(key_gain.astype(F32))
+
+    def by_rank(w):
+        return jnp.moveaxis(w.reshape(shard, inner, w.shape[1] // inner), 1, 0)
+
+    gains = jnp.zeros((shard, 128), BF).at[:, 0].set(attn_gain).at[:, 1].set(mlp_gain)
+    pack = jnp.concatenate(
+        [by_rank(w_query), by_rank(w_key), by_rank(w_value), by_rank(w_out.T),
+         jnp.broadcast_to(gains[None], (inner, shard, 128))], 2)
+    cols = pack.shape[2]
+    unit = hidden_units // 4
+    fold_scratch = tp_fold_scratch(length, part, halves)
+    block = width // groups
+    (attn_w, first_w, other_w, normed_one, pre, qkv, stats, mixed, middle, r_two, piece, grad_full, gain_rows) = comm_call(
+        partial(fore_kernel, groups, heads, hd), [SMEM] + [ANY] * 4 + [VMEM, ANY, VMEM, VMEM],
+        [(shape((width, cols), BF), ANY), (shape((2, width, 3 * unit), BF), ANY), (shape((2, block, 3 * unit), BF), ANY),
+         (shape((tokens, width), BF), ANY), (shape((tokens, kv), F32), VMEM), (shape((tokens, kv), BF), VMEM),
+         (shape((tokens, 128), F32), VMEM), (shape((tokens, nq), BF), VMEM), (shape((length, part), F32), VMEM),
+         (shape((length, 128), F32), VMEM), (shape((length, part), BF), VMEM), (shape((tokens, width), BF), ANY),
+         (shape((8, width), F32), VMEM)],
+        fold_scratch + [
+            pltpu.VMEM((tokens, width), BF), pltpu.VMEM((width, cols), BF), pltpu.VMEM((length, 128), F32), DMA((2,)),
+            DMA((39,)), DMA((39,)), DMA((13,)), DMA((18,)), DMA((18,)),
+            DMA((16,)), DMA((16,)), DMA((2,)), DMA((1,)), DMA((1,))], 0,
+    )(cuts, pack, w_gate, w_up, w_down.T, hidden_in, cotangent, qk_gain, table)
+    own_gains = lax.dynamic_slice(gain_rows, (0, m_index * part), (2, part))
+
+    (_, mlp_grads, _, _, mlp_back, out_parts, d_middle, d_gain_two, d_low) = comm_call(
+        partial(mlp_kernel, groups), [ANY] * 4 + [VMEM] * 4,
+        [(shape((2, width, 3 * unit), BF), ANY), (shape((4, groups, 3 * unit, block), BF), ANY),
+         (shape((3, 3, 3 * unit, block), BF), ANY), (shape((3, 3, 3 * unit, block), BF), ANY),
+         (shape((3, inner, 3 * unit, shard), BF), ANY), (shape((tokens, width), BF), ANY),
+         (shape((length, part), F32), VMEM), (shape((8, part), F32), VMEM), (shape((length, part), BF), VMEM)],
+        [pltpu.VMEM((tokens, width), BF), pltpu.VMEM((tokens, width), BF), pltpu.VMEM((4, width, 3 * unit), BF),
+         pltpu.VMEM((4, tokens, 3 * unit), BF), pltpu.VMEM((3 * unit, tokens), BF),
+         pltpu.VMEM((2, 3 * unit, block), BF), pltpu.VMEM((4, 3 * unit, block), BF), pltpu.VMEM((3 * unit, block), BF),
+         pltpu.VMEM((length, 128), F32), pltpu.VMEM((length, 128), F32), DMA((12,)),
+         DMA((8,)), DMA((8,)), DMA((1,)), DMA((12,)), DMA((12,)), DMA((18,)), DMA((18,)), DMA((12,)), DMA((12,)),
+         DMA((7,)), DMA((7,)), DMA((1,)), DMA((1,)), pltpu.SemaphoreType.REGULAR], 1,
+    )(piece, grad_full, first_w, other_w, middle, r_two, cotangent, own_gains[1:2])
+
+    d_input, block_out, attn_back, gains_out, _, _, last_back = comm_call(
+        partial(aft_kernel, groups, heads, hd), [SMEM] + [ANY] * 12 + [VMEM] * 4,
+        [(shape((length, part), F32), VMEM), (shape((length, part), BF), VMEM),
+         (shape((inner, nq + kv, block // inner), BF), ANY), (shape((8, width), F32), VMEM),
+         (shape((3, 3 * unit, block), BF), ANY), (shape((3, 3 * unit, block), BF), ANY),
+         (shape((inner, 3 * unit, shard), BF), ANY)],
+        fold_scratch + tp_reduce_scratch(length, part, halves) + [
+            pltpu.VMEM((tokens, width), BF), pltpu.VMEM((length, width), BF), pltpu.VMEM((length, kv), F32),
+            pltpu.VMEM((length, kv), BF), pltpu.VMEM((length, 128), F32), pltpu.VMEM((length, nq), BF),
+            pltpu.VMEM((length, 128), F32),
+            pltpu.VMEM((width, nq + kv), BF), pltpu.VMEM((length, part), F32), pltpu.VMEM((nq + kv, width), F32),
+            pltpu.VMEM((groups, nq + kv, block), BF),
+            pltpu.VMEM((groups - 1, nq + kv, block), BF), pltpu.VMEM((groups - 1, nq + kv, block), BF),
+            pltpu.VMEM((nq + kv, block), BF), pltpu.VMEM((length, nq), BF), pltpu.VMEM((length, kv), BF),
+            pltpu.VMEM((length, 2 * hd), F32), pltpu.VMEM((8, 2 * hd), F32),
+            pltpu.VMEM((length, 128), F32), pltpu.VMEM((length, 128), F32), pltpu.VMEM((5, 8, width), F32),
+            DMA((8,)), DMA((8,)), DMA((8,)), DMA((1,)),
+            DMA((4,)), DMA((4,)), DMA((2 * groups,)), DMA((2 * groups,)), DMA((5,)), DMA((5,)),
+            DMA((1,)), DMA((1,)), DMA((1,)),
+            pltpu.VMEM((4, 3 * unit, block), BF), pltpu.VMEM((3 * unit, block), BF), DMA((3,)),
+            DMA((6,)), DMA((6,)), DMA((4,)), DMA((4,))], 2,
+    )(cuts, d_low, normed_one, out_parts, attn_w, pre, middle, d_middle, qkv, stats, mixed, table, mlp_grads,
+      qk_gain, hidden_in, own_gains[0:1], d_gain_two)
+    all_back = jnp.concatenate([mlp_back, last_back[None]], axis=0)
+
+    def mlp_columns(first):
+        part_of = all_back[:, :, first:first + unit, :]
+        return jnp.transpose(part_of, (3, 1, 0, 2)).reshape(shard, inner * hidden_units).astype(F32)
+
+    d_down = jnp.transpose(all_back[:, :, 2 * unit:, :], (1, 0, 2, 3)).reshape(inner * hidden_units, shard).astype(F32)
+    own = lax.dynamic_slice(gains_out, (0, (t_index * inner + i_index) * shard), (2, shard))
+
+    def columns(first, last):
+        return jnp.moveaxis(attn_back[:, first:last, :], 2, 0).reshape(shard, -1).astype(F32)
+
+    return (
+        block_out, d_input, own[0], columns(0, nq), columns(nq, nq + hd), columns(nq + hd, kv),
+        gains_out[2, :hd], gains_out[2, hd:2 * hd],
+        attn_back[:, kv:kv + nq, :].reshape(inner * nq, shard).astype(F32), own[1],
+        mlp_columns(0), mlp_columns(unit), d_down,
+    )
+
+
 def solution(mesh):
     dp, halves = mesh.shape["dp"], mesh.shape["mp"]
     inner = 4
@@ -244,6 +1431,7 @@
     rows = P(("t", "i"))
     block = P(("t", "i"), "m")
     turned = P("m", ("t", "i"))
+    body = fast_body if groups == 4 and halves == 2 else plain_body
     return jax.shard_map(
         partial(body, groups=groups, inner=inner, halves=halves),
         mesh=fine,

time: 1430 us -> 745 us (0.52)
  Pallas kernels: 0 us -> 695 us
  waiting for transfers between devices: 558 us -> 0 us
  local copies, waits for them, and re-layouts: 361 us -> 23.8 us
  matrix products: 229 us -> 0 us
  blocking collectives: 162 us -> 0 us
  other arithmetic: 76.3 us -> 16.9 us
  starting transfers between devices: 15.8 us -> 0 us
  between operations: 15.6 us -> 1.05 us
    pallas_call x0 -> x3, Pallas kernels: none -> 695 us  [the longest x1 256 us: fast_body(): comm_call(partial(mlp_kernel, groups), [ANY] * 4 + [VMEM] * 4, [(shape((2...]
    all_gather x8 -> x0, waiting for transfers between devices: 306 us -> none  [the longest x4 221 us: full_rows(): return lax.all_gather(spread(local, inner), 't', axis=0, tiled=True)]
    dot_general x45 -> x0, matrix products: 229 us -> none  [the longest x17 176 us: dot_f32(): lax.dot_general(left, right, (dims, ((), ())), preferred_element_type=F32)]
    reduce_scatter x8 -> x0, waiting for transfers between devices: 209 us -> none  [the longest x4 207 us: scatter_pieces(): mine = lax.psum_scatter(parts, TP, scatter_dimension=0, tiled=False)]
    reshape x17 -> x4, local copies, waits for them, and re-layouts: 123 us -> 0.57 us  [by_rank(): return jnp.moveaxis(w.reshape(shard, inner, w.shape[1] // inner), 1, 0)]
    all_to_all x4 -> x0, blocking collectives: 86.1 us -> none  [spread(): parts = lax.all_to_all(parts, 'i', 0, 0, tiled=False)]
    dynamic_update_slice x16 -> x0, local copies, waits for them, and re-layouts: 61.7 us -> none  [body(): lax.map(partial(attend_grad, scale=scale), (query_stack, key_stack, value...]
    psum x4 -> x0, blocking collectives: 55 us -> none  [the longest x1 39.7 us: body(): small = lax.psum(small, ALL)]
  transfers between devices with their start and end apart: 20 -> 0, of which waited for: 16 -> 0; matrix products, arithmetic and copies ran while one was open for 29% -> 0% of each run, Pallas kernels for 0% -> 0%
where the time goes in v3:
time: 745 us; the launch traced here: 737 us
  Pallas kernels  695 us (93%)
  local copies, waits for them, and re-layouts  23.8 us (3%)
  other arithmetic  16.9 us (2%)
    pallas_call x1, Pallas kernels, fast_body(): comm_call(partial(mlp_kernel, groups), [ANY] * 4 + [VMEM] * 4, [(shape((2...  256 us
    pallas_call x1, Pallas kernels, fast_body(): comm_call(partial(aft_kernel, groups, heads, hd), [SMEM] + [ANY] * 12 + [...  247 us
    pallas_call x1, Pallas kernels, fast_body(): comm_call(partial(fore_kernel, groups, heads, hd), [SMEM] + [ANY] * 4 + [...  192 us

profile of v3, /device:TPU:0, one launch (start us, length us, event | category | flops | bytes accessed | tf_op | source)
XLA Modules:
  0.0 736.6 jit_solution(2022319767812899903)
XLA Ops:
  0.6 0.0 copy-start
  0.7 0.0 copy-start.6
  0.7 0.6 compare_reduce_fusion.1
  1.3 0.6 compare_reduce_fusion
  1.9 1.3 fusion.7
  3.3 1.3 fusion.6
  4.6 0.0 copy-done
  4.6 0.1 constant_dynamic-slice_fusion.2
  4.6 0.7 bitcast_convert_fusion.1
  5.3 0.1 copy.51.cuts
  5.4 0.0 copy-start.7
  5.4 0.2 slice_reduce_fusion
  5.6 0.7 pad_convert_fusion
  6.3 0.0 copy-start.8
  6.3 0.1 broadcast_bitcast_fusion
  6.5 0.1 copy.41
  6.6 1.0 copy.36
  7.5 0.1 copy.37
  7.7 1.0 copy.38
  8.6 0.1 copy.39
  8.8 0.0 copy-start.4
  8.8 1.2 copy.34
  10.0 0.2 copy.35
  10.2 0.0 copy-done.6
  10.2 0.1 copy.40
  10.4 1.1 concatenate.22.pack
  11.4 0.0 copy-done.7
  11.4 0.0 copy-done.8
  11.4 0.3 broadcast_multiply_fusion
  11.8 0.0 copy-done.4
  11.8 1.3 copy.42
  13.1 4.0 fusion.3
  17.1 1.3 pad_maximum_fusion.2.table.table_in
  18.4 192.0 %shard_map.237 = (bf16[2048,768]{1,0:T(8,128)(2,1)}, bf16[2,2048,768]{2,1,0:T(8,128)(2,1)}, bf16[2,512,768]{2,1,0:T(8,128)(2,1)}, bf16[2048,2048]{1,0:T(8,128)(2...) custom-call(s32[4,2]{1,0:T(4,128)} %copy-done.7, ...), custom_call_target="tpu_custom_call" | custom-call | tf_op jit(solution)/shard_map/pallas_call | solution.py:1355
  210.5 1.5 constant_dynamic-slice_fusion.1
  212.0 255.7 %shard_map.238 = (bf16[2,2048,768]{2,1,0:T(8,128)(2,1)}, bf16[4,4,768,512]{3,2,1,0:T(8,128)(2,1)}, bf16[3,3,768,512]{3,2,1,0:T(8,128)(2,1)}, bf16[3,3,768,512]{3...) custom-call(bf16[512,1024]{1,0:T(8,128)(2,1)} %get-tuple-element.85., ...), custom_call_target="tpu_custom_call" | custom-call | tf_op jit(solution)/shard_map/pallas_call | solution.py:1369
  467.7 247.1 %shard_map.239 = (f32[512,1024]{1,0:T(8,128)}, bf16[512,1024]{1,0:T(8,128)(2,1)}, bf16[4,640,128]{2,1,0:T(8,128)(2,1)}, f32[8,2048]{1,0:T(8,128)}, bf16[3,768,51...) custom-call(s32[4,2]{1,0:T(4,128)} %copy-done.7, ...), custom_call_target="tpu_custom_call" | custom-call | tf_op jit(solution)/shard_map/pallas_call | solution.py:1383
  714.8 0.0 copy-start.2
  714.9 0.8 constant_dynamic-slice_fusion
  715.7 1.3 slice_bitcast_fusion.1
  717.0 0.5 slice_bitcast_fusion
  717.5 0.9 slice_convert_fusion.1
  718.4 0.8 copy.48
  719.2 0.8 copy.47
  719.9 1.1 fusion.8
  721.0 1.0 copy.46
  722.0 0.8 bitcast_convert_fusion
  722.9 0.0 copy-done.2
  722.9 3.2 convert_bitcast_fusion
  726.1 1.5 copy.45
  727.6 0.1 copy.43
  727.8 1.8 copy.49
  729.6 1.7 copy.44
  731.3 0.0 copy-start.5
  731.3 1.8 copy.50
  733.1 0.0 copy-done.5
  733.1 0.0 copy-start.3
  733.1 0.0 copy-start.1
  733.1 1.0 copy.59
  734.1 1.0 copy-done.3
  735.1 1.3 copy.60
  736.4 0.0 copy-done.1
  (10 shorter events, 0.1 us)
Async XLA Ops:
  0.6 3.9 copy-start
  0.7 9.5 %copy-start.6 = (bf16[1024,128]{1,0:T(8,128)(2,1)S(1)}, bf16[1024,128]{1,0:T(8,128)(2,1)}, u32[]{:S(2)}) copy-start(bf16[1024,128]{1,0:T(8,128)(2,1)} %param.30) | copy-start | bytes 786436
  5.4 6.0 copy-start.7
  6.3 5.1 copy-start.8
  8.8 3.0 copy-start.4
  714.8 8.0 %copy-start.2 = (bf16[3,4,768,128]{3,2,1,0:T(8,128)(2,1)S(1)}, bf16[3,4,768,128]{3,2,1,0:T(8,128)(2,1)}, u32[]{:S(2)}) copy-start(bf16[3,4,768,128]{3,2,1,0:T(8,128)(2,1)} %get-tuple-element.107) | copy-start | bytes 7077892
  731.3 1.8 copy-start.5
  733.1 2.0 copy-start.3
  733.1 3.3 copy-start.1

commit v4 on v3

--- a/solution.py
+++ b/solution.py
@@ -385,10 +385,9 @@
             self.copies[k].start()
             self.loads[k].start()
 
-    def run(self):
-        own, mate, by_x, by_y, last, out, m, rows, cols, half = self.args
-        copies, ours = self.copies, self.ours
-        low, high = pl.ds(0, half), pl.ds(half, half)
+    def fold_pair(self):
+        own, mate = self.args[:2]
+        copies = self.copies
         for side, k in ((1, 0), (0, 1)):
             self.loads[k].wait()
             copies[k].wait_recv()
@@ -398,6 +397,11 @@
                 copies[4].start()
             else:
                 copies[3].start()
+
+    def fold_links(self):
+        own, mate, by_x, by_y, last, out, m, rows, cols, half = self.args
+        copies, ours = self.copies, self.ours
+        low, high = pl.ds(0, half), pl.ds(half, half)
         copies[2].wait_recv()
         add_rows(own.at[1, low, ours], own.at[1, low, ours], by_x.at[1])
         copies[5].start()
@@ -490,7 +494,8 @@
 
 
 class LineGather:
-    def __init__(self, own, full, sems, base, groups, t):
+    def __init__(self, own, full, sems, base, groups, t, near=None):
+        self.near = near
         self.own, self.full, self.sems, self.base, self.groups, self.t = own, full, sems, base, groups, t
         self.rows = full.shape[0] // groups
 
@@ -500,6 +505,8 @@
     def go(self, b, k, step, own=False):
         n = self.base + (0 if step > 0 else self.groups - 1) + k
         src = self.own if own else self.block(b)
+        if self.near is not None and k == 1:
+            src = self.near[0 if step > 0 else 1]
         return remote(src, self.block(b), self.sems, n, {"t": self.t + step})
 
     def send(self, k):
@@ -525,13 +532,14 @@
             self.go(t + k + 1, k, -1).wait_recv()
 
     def pass_on(self, k):
-        self.arrive(k - 1)
+        if self.near is None or k > 1:
+            self.arrive(k - 1)
         if k < self.groups - 1:
             self.send(k)
 
     def wait_sends(self):
         t, last = self.t, self.groups - 1
-        for k in range(self.groups - 1):
+        for k in range(0 if self.near is None else 1, self.groups - 1):
             @pl.when((t < last) & (t - k >= 0))
             def _():
                 self.go(t - k, k, 1, k == 0).wait_send()
@@ -542,10 +550,10 @@
 
 
 class LineReduce:
-    def __init__(self, grads, ups, downs, back, stage, spare, load, sems, base, move_sems, t, i, before):
+    def __init__(self, grads, ups, downs, back, stage, spare, load, sems, base, move_sems, t, i, before, early=None):
         self.grads, self.ups, self.downs, self.back, self.stage, self.spare = grads, ups, downs, back, stage, spare
         self.load, self.sems, self.base, self.move_sems = load, sems, base, move_sems
-        self.t, self.i, self.before = t, i, before
+        self.t, self.i, self.before, self.early = t, i, before, early
 
     def up(self, k, src):
         return remote(src, self.ups.at[k], self.sems, self.base + k, {"t": self.t + 1})
@@ -578,7 +586,10 @@
     def relay(self, place, way, k):
         make = self.up if way == "up" else self.down
         slots = self.ups if way == "up" else self.downs
-        make(k, slots.at[k]).wait_recv()
+        if self.early is not None and place == 0:
+            slots = self.early[0 if way == "up" else 1]
+        else:
+            make(k, slots.at[k]).wait_recv()
         self.total(place, [slots.at[k], self.grads.at[3 - k if way == "up" else k]])
         make(k, self.stage.at[place]).start()
 
@@ -633,16 +644,25 @@
             move.wait()
         keep.wait()
 
-    def wait_firsts(self):
+    def wait_firsts(self, ks=(0, 1, 2)):
         @pl.when(self.t == 0)
         def _():
-            for k in range(3):
+            for k in ks:
                 self.up(k, self.grads.at[3 - k]).wait_send()
 
         @pl.when(self.t == 3)
         def _():
-            for k in range(3):
+            for k in ks:
                 self.down(k, self.grads.at[k]).wait_send()
+
+    def wait_early(self):
+        @pl.when(self.t == 1)
+        def _():
+            self.up(0, self.ups.at[0]).wait_recv()
+
+        @pl.when(self.t == 2)
+        def _():
+            self.down(0, self.downs.at[0]).wait_recv()
 
     def wait_relays(self):
         for t, plan in self.PLAN.items():
@@ -665,9 +685,9 @@
     return wrap
 
 
-def mlp_kernel(groups, piece_in, grad_full, first_w, other_w, middle, stat, cot, gain,
-               rest_w, grads, ups, downs, back, out_parts, d_middle, d_gain, piece, *scratch):
-    (x, g, w, act, act_t, fresh, stage, spare, sums, other, load, g_send, g_recv, g_local, z_send, z_recv,
+def mlp_kernel(groups, two_full, grad_full, first_w, other_w, near_w, middle, stat, cot, gain,
+               rest_w, grads, ups, downs, next_up, next_down, back, out_parts, d_middle, d_gain, piece, *scratch):
+    (x, g, w, act, act_t, fresh, stage, spare, sums, other, load, z_send, z_recv,
      r_send, r_recv, m_send, m_recv, f_send, f_recv, s_send, s_recv, free) = scratch
     t, i, m = lax.axis_index("t"), lax.axis_index("i"), lax.axis_index("m")
     others = [{"i": flip(i, j)} for j in (1, 2, 3)]
@@ -677,42 +697,63 @@
     unit = w.shape[2] // 3
     two, three = 2 * unit, 3 * unit
     block = wide // groups
-    gather = TpGather(piece_in, x, (g_send, g_recv, g_local), 0, i, m)
-    gather.start()
-    lines = [LineGather(other_w.at[c], rest_w.at[c], (z_send, z_recv), 6 * c, groups, t) for c in range(2)]
-    lines[0].send(0)
+    sems = (z_send, z_recv)
+    lines = [
+        LineGather(other_w.at[c], rest_w.at[c], sems, 6 * c, groups, t, [near_w.at[0], near_w.at[1]] if c == 0 else None)
+        for c in range(2)
+    ]
+    lines[0].pass_on(1)
+    lines[1].send(0)
     take_g = pltpu.make_async_copy(grad_full, g, load.at[3])
+    take_x = pltpu.make_async_copy(two_full, x, load.at[8])
     take_w = [pltpu.make_async_copy(first_w.at[c], w.at[c], load.at[4 + c]) for c in range(2)]
     own = [
-        pltpu.make_async_copy(other_w.at[c], rest_w.at[c, at(t * block, block), :], load.at[6 + c]) for c in range(2)
+        pltpu.make_async_copy(other_w.at[c], w.at[2 + c, at(t * block, block), :], load.at[6 + c]) for c in range(2)
     ]
-    rest = [pltpu.make_async_copy(rest_w.at[c], w.at[2 + c], load.at[8 + c]) for c in range(2)]
-    for copy in [take_w[0], take_g, take_w[1]] + own:
+
+    def rest(c):
+        spans = [at(flip(t, j) * block, block) for j in (1, 2, 3)]
+        return [
+            pltpu.make_async_copy(rest_w.at[c, span, :], w.at[2 + c, span, :], load.at[9 + 3 * c + j])
+            for j, span in enumerate(spans)
+        ]
+
+    def fetch(c):
+        for j, copy in enumerate(rest(c)):
+            if c == 1:
+                copy.start()
+                continue
+            b = flip(t, j + 1)
+            span = at(b * block, block)
+            for step, side in ((-1, 0), (1, 1)):
+                @pl.when(b == t + step)
+                def _():
+                    pltpu.make_async_copy(near_w.at[side], w.at[2, span, :], load.at[9 + j]).start()
+
+            @pl.when((b != t - 1) & (b != t + 1))
+            def _():
+                copy.start()
+
+    first = [take_w[0], take_x, take_g, take_w[1]] + own
+    for copy in first:
         copy.start()
-    gather.relay()
-    lines[0].pass_on(1)
-    gather.relay_far()
-    lines[0].pass_on(2)
-    lines[1].send(0)
-    for copy in [take_w[0], take_g, take_w[1]] + own:
+    for copy in first:
         copy.wait()
-    gather.finish()
     reds = []
-    for c in range(3):
+    for c in range(2):
         reds.append(LineReduce(
             grads.at[c], ups.at[c], downs.at[c], back.at[c], stage, spare, load, (r_send, r_recv), 6 * c,
             (m_send, m_recv), t, i, reds[-1] if reds else None))
+    ahead = LineReduce(grads.at[2], next_up, next_down, None, stage, spare, load, (r_send, r_recv), 12,
+                       (m_send, m_recv), t, i, None)
     order = (3, 0, 2, 1)
     events = {
-        (0, 3): lambda: (lines[0].pass_on(3), rest[0].start()),
-        (1, 0): lambda: lines[1].pass_on(1),
-        (1, 3): lambda: reds[0].hop((0,)),
-        (1, 5): lambda: lines[1].pass_on(2),
-        (2, 0): lambda: reds[0].hop((1, 2)),
-        (2, 1): lambda: (lines[1].pass_on(3), rest[1].start()),
-        (2, 5): lambda: reds[0].close(),
-        (3, 0): lambda: reds[1].hop((0,)),
-        (3, 5): lambda: reds[1].hop((1, 2)),
+        (1, 0): lambda: lines[0].pass_on(2),
+        (1, 4): lambda: lines[1].pass_on(1),
+        (1, 7): lambda: (lines[0].pass_on(3), fetch(0), reds[0].hop((0,))),
+        (2, 7): lambda: (lines[1].pass_on(2), reds[0].hop((1, 2)), lines[1].pass_on(3), fetch(1)),
+        (3, 0): lambda: reds[0].close(),
+        (3, 4): lambda: reds[1].hop((0,)),
     }
 
     def hook(c, slot):
@@ -723,14 +764,15 @@
                     run()
 
     def stored(c, n):
-        return pltpu.make_async_copy(fresh.at[n % 2], grads.at[c, order[n]], load.at[10 + n % 2])
+        return pltpu.make_async_copy(fresh.at[n % 2], grads.at[c, order[n]], load.at[15 + n % 2])
 
     @pl.loop(0, 4)
     def _(c):
         for n in range(2):
             @pl.when(c == 2 + n)
             def _():
-                rest[n].wait()
+                for copy in rest(n):
+                    copy.wait()
 
         for n in range(4):
             span = pl.ds(n * rows, rows)
@@ -754,10 +796,15 @@
             for done in ((n - 1,) if n < 3 else (2, 3)):
                 if done >= 0:
                     stored(c, done).wait()
-                    for q in range(3):
+                    for q in range(2):
                         @pl.when(c == q)
                         def _():
                             reds[q].first(order[done])
+
+                    if done < 2:
+                        @pl.when(c == 2)
+                        def _():
+                            ahead.first(order[done])
             hook(c, 4 + n)
 
     for peer in tp_group(i, m):
@@ -799,14 +846,13 @@
         @pl.when(step == 1)
         def _():
             fold.send(1)
-            reds[1].close()
+            reds[1].hop((1, 2))
 
         @pl.when(step == 2)
         def _():
             fold.side(1)
 
     fold.side(0)
-    reds[2].hop((0,))
 
     def project(first):
         @pl.loop(first, first + 2)
@@ -817,14 +863,13 @@
             def _(cols):
                 act_t[0:rows, cols] = product(span, cols, two, three)
 
-            put = pltpu.make_async_copy(act_t.at[pl.ds(0, rows), :], out_parts.at[span, :], load.at[10])
+            put = pltpu.make_async_copy(act_t.at[pl.ds(0, rows), :], out_parts.at[span, :], load.at[15])
             put.start()
             put.wait()
 
     project(0)
-    fold.finish(lambda: project(2))
+    fold.finish(lambda: (project(2), reds[1].close()))
     d_gain[...] = jnp.zeros_like(d_gain)
-    reds[2].hop((1, 2))
 
     @row_loop(rows)
     def _(span):
@@ -847,11 +892,12 @@
     fold.wait_sends()
     for line in lines:
         line.wait_sends()
-    reds[2].close()
+    ahead.wait_early()
+    ahead.wait_firsts((0,))
     for red in reds:
         red.wait_firsts()
-    reds[2].wait_relays()
-    reds[2].closed()
+    reds[1].wait_relays()
+    reds[1].closed()
 
 
 def shape(dims, dtype):
@@ -890,9 +936,10 @@
 
 
 def fore_kernel(groups, heads, hd, cuts, pack, gate, up, down, hidden, cot, qk_gain, table,
-                attn, first_w, other_w, normed_out, pre, qkv, stats, mixed, middle, stat, piece, grad_full, gain_rows,
+                attn, first_w, other_w, near_w, normed_out, pre, qkv, stats, mixed, middle, stat, two_full, grad_full,
+                gain_rows,
                 *scratch):
-    fold_scratch, (full, weights, other, load, w_send, w_recv, w_local, z_send, z_recv,
+    fold_scratch, (full, weights, piece, other, load, w_send, w_recv, w_local, z_send, z_recv,
                    g_send, g_recv, g_local, s_send, s_recv) = scratch[:6], scratch[6:]
     x = full
     t, i, m = lax.axis_index("t"), lax.axis_index("i"), lax.axis_index("m")
@@ -947,6 +994,18 @@
     lines = [
         LineGather(first_w.at[c, at(t * block, block), :], first_w.at[c], sems, 6 * c + 6, groups, t) for c in range(2)
     ]
+    above = remote(other_w.at[0], near_w.at[0], sems, 18, {"t": t + 1})
+    below = remote(other_w.at[0], near_w.at[1], sems, 19, {"t": t - 1})
+
+    def near_start():
+        @pl.when(t < groups - 1)
+        def _():
+            above.start()
+
+        @pl.when(t > 0)
+        def _():
+            below.start()
+
     own.wait()
     for copy in spread:
         copy.wait_recv()
@@ -1029,13 +1088,12 @@
         @pl.when(step == 0)
         def _():
             fold.send(0)
+
+        @pl.when(step == 1)
+        def _():
+            fold.send(1)
+            lines[0].pass_on(1)
             gather_g.relay()
-
-        @pl.when(step == 1)
-        def _():
-            fold.send(1)
-            gather_g.relay_far()
-            lines[0].pass_on(1)
 
         @pl.when(step == 2)
         def _():
@@ -1044,7 +1102,8 @@
 
     fold.side(0)
     lines[0].pass_on(2)
-    fold.finish(lambda: lines[1].pass_on(2))
+    gather_g.relay_far()
+    fold.finish(lambda: (lines[1].pass_on(2), landed(2), near_start()))
 
     @row_loop(rows)
     def _(span):
@@ -1062,23 +1121,38 @@
         stat[span, :] = r
         piece[span, :] = (middle[span, :] * r[:, :1] * gain_two).astype(BF)
 
+    gather = TpGather(piece, two_full, (g_send, g_recv, g_local), 16, i, m)
+    gather.start()
     gather_g.finish()
     fold.wait_sends()
+    lines[0].pass_on(3)
+    landed(3)
     for c in range(4):
-        if c >= 2:
-            landed(c)
         for copy in chunks[c][0]:
             copy.wait_send()
     for copy in spread:
         copy.wait_send()
-    for one in lines:
-        one.pass_on(3)
+    gather.relay()
+    lines[1].pass_on(3)
+    gather.relay_far()
     for one in [line] + lines:
         one.wait_sends()
 
+    @pl.when(t > 0)
+    def _():
+        above.wait_recv()
+        below.wait_send()
+
+    @pl.when(t < groups - 1)
+    def _():
+        below.wait_recv()
+        above.wait_send()
+
+    gather.finish()
+
 
 def aft_kernel(groups, heads, hd, cuts, piece, normed, out_parts, attn, pre_in, middle, d_middle, qkv_in, stats_in,
-               mixed_in, table_in, mlp_grads, qk_gain, hidden, gain, d_gain_two,
+               mixed_in, table_in, mlp_grads, early_up, early_down, qk_gain, hidden, gain, d_gain_two,
                d_input, block_out, back, gains, ups, downs, mlp_back, *scratch):
     fold_scratch, out_scratch = scratch[:6], scratch[6:14]
     (dm, nrm, pre, qkv, stats, mixed, table, weights, res, acc, grads, up_in, down_in, total, d_mix, d_pre, d_kv, qk_sum, sums, other,
@@ -1092,10 +1166,16 @@
     scale = hd ** -0.5
     gather = TpGather(piece, dm, (a_send, a_recv, a_local), 0, i, m)
     gather.start()
-    red = LineReduce(mlp_grads.at[3], ups, downs, mlp_back, stage, spare, line_load, (r_send, r_recv), 0,
-                     (m_send, m_recv), t, i, None)
+    reds = []
+    for c in range(2):
+        reds.append(LineReduce(
+            mlp_grads.at[2 + c], ups.at[c], downs.at[c], mlp_back.at[c], stage, spare, line_load, (r_send, r_recv),
+            6 * c, (m_send, m_recv), t, i, reds[-1] if reds else None, (early_up, early_down) if c == 0 else None))
+    for b in (2, 1):
+        reds[0].first(b)
     for b in (3, 0, 2, 1):
-        red.first(b)
+        reds[1].first(b)
+    reds[0].hop((0,))
     fill = pltpu.make_async_copy(attn.at[:, pl.ds(0, kv + nq)], weights, load.at[2])
     fill.start()
 
@@ -1103,22 +1183,64 @@
         span = at(pick(step, i) * rows, rows)
         return (pltpu.make_async_copy(normed.at[span, :], nrm, load.at[0]),
                 *[pltpu.make_async_copy(src.at[span, :], dst, load.at[n]) for n, src, dst in (
-                    (1, pre_in, pre), (4, qkv_in, qkv), (5, stats_in, stats), (6, mixed_in, mixed),
+                    (1, pre_in, pre), (4, qkv_in, qkv), (5, stats_in, stats),
                     (7, table_in, table))])
 
-    take = pltpu.make_async_copy(middle, d_input, load.at[3])
-    take.start()
     two = TpReduce(out_parts, res, out_scratch, i, m)
     acc[...] = jnp.zeros_like(acc)
     qk_sum[...] = jnp.zeros_like(qk_sum)
     fold = TpFold(dm, d_input, fold_scratch, i, m)
-    fill.wait()
     gather.relay()
-    red.hop((0,))
+    reds[0].hop((1, 2))
     gather.relay_far()
     two.start()
-    red.hop((1, 2))
+    reds[0].close()
+    fill.wait()
     gather.finish()
+
+    block = wide // groups
+    spans = (slice(0, kv), slice(kv, kv + nq))
+
+    def settle(which):
+        for b in range(groups):
+            grads[b, spans[which], :] = acc[spans[which], b * block:(b + 1) * block].astype(BF)
+
+    def up(k, src, which):
+        dst = up_in.at[k, spans[which], :]
+        return remote(src, dst, (z_send, z_recv), 8 * which + k, {"t": t + 1})
+
+    def down(k, src, which):
+        dst = down_in.at[k, spans[which], :]
+        return remote(src, dst, (z_send, z_recv), 8 * which + 4 + k, {"t": t - 1})
+
+    def own_grads(b, which):
+        return grads.at[b, spans[which], :]
+
+    def begin(which):
+        @pl.when(t == 0)
+        def _():
+            for k in range(groups - 1):
+                up(k, own_grads(groups - 1 - k, which), which).start()
+
+        @pl.when(t == groups - 1)
+        def _():
+            for k in range(groups - 1):
+                down(k, own_grads(k, which), which).start()
+
+    @pl.loop(0, 4)
+    def _(s):
+        span = at(s * rows, rows)
+        take = pltpu.make_async_copy(mixed_in.at[span, :], mixed, load.at[6])
+        take.start()
+        take.wait()
+
+        @pl.loop(0, wide, step=512)
+        def _(col):
+            cols = pl.ds(pl.multiple_of(col, 512), 512)
+            acc[kv:kv + nq, cols] += tn(mixed[...], dm[span, cols])
+
+    settle(1)
+    begin(1)
 
     @pl.loop(0, 4)
     def _(step):
@@ -1176,80 +1298,53 @@
         def _(col):
             cols = pl.ds(pl.multiple_of(col, 512), 512)
             acc[0:kv, cols] += tn(d_pre[...], nrm[:, cols])
-            acc[kv:kv + nq, cols] += tn(mixed[...], dm[everything, cols])
             dm[everything, cols] = nt(d_pre[...], weights[cols, 0:kv]).astype(BF)
 
-        @pl.when(step < 2)
-        def _():
-            @pl.when(step == 0)
+        @pl.when(step == 0)
+        def _():
+            fold.send(0)
+            two.fold_pair()
+            reds[1].hop((0,))
+
+        @pl.when(step == 1)
+        def _():
+            fold.send(1)
+            reds[1].hop((1, 2))
+
+        @pl.when(step == 2)
+        def _():
+            fold.side(1)
+
+        @pl.when(step == 3)
+        def _():
+            fold.side(0)
+
+    settle(0)
+    begin(0)
+    part = hidden.shape[1]
+    kept = [acc.at[pl.ds(0, rows), pl.ds(n * part, part)] for n in range(2)]
+    takes = [pltpu.make_async_copy(src, kept[n], load.at[2 + n]) for n, src in enumerate((middle, d_middle))]
+    for take in takes:
+        take.start()
+
+    def hop(places, which):
+        for at_t, plan in LineReduce.PLAN.items():
+            @pl.when(t == at_t)
             def _():
-                fold.send(0)
-
-            @pl.when(step == 1)
-            def _():
-                fold.send(1)
-
-        @pl.when(step == 2)
-        def _():
-            fold.side(1)
-
-        @pl.when(step == 3)
-        def _():
-            fold.side(0)
-
-        @pl.when(step == 0)
-        def _():
-            two.run()
-            take.wait()
-
-            @row_loop(rows)
-            def _(span):
-                block_out[span, :] = (d_input[span, :] + res[span, :]).astype(BF)
-
-            pltpu.make_async_copy(d_middle, res, load.at[3]).start()
-            red.close()
-
-    block = wide // groups
-
-    @pl.loop(0, groups)
-    def _(b):
-        cols = at(b * block, block)
-        grads[b] = acc[:, cols].astype(BF)
-
-    def up(k, src):
-        return remote(src, up_in.at[k], (z_send, z_recv), k, {"t": t + 1})
-
-    def down(k, src):
-        return remote(src, down_in.at[k], (z_send, z_recv), groups + k, {"t": t - 1})
-
-    @pl.when(t == 0)
-    def _():
-        for k in range(groups - 1):
-            up(k, grads.at[groups - 1 - k]).start()
-
-    @pl.when(t == groups - 1)
-    def _():
-        for k in range(groups - 1):
-            down(k, grads.at[k]).start()
-
-    def hop(k):
-        b = groups - 1 - k
-
-        @pl.when((t > 0) & (b > t))
-        def _():
-            up(k, up_in.at[k]).wait_recv()
-            add_rows(up_in.at[k], up_in.at[k], grads.at[b])
-            up(k, up_in.at[k]).start()
-
-        @pl.when((t < groups - 1) & (k < t))
-        def _():
-            down(k, down_in.at[k]).wait_recv()
-            add_rows(down_in.at[k], down_in.at[k], grads.at[k])
-            down(k, down_in.at[k]).start()
-
-    hop(0)
-    pltpu.make_async_copy(d_middle, res, load.at[3]).wait()
-    fold.finish(lambda: hop(1))
+                for place, way, n in plan:
+                    if place in places:
+                        make, slots = (up, up_in) if way == "up" else (down, down_in)
+                        slot = slots.at[n, spans[which], :]
+                        make(n, slot, which).wait_recv()
+                        add_rows(slot, slot, own_grads(groups - 1 - n if way == "up" else n, which))
+                        make(n, slot, which).start()
+
+    hop((0,), 1)
+    reds[1].close()
+    for take in takes:
+        take.wait()
+    hop((1, 2), 1)
+    fold.finish(lambda: hop((0,), 0))
     gains[...] = jnp.zeros_like(gains)
     own_half = at(m * (wide // 2), wide // 2)
     gains[1:2, own_half] = d_gain_two[0:1, :]
@@ -1269,28 +1364,47 @@
     def trade(k):
         return remote(gains, g_in.at[k], (g_send, g_recv), k, ways[k])
 
-    trade(0).start()
+    def give(n):
+        trade(n).start()
+        trade(n).wait()
+        gains[...] += g_in[n]
+
+    give(0)
     swap.wait()
 
     @row_loop(rows)
     def _(span):
         r = stats[span, heads:heads + 1]
         factor = r * r * r * ((sums[span, :] + other[span, :]) / wide)[:, :1]
-        d = res[span, :] + r * (d_input[span, :] * gain[...])
+        d = kept[1][span, :] + r * (d_input[span, :] * gain[...])
         d_input[span, :] = d - hidden[span, :].astype(F32) * factor
 
-    hop(2)
+    give(1)
+    hop((1, 2), 0)
+    give(2)
+    give(3)
+    give(4)
+    two.fold_links()
+
+    @row_loop(rows)
+    def _(span):
+        block_out[span, :] = (kept[0][span, :] + res[span, :]).astype(BF)
+
     for b in range(groups):
         @pl.when(t == b)
         def _():
-            own = grads.at[b]
-            if b > 0:
-                up(groups - 1 - b, up_in.at[0]).wait_recv()
-                add_rows(total, own, up_in.at[groups - 1 - b])
-                own = total
-            if b < groups - 1:
-                down(b, down_in.at[0]).wait_recv()
-                add_rows(total, own, down_in.at[b])
+            for which in (1, 0):
+                final = total.at[spans[which], :]
+                own = own_grads(b, which)
+                if b > 0:
+                    slot = up_in.at[groups - 1 - b, spans[which], :]
+                    up(groups - 1 - b, slot, which).wait_recv()
+                    add_rows(final, own, slot)
+                    own = final
+                if b < groups - 1:
+                    slot = down_in.at[b, spans[which], :]
+                    down(b, slot, which).wait_recv()
+                    add_rows(final, own, slot)
 
     sub_cols = block // 4
     moves = []
@@ -1301,27 +1415,100 @@
     for move in moves:
         move.start()
     keep.start()
-    for k in range(5):
-        if k > 0:
-            trade(k).start()
-        trade(k).wait()
-        gains[...] += g_in[k]
-    for k in range(groups - 1):
-        @pl.when(t < groups - 1 - k)
-        def _():
-            up(k, up_in.at[k]).wait_send()
-
-        @pl.when(t > k)
-        def _():
-            down(k, down_in.at[k]).wait_send()
+    for which in range(2):
+        for k in range(groups - 1):
+            @pl.when(t < groups - 1 - k)
+            def _():
+                up(k, up_in.at[k, spans[which], :], which).wait_send()
+
+            @pl.when(t > k)
+            def _():
+                down(k, down_in.at[k, spans[which], :], which).wait_send()
 
     fold.wait_sends()
-    red.wait_firsts()
-    red.wait_relays()
-    red.closed()
+    reds[0].wait_firsts((1, 2))
+    reds[1].wait_firsts()
+    reds[1].wait_relays()
+    reds[1].closed()
     keep.wait()
     for move in moves:
         move.wait()
+
+
+class Dims:
+    def __init__(self, length, part, halves, inner, groups, hd, nq, shard, hidden_units):
+        self.length, self.part, self.halves, self.inner, self.groups, self.hd = length, part, halves, inner, groups, hd
+        self.nq, self.shard, self.heads, self.kv = nq, shard, nq // hd, nq + 2 * hd
+        self.width, self.tokens = part * halves, length * inner
+        self.unit, self.block, self.cols = hidden_units // 4, part * halves // groups, nq + 2 * hd + nq + 128
+
+    def values(self):
+        return (self.length, self.part, self.halves, self.inner, self.groups, self.hd, self.nq, self.shard,
+                self.heads, self.kv, self.width, self.tokens, self.unit, self.block, self.cols)
+
+
+def call_fore(dims, *args):
+    (length, part, halves, inner, groups, hd, nq, shard, heads, kv, width, tokens, unit, block, cols) = dims.values()
+    fold_scratch = tp_fold_scratch(length, part, halves)
+    return comm_call(
+        partial(fore_kernel, groups, heads, hd), [SMEM] + [VMEM] * 8,
+        [(shape((width, cols), BF), ANY), (shape((2, width, 3 * unit), BF), ANY), (shape((2, block, 3 * unit), BF), ANY),
+         (shape((2, block, 3 * unit), BF), ANY),
+         (shape((tokens, width), BF), ANY), (shape((tokens, kv), F32), VMEM), (shape((tokens, kv), BF), VMEM),
+         (shape((tokens, 128), F32), VMEM), (shape((tokens, nq), BF), VMEM), (shape((length, part), F32), VMEM),
+         (shape((length, 128), F32), VMEM), (shape((tokens, width), BF), ANY), (shape((tokens, width), BF), ANY),
+         (shape((8, width), F32), VMEM)],
+        fold_scratch + [
+            pltpu.VMEM((tokens, width), BF), pltpu.VMEM((width, cols), BF), pltpu.VMEM((length, part), BF),
+            pltpu.VMEM((length, 128), F32), DMA((2,)),
+            DMA((39,)), DMA((39,)), DMA((13,)), DMA((20,)), DMA((20,)),
+            DMA((24,)), DMA((24,)), DMA((3,)), DMA((1,)), DMA((1,))], 0,
+    )(*args)
+
+
+def call_mlp(dims, *args):
+    (length, part, halves, inner, groups, hd, nq, shard, heads, kv, width, tokens, unit, block, cols) = dims.values()
+    return comm_call(
+        partial(mlp_kernel, groups), [ANY] * 5 + [VMEM] * 4,
+        [(shape((2, width, 3 * unit), BF), ANY), (shape((4, groups, 3 * unit, block), BF), ANY),
+         (shape((2, 3, 3 * unit, block), BF), ANY), (shape((2, 3, 3 * unit, block), BF), ANY),
+         (shape((1, 3 * unit, block), BF), ANY), (shape((1, 3 * unit, block), BF), ANY),
+         (shape((2, inner, 3 * unit, shard), BF), ANY), (shape((tokens, width), BF), ANY),
+         (shape((length, part), F32), VMEM), (shape((8, part), F32), VMEM), (shape((length, part), BF), VMEM)],
+        [pltpu.VMEM((tokens, width), BF), pltpu.VMEM((tokens, width), BF), pltpu.VMEM((4, width, 3 * unit), BF),
+         pltpu.VMEM((4, tokens, 3 * unit), BF), pltpu.VMEM((3 * unit, tokens), BF),
+         pltpu.VMEM((2, 3 * unit, block), BF), pltpu.VMEM((4, 3 * unit, block), BF), pltpu.VMEM((3 * unit, block), BF),
+         pltpu.VMEM((length, 128), F32), pltpu.VMEM((length, 128), F32), DMA((17,)),
+         DMA((12,)), DMA((12,)), DMA((18,)), DMA((18,)), DMA((8,)), DMA((8,)),
+         DMA((7,)), DMA((7,)), DMA((1,)), DMA((1,)), pltpu.SemaphoreType.REGULAR], 1,
+    )(*args)
+
+
+def call_aft(dims, *args):
+    (length, part, halves, inner, groups, hd, nq, shard, heads, kv, width, tokens, unit, block, cols) = dims.values()
+    fold_scratch = tp_fold_scratch(length, part, halves)
+    return comm_call(
+        partial(aft_kernel, groups, heads, hd), [SMEM] + [ANY] * 14 + [VMEM] * 4,
+        [(shape((length, part), F32), VMEM), (shape((length, part), BF), VMEM),
+         (shape((inner, nq + kv, block // inner), BF), ANY), (shape((8, width), F32), VMEM),
+         (shape((2, 3, 3 * unit, block), BF), ANY), (shape((2, 3, 3 * unit, block), BF), ANY),
+         (shape((2, inner, 3 * unit, shard), BF), ANY)],
+        fold_scratch + tp_reduce_scratch(length, part, halves) + [
+            pltpu.VMEM((tokens, width), BF), pltpu.VMEM((length, width), BF), pltpu.VMEM((length, kv), F32),
+            pltpu.VMEM((length, kv), BF), pltpu.VMEM((length, 128), F32), pltpu.VMEM((length, nq), BF),
+            pltpu.VMEM((length, 128), F32),
+            pltpu.VMEM((width, nq + kv), BF), pltpu.VMEM((length, part), F32), pltpu.VMEM((nq + kv, width), F32),
+            pltpu.VMEM((groups, nq + kv, block), BF),
+            pltpu.VMEM((groups - 1, nq + kv, block), BF), pltpu.VMEM((groups - 1, nq + kv, block), BF),
+            pltpu.VMEM((nq + kv, block), BF), pltpu.VMEM((length, nq), BF), pltpu.VMEM((length, kv), BF),
+            pltpu.VMEM((length, 2 * hd), F32), pltpu.VMEM((8, 2 * hd), F32),
+            pltpu.VMEM((length, 128), F32), pltpu.VMEM((length, 128), F32), pltpu.VMEM((5, 8, width), F32),
+            DMA((8,)), DMA((8,)), DMA((8,)), DMA((1,)),
+            DMA((4,)), DMA((4,)), DMA((16,)), DMA((16,)), DMA((5,)), DMA((5,)),
+            DMA((1,)), DMA((1,)), DMA((1,)),
+            pltpu.VMEM((4, 3 * unit, block), BF), pltpu.VMEM((3 * unit, block), BF), DMA((3,)),
+            DMA((12,)), DMA((12,)), DMA((8,)), DMA((8,))], 2,
+    )(*args)
 
 
 def fast_body(
@@ -1348,62 +1535,20 @@
     pack = jnp.concatenate(
         [by_rank(w_query), by_rank(w_key), by_rank(w_value), by_rank(w_out.T),
          jnp.broadcast_to(gains[None], (inner, shard, 128))], 2)
-    cols = pack.shape[2]
-    unit = hidden_units // 4
-    fold_scratch = tp_fold_scratch(length, part, halves)
-    block = width // groups
-    (attn_w, first_w, other_w, normed_one, pre, qkv, stats, mixed, middle, r_two, piece, grad_full, gain_rows) = comm_call(
-        partial(fore_kernel, groups, heads, hd), [SMEM] + [ANY] * 4 + [VMEM, ANY, VMEM, VMEM],
-        [(shape((width, cols), BF), ANY), (shape((2, width, 3 * unit), BF), ANY), (shape((2, block, 3 * unit), BF), ANY),
-         (shape((tokens, width), BF), ANY), (shape((tokens, kv), F32), VMEM), (shape((tokens, kv), BF), VMEM),
-         (shape((tokens, 128), F32), VMEM), (shape((tokens, nq), BF), VMEM), (shape((length, part), F32), VMEM),
-         (shape((length, 128), F32), VMEM), (shape((length, part), BF), VMEM), (shape((tokens, width), BF), ANY),
-         (shape((8, width), F32), VMEM)],
-        fold_scratch + [
-            pltpu.VMEM((tokens, width), BF), pltpu.VMEM((width, cols), BF), pltpu.VMEM((length, 128), F32), DMA((2,)),
-            DMA((39,)), DMA((39,)), DMA((13,)), DMA((18,)), DMA((18,)),
-            DMA((16,)), DMA((16,)), DMA((2,)), DMA((1,)), DMA((1,))], 0,
-    )(cuts, pack, w_gate, w_up, w_down.T, hidden_in, cotangent, qk_gain, table)
+    dims = Dims(length, part, halves, inner, groups, hd, nq, shard, hidden_units)
+    unit = dims.unit
+    (attn_w, first_w, other_w, near_w, normed_one, pre, qkv, stats, mixed, middle, r_two, two_full, grad_full, gain_rows) = call_fore(
+        dims, cuts, pack, w_gate, w_up, w_down.T, hidden_in, cotangent, qk_gain, table)
+
     own_gains = lax.dynamic_slice(gain_rows, (0, m_index * part), (2, part))
 
-    (_, mlp_grads, _, _, mlp_back, out_parts, d_middle, d_gain_two, d_low) = comm_call(
-        partial(mlp_kernel, groups), [ANY] * 4 + [VMEM] * 4,
-        [(shape((2, width, 3 * unit), BF), ANY), (shape((4, groups, 3 * unit, block), BF), ANY),
-         (shape((3, 3, 3 * unit, block), BF), ANY), (shape((3, 3, 3 * unit, block), BF), ANY),
-         (shape((3, inner, 3 * unit, shard), BF), ANY), (shape((tokens, width), BF), ANY),
-         (shape((length, part), F32), VMEM), (shape((8, part), F32), VMEM), (shape((length, part), BF), VMEM)],
-        [pltpu.VMEM((tokens, width), BF), pltpu.VMEM((tokens, width), BF), pltpu.VMEM((4, width, 3 * unit), BF),
-         pltpu.VMEM((4, tokens, 3 * unit), BF), pltpu.VMEM((3 * unit, tokens), BF),
-         pltpu.VMEM((2, 3 * unit, block), BF), pltpu.VMEM((4, 3 * unit, block), BF), pltpu.VMEM((3 * unit, block), BF),
-         pltpu.VMEM((length, 128), F32), pltpu.VMEM((length, 128), F32), DMA((12,)),
-         DMA((8,)), DMA((8,)), DMA((1,)), DMA((12,)), DMA((12,)), DMA((18,)), DMA((18,)), DMA((12,)), DMA((12,)),
-         DMA((7,)), DMA((7,)), DMA((1,)), DMA((1,)), pltpu.SemaphoreType.REGULAR], 1,
-    )(piece, grad_full, first_w, other_w, middle, r_two, cotangent, own_gains[1:2])
-
-    d_input, block_out, attn_back, gains_out, _, _, last_back = comm_call(
-        partial(aft_kernel, groups, heads, hd), [SMEM] + [ANY] * 12 + [VMEM] * 4,
-        [(shape((length, part), F32), VMEM), (shape((length, part), BF), VMEM),
-         (shape((inner, nq + kv, block // inner), BF), ANY), (shape((8, width), F32), VMEM),
-         (shape((3, 3 * unit, block), BF), ANY), (shape((3, 3 * unit, block), BF), ANY),
-         (shape((inner, 3 * unit, shard), BF), ANY)],
-        fold_scratch + tp_reduce_scratch(length, part, halves) + [
-            pltpu.VMEM((tokens, width), BF), pltpu.VMEM((length, width), BF), pltpu.VMEM((length, kv), F32),
-            pltpu.VMEM((length, kv), BF), pltpu.VMEM((length, 128), F32), pltpu.VMEM((length, nq), BF),
-            pltpu.VMEM((length, 128), F32),
-            pltpu.VMEM((width, nq + kv), BF), pltpu.VMEM((length, part), F32), pltpu.VMEM((nq + kv, width), F32),
-            pltpu.VMEM((groups, nq + kv, block), BF),
-            pltpu.VMEM((groups - 1, nq + kv, block), BF), pltpu.VMEM((groups - 1, nq + kv, block), BF),
-            pltpu.VMEM((nq + kv, block), BF), pltpu.VMEM((length, nq), BF), pltpu.VMEM((length, kv), BF),
-            pltpu.VMEM((length, 2 * hd), F32), pltpu.VMEM((8, 2 * hd), F32),
-            pltpu.VMEM((length, 128), F32), pltpu.VMEM((length, 128), F32), pltpu.VMEM((5, 8, width), F32),
-            DMA((8,)), DMA((8,)), DMA((8,)), DMA((1,)),
-            DMA((4,)), DMA((4,)), DMA((2 * groups,)), DMA((2 * groups,)), DMA((5,)), DMA((5,)),
-            DMA((1,)), DMA((1,)), DMA((1,)),
-            pltpu.VMEM((4, 3 * unit, block), BF), pltpu.VMEM((3 * unit, block), BF), DMA((3,)),
-            DMA((6,)), DMA((6,)), DMA((4,)), DMA((4,))], 2,
-    )(cuts, d_low, normed_one, out_parts, attn_w, pre, middle, d_middle, qkv, stats, mixed, table, mlp_grads,
-      qk_gain, hidden_in, own_gains[0:1], d_gain_two)
-    all_back = jnp.concatenate([mlp_back, last_back[None]], axis=0)
+    (_, mlp_grads, _, _, next_up, next_down, mlp_back, out_parts, d_middle, d_gain_two, d_low) = call_mlp(
+        dims, two_full, grad_full, first_w, other_w, near_w, middle, r_two, cotangent, own_gains[1:2])
+
+    d_input, block_out, attn_back, gains_out, _, _, last_back = call_aft(
+        dims, cuts, d_low, normed_one, out_parts, attn_w, pre, middle, d_middle, qkv, stats, mixed, table, mlp_grads, next_up, next_down, qk_gain, hidden_in, own_gains[0:1], d_gain_two)
+
+    all_back = jnp.concatenate([mlp_back, last_back], axis=0)
 
     def mlp_columns(first):
         part_of = all_back[:, :, first:first + unit, :]

time: 745 us -> 651 us (0.87)
  Pallas kernels: 695 us -> 604 us
    pallas_call x3, Pallas kernels: 695 us -> 604 us  [the longest x1 204 us: call_aft(): comm_call(partial(aft_kernel, groups, heads, hd), [SMEM] + [ANY] * 14 + [...]
where the time goes in v4:
time: 651 us; the launch traced here: 646 us
  Pallas kernels  604 us (93%)
  local copies, waits for them, and re-layouts  24.7 us (4%)
  other arithmetic  15.8 us (2%)
    pallas_call x1, Pallas kernels, call_aft(): comm_call(partial(aft_kernel, groups, heads, hd), [SMEM] + [ANY] * 14 + [...  204 us
    pallas_call x1, Pallas kernels, call_fore(): comm_call(partial(fore_kernel, groups, heads, hd), [SMEM] + [VMEM] * 8, [...  203 us
    pallas_call x1, Pallas kernels, call_mlp(): comm_call(partial(mlp_kernel, groups), [ANY] * 5 + [VMEM] * 4, [(shape((2...  197 us
    unnamed x38, local copies, waits for them, and re-layouts  14.8 us

profile of v4, /device:TPU:0, one launch (start us, length us, event | category | flops | bytes accessed | tf_op | source)
XLA Modules:
  0.0 645.6 jit_solution(12774666893026547553)
XLA Ops:
  0.6 0.0 copy-start
  0.7 0.0 copy-start.7
  0.7 0.6 compare_reduce_fusion.1
  1.3 0.6 compare_reduce_fusion
  1.9 1.3 fusion.5
  3.3 1.3 fusion.4
  4.6 0.0 copy-done
  4.6 0.1 constant_dynamic-slice_fusion.2
  4.6 0.7 bitcast_convert_fusion.1
  5.3 0.1 copy.51.cuts
  5.4 0.0 copy-start.8
  5.4 0.2 slice_reduce_fusion
  5.6 0.7 pad_convert_fusion
  6.3 0.0 copy-start.9
  6.3 0.1 broadcast_bitcast_fusion
  6.5 0.1 copy.41
  6.6 1.0 copy.36
  7.5 0.1 copy.37
  7.7 1.0 copy.38
  8.6 0.1 copy.39
  8.8 0.0 copy-start.5
  8.8 1.2 copy.34
  10.0 0.2 copy.35
  10.2 0.0 copy-done.7
  10.2 0.1 copy.40
  10.4 1.1 concatenate.22.pack
  11.4 0.0 copy-done.8
  11.4 0.0 copy-done.9
  11.4 0.3 broadcast_multiply_fusion
  11.8 0.0 copy-done.5
  11.8 1.3 copy.42
  13.1 4.0 fusion.1
  17.1 1.3 pad_maximum_fusion.1.table.table_in
  18.4 203.4 %shard_map.237 = (bf16[2048,768]{1,0:T(8,128)(2,1)}, bf16[2,2048,768]{2,1,0:T(8,128)(2,1)}, bf16[2,512,768]{2,1,0:T(8,128)(2,1)}, bf16[2,512,768]{2,1,0:T(8,128)...) custom-call(s32[4,2]{1,0:T(4,128)} %copy-done.8, ...), custom_call_target="tpu_custom_call" | custom-call | tf_op jit(solution)/shard_map/pallas_call | solution.py:1453
  221.9 1.5 constant_dynamic-slice_fusion.1
  223.4 196.7 %shard_map.238 = (bf16[2,2048,768]{2,1,0:T(8,128)(2,1)}, bf16[4,4,768,512]{3,2,1,0:T(8,128)(2,1)}, bf16[2,3,768,512]{3,2,1,0:T(8,128)(2,1)}, bf16[2,3,768,512]{3...) custom-call(bf16[2048,2048]{1,0:T(8,128)(2,1)} %get-tuple-element.88, ...), custom_call_target="tpu_custom_call" | custom-call | tf_op jit(solution)/shard_map/pallas_call | solution.py:1471
  420.1 203.8 %shard_map.239 = (f32[512,1024]{1,0:T(8,128)}, bf16[512,1024]{1,0:T(8,128)(2,1)}, bf16[4,640,128]{2,1,0:T(8,128)(2,1)}, f32[8,2048]{1,0:T(8,128)}, bf16[2,3,768,...) custom-call(s32[4,2]{1,0:T(4,128)} %copy-done.8, ...), custom_call_target="tpu_custom_call" | custom-call | tf_op jit(solution)/shard_map/pallas_call | solution.py:1490
  623.9 0.0 copy-start.3
  624.0 0.8 constant_dynamic-slice_fusion
  624.8 1.3 slice_bitcast_fusion.1
  626.1 0.5 slice_bitcast_fusion
  626.6 0.9 slice_convert_fusion.1
  627.5 0.8 copy.48
  628.3 0.8 copy.47
  629.0 1.1 fusion.6
  630.1 1.0 copy.46
  631.1 0.0 copy-start.4
  631.1 0.8 bitcast_convert_fusion
  632.0 0.0 copy-done.3
  632.0 0.1 constant_dynamic-update-slice_fusion.1
  632.1 0.6 copy-done.4
  632.7 0.2 constant_dynamic-update-slice_fusion
  632.9 2.1 convert_bitcast_fusion
  635.0 1.5 copy.45
  636.5 0.1 copy.44
  636.7 1.8 copy.50
  638.5 1.7 copy.43
  640.2 0.0 copy-start.6
  640.2 1.8 copy.49
  642.1 0.0 copy-done.6
  642.1 1.0 copy.60
  643.0 1.0 copy-done.2
  644.0 1.3 copy.61
  645.3 0.0 copy-done.1
  (12 shorter events, 0.1 us)
Async XLA Ops:
  0.6 3.9 copy-start
  0.7 9.5 %copy-start.7 = (bf16[1024,128]{1,0:T(8,128)(2,1)S(1)}, bf16[1024,128]{1,0:T(8,128)(2,1)}, u32[]{:S(2)}) copy-start(bf16[1024,128]{1,0:T(8,128)(2,1)} %param.30) | copy-start | bytes 786436
  5.4 6.0 copy-start.8
  6.3 5.1 copy-start.9
  8.8 3.0 copy-start.5
  623.9 8.0 %copy-start.3 = (bf16[2,4,768,128]{3,2,1,0:T(8,128)(2,1)S(1)}, bf16[2,4,768,128]{3,2,1,0:T(8,128)(2,1)}, u32[]{:S(2)}) copy-start(bf16[2,4,768,128]{3,2,1,0:T(8,128)(2,1)} %get-tuple-element.113) | copy-start | bytes 4718596
  631.1 1.6 copy-start.4
  640.2 1.8 copy-start.6
  642.1 2.0 copy-start.2
  642.1 3.3 copy-start.1

commit v5 on v4

--- a/solution.py
+++ b/solution.py
@@ -277,7 +277,8 @@
 
 
 class TpGather:
-    def __init__(self, piece, full, sems, base, i, m):
+    def __init__(self, piece, full, sems, base, i, m, lean=False):
+        self.lean = lean
         rows, cols = piece.shape
         half = rows // 2
         core, across, along = tp_peers(i, m)
@@ -298,7 +299,7 @@
             go(piece, mine, 2, along),
             go(slot(i, 1 - m, 0), slot(i, 1 - m, 0), 3, along),
             go(slot(i, 1 - m), slot(i, 1 - m), 4, core),
-            go(slot(far, m, 1), slot(far, m, 1), 5, across),
+            go(slot(far, m, None if lean else 1), slot(far, m, None if lean else 1), 5, across),
             go(slot(far, m), slot(far, m), 6, core),
             go(slot(far, 1 - m), slot(far, 1 - m), 7, core),
         ]
@@ -310,22 +311,25 @@
 
     def relay(self):
         self.copies[1].wait_recv()
-        self.copies[3].start()
+        if not self.lean:
+            self.copies[3].start()
         self.copies[4].start()
         self.copies[2].wait_recv()
         self.copies[5].start()
         self.copies[6].start()
 
     def relay_far(self):
-        self.copies[3].wait_recv()
+        if not self.lean:
+            self.copies[3].wait_recv()
         self.copies[5].wait_recv()
         self.copies[7].start()
 
     def finish(self):
         for k in (0, 4, 6, 7):
             self.copies[k].wait_recv()
-        for copy in self.copies:
-            copy.wait_send()
+        for k, copy in enumerate(self.copies):
+            if k != 3 or not self.lean:
+                copy.wait_send()
         self.local.wait()
 
 
@@ -490,7 +494,7 @@
 
 
 def pick(step, i):
-    return jnp.where(step == 0, flip(i, 3), jnp.where(step == 1, flip(i, 1), jnp.where(step == 2, flip(i, 2), i)))
+    return jnp.where(step == 0, flip(i, 3), jnp.where(step == 1, flip(i, 2), jnp.where(step == 2, flip(i, 1), i)))
 
 
 class LineGather:
@@ -685,7 +689,7 @@
     return wrap
 
 
-def mlp_kernel(groups, two_full, grad_full, first_w, other_w, near_w, middle, stat, cot, gain,
+def mlp_kernel(groups, two_full, grad_full, first_w, other_w, near_w, middle, stat, cot, gain_rows,
                rest_w, grads, ups, downs, next_up, next_down, back, out_parts, d_middle, d_gain, piece, *scratch):
     (x, g, w, act, act_t, fresh, stage, spare, sums, other, load, z_send, z_recv,
      r_send, r_recv, m_send, m_recv, f_send, f_recv, s_send, s_recv, free) = scratch
@@ -695,6 +699,7 @@
     tokens, wide = x.shape
     rows, part = middle.shape
     unit = w.shape[2] // 3
+    gain = gain_rows[1:2, at(m * part, part)]
     two, three = 2 * unit, 3 * unit
     block = wide // groups
     sems = (z_send, z_recv)
@@ -845,12 +850,12 @@
 
         @pl.when(step == 1)
         def _():
+            fold.side(1)
+            reds[1].hop((1, 2))
+
+        @pl.when(step == 2)
+        def _():
             fold.send(1)
-            reds[1].hop((1, 2))
-
-        @pl.when(step == 2)
-        def _():
-            fold.side(1)
 
     fold.side(0)
 
@@ -874,7 +879,7 @@
     @row_loop(rows)
     def _(span):
         dn, v, r = d_middle[span, :], middle[span, :], stat[span, :]
-        sums[span, :] = jnp.broadcast_to(jnp.sum(dn * gain[...] * v, axis=-1, keepdims=True), r.shape)
+        sums[span, :] = jnp.broadcast_to(jnp.sum(dn * gain * v, axis=-1, keepdims=True), r.shape)
         d_gain[0:1, :] += jnp.sum(dn * v * r[:, :1], axis=0, keepdims=True)
 
     swap = remote(sums, other, (s_send, s_recv), 0, {"m": 1 - m})
@@ -885,7 +890,7 @@
     def _(span):
         r = stat[span, :]
         factor = (r * r * r * ((sums[span, :] + other[span, :]) / wide))[:, :1]
-        d = cot[span, :].astype(F32) + r[:, :1] * (d_middle[span, :] * gain[...]) - middle[span, :] * factor
+        d = cot[span, :].astype(F32) + r[:, :1] * (d_middle[span, :] * gain) - middle[span, :] * factor
         d_middle[span, :] = d
         piece[span, :] = d.astype(BF)
 
@@ -935,11 +940,11 @@
     return jnp.concatenate([v[:, half:], -v[:, :half]], axis=1)
 
 
-def fore_kernel(groups, heads, hd, cuts, pack, gate, up, down, hidden, cot, qk_gain, table,
-                attn, first_w, other_w, near_w, normed_out, pre, qkv, stats, mixed, middle, stat, two_full, grad_full,
+def fore_kernel(groups, heads, hd, cuts, w_query, w_key, w_value, w_out, gain_a, gain_b, gate, up, w_down, hidden,
+                cot, gain_q, gain_k, table, attn, first_w, other_w, near_w, normed_out, pre, qkv, stats, mixed, middle, stat, two_full, grad_full,
                 gain_rows,
                 *scratch):
-    fold_scratch, (full, weights, piece, other, load, w_send, w_recv, w_local, z_send, z_recv,
+    fold_scratch, (full, weights, pack, down, marks, piece, other, load, c_send, c_recv, w_send, w_recv, w_local, z_send, z_recv,
                    g_send, g_recv, g_local, s_send, s_recv) = scratch[:6], scratch[6:]
     x = full
     t, i, m = lax.axis_index("t"), lax.axis_index("i"), lax.axis_index("m")
@@ -948,16 +953,31 @@
     shard = pack.shape[1]
     unit = first_w.shape[2] // 3
     others = [{"i": flip(i, j)} for j in (1, 2, 3)]
-    meet(others + [{"m": 1 - m}] + [{"t": flip(t, j)} for j in (1, 2, 3)])
+    away = [(a, b) for a in range(4) for b in range(4) if a + b > 0]
+    places = {(a, b): {"t": flip(t, a) if a else t, "i": flip(i, b) if b else i} for a, b in away}
+    meet([{"m": 1 - m}] + [places[ab] for ab in away])
+    for p in range(4):
+        pack[p, :, 0:nq] = w_query[:, p * nq:(p + 1) * nq]
+        pack[p, :, nq:nq + hd] = w_key[:, p * hd:(p + 1) * hd]
+        pack[p, :, nq + hd:kv] = w_value[:, p * hd:(p + 1) * hd]
+        pack[p, :, kv:kv + nq] = w_out[p * nq:(p + 1) * nq, :].T
     mine = attn.at[at((t * 4 + i) * shard, shard), :]
     spread = [remote(pack.at[flip(i, j)], mine, (w_send, w_recv), j - 1, others[j - 1]) for j in (2, 3, 1)]
     own = pltpu.make_async_copy(pack.at[i], mine, w_local.at[0])
     for copy in spread:
         copy.start()
     own.start()
-    gather_h = TpGather(hidden, full, (g_send, g_recv, g_local), 0, i, m)
-    gather_g = TpGather(cot, grad_full, (g_send, g_recv, g_local), 8, i, m)
+    gather_h = TpGather(hidden, full, (g_send, g_recv, g_local), 0, i, m, True)
+    gather_g = TpGather(cot, grad_full, (g_send, g_recv, g_local), 8, i, m, True)
     gather_h.start()
+    here = t * 4 + i
+    marks[here] = jnp.concatenate([gain_a[...], gain_b[...], jnp.zeros((14, shard), BF)], axis=0)
+    mark = [remote(marks.at[here], marks.at[here], (c_send, c_recv), 4 * a + b, places[(a, b)]) for a, b in away]
+    for copy in mark:
+        copy.start()
+    for r in range(0, w_down.shape[0], 512):
+        down[:, r:r + 512] = w_down[r:r + 512, :].T
+    gq, gk = gain_q[...].astype(F32), gain_k[...].astype(F32)
 
     def chunk(c):
         if c < 2:
@@ -1011,6 +1031,18 @@
         copy.wait_recv()
     line.send(0)
     begin(0)
+    lane = lax.rem(lax.broadcasted_iota(jnp.int32, (1, hd), 1), hd // 2).astype(F32)
+    freqs = jnp.exp(lane * (-math.log(1000000.0) * 2.0 / hd))
+
+    @pl.loop(0, 4)
+    def _(s):
+        c1, c2 = cuts[t * 4 + s, 0], cuts[t * 4 + s, 1]
+        position = lax.broadcasted_iota(jnp.int32, (rows, hd), 0)
+        start = jnp.where(position >= c2, c2, jnp.where(position >= c1, c1, 0))
+        angle = (position - start).astype(F32) * freqs
+        table[at(s * rows, rows), 0:hd] = jnp.cos(angle)
+        table[at(s * rows, rows), hd:2 * hd] = jnp.sin(angle)
+
     line.pass_on(1)
     gather_h.relay()
     begin(1)
@@ -1028,8 +1060,10 @@
     fill.start()
     gather_h.finish()
     fill.wait()
-    gain_rows[...] = jnp.transpose(weights[:, kv + nq:kv + nq + 128].astype(F32))[0:8, :]
-    gain = gain_rows[0:1, :]
+    for copy in mark:
+        copy.wait()
+    for n in range(4 * groups):
+        gain_rows[:, n * shard:(n + 1) * shard] = marks[n].astype(F32)[0:8, :]
     gain_two = gain_rows[1:2, at(m * (wide // 2), wide // 2)]
     parts = full
     fold = TpFold(parts, middle, fold_scratch, i, m)
@@ -1041,7 +1075,7 @@
         def sub(r, size):
             return pl.ds(pl.multiple_of(start + r, size), size)
 
-        cut = (cuts[s, 0], cuts[s, 1])
+        cut = (cuts[t * 4 + s, 0], cuts[t * 4 + s, 1])
 
         @pl.loop(0, rows, step=64)
         def _(r):
@@ -1059,7 +1093,7 @@
         c, sn = table[everything, 0:hd], table[everything, hd:2 * hd]
         for h in range(heads + 1):
             lanes = slice(h * hd, (h + 1) * hd)
-            n = rms_rows(heads_pre[:, lanes], qk_gain[0:1, :] if h < heads else qk_gain[1:2, :])
+            n = rms_rows(heads_pre[:, lanes], gq if h < heads else gk)
             qkv[everything, lanes] = (n * c + turn(n) * sn).astype(BF)
         qkv[everything, nq + hd:kv] = heads_pre[:, nq + hd:kv].astype(BF)
         half = rows // 2
@@ -1091,14 +1125,14 @@
 
         @pl.when(step == 1)
         def _():
+            fold.side(1)
+            lines[0].pass_on(1)
+
+        @pl.when(step == 2)
+        def _():
             fold.send(1)
-            lines[0].pass_on(1)
+            lines[1].pass_on(1)
             gather_g.relay()
-
-        @pl.when(step == 2)
-        def _():
-            fold.side(1)
-            lines[1].pass_on(1)
 
     fold.side(0)
     lines[0].pass_on(2)
@@ -1152,7 +1186,7 @@
 
 
 def aft_kernel(groups, heads, hd, cuts, piece, normed, out_parts, attn, pre_in, middle, d_middle, qkv_in, stats_in,
-               mixed_in, table_in, mlp_grads, early_up, early_down, qk_gain, hidden, gain, d_gain_two,
+               mixed_in, table_in, mlp_grads, early_up, early_down, gain_q, gain_k, hidden, gain_rows, d_gain_two,
                d_input, block_out, back, gains, ups, downs, mlp_back, *scratch):
     fold_scratch, out_scratch = scratch[:6], scratch[6:14]
     (dm, nrm, pre, qkv, stats, mixed, table, weights, res, acc, grads, up_in, down_in, total, d_mix, d_pre, d_kv, qk_sum, sums, other,
@@ -1164,6 +1198,8 @@
     rows, wide = hidden.shape[0], dm.shape[1]
     nq, kv = heads * hd, (heads + 2) * hd
     scale = hd ** -0.5
+    gain = gain_rows[0:1, at(m * (wide // 2), wide // 2)]
+    qk_gain = (gain_q[...].astype(F32), gain_k[...].astype(F32))
     gather = TpGather(piece, dm, (a_send, a_recv, a_local), 0, i, m)
     gather.start()
     reds = []
@@ -1176,7 +1212,7 @@
     for b in (3, 0, 2, 1):
         reds[1].first(b)
     reds[0].hop((0,))
-    fill = pltpu.make_async_copy(attn.at[:, pl.ds(0, kv + nq)], weights, load.at[2])
+    fill = pltpu.make_async_copy(attn, weights, load.at[2])
     fill.start()
 
     def fetch(step):
@@ -1196,6 +1232,8 @@
     two.start()
     reds[0].close()
     fill.wait()
+    for copy in fetch(0)[1:]:
+        copy.start()
     gather.finish()
 
     block = wide // groups
@@ -1246,13 +1284,12 @@
     def _(step):
         s = pick(step, i)
         start = s * rows
-        for copy in fetch(step):
-            copy.start()
+        fetch(step)[0].start()
 
         def sub(r, size):
             return pl.ds(pl.multiple_of(start + r, size), size)
 
-        cut = (cuts[s, 0], cuts[s, 1])
+        cut = (cuts[t * 4 + s, 0], cuts[t * 4 + s, 1])
         everything = sub(0, rows)
         d_mix[...] = nn(dm[everything, :], weights[:, kv:kv + nq]).astype(BF)
         d_kv[...] = jnp.zeros_like(d_kv)
@@ -1266,7 +1303,7 @@
             v = pre[:, lanes]
             r = lax.rsqrt(jnp.mean(v * v, axis=-1, keepdims=True) + EPS)
             qk_sum[0:1, row * hd:(row + 1) * hd] += jnp.sum(u * v * r, axis=0, keepdims=True)
-            scaled = u * qk_gain[row:row + 1, :]
+            scaled = u * qk_gain[row]
             undone = r * scaled - v * (r * r * r) * jnp.mean(scaled * v, axis=-1, keepdims=True)
             d_pre[:, lanes] = undone.astype(BF)
 
@@ -1292,6 +1329,12 @@
             undo(h, jnp.concatenate(found, axis=0))
         undo(heads, d_kv[:, 0:hd])
         d_pre[:, nq + hd:kv] = d_kv[:, hd:2 * hd].astype(BF)
+
+        @pl.when(step < 3)
+        def _():
+            for copy in fetch(step + 1)[1:]:
+                copy.start()
+
         fetch(step)[0].wait()
 
         @pl.loop(0, wide, step=512)
@@ -1308,12 +1351,12 @@
 
         @pl.when(step == 1)
         def _():
+            fold.side(1)
+            reds[1].hop((1, 2))
+
+        @pl.when(step == 2)
+        def _():
             fold.send(1)
-            reds[1].hop((1, 2))
-
-        @pl.when(step == 2)
-        def _():
-            fold.side(1)
 
         @pl.when(step == 3)
         def _():
@@ -1354,7 +1397,7 @@
     def _(span):
         dn, v = d_input[span, :], hidden[span, :].astype(F32)
         r = stats[span, heads:heads + 1]
-        sums[span, :] = jnp.broadcast_to(jnp.sum(dn * gain[...] * v, axis=-1, keepdims=True), sums[span, :].shape)
+        sums[span, :] = jnp.broadcast_to(jnp.sum(dn * gain * v, axis=-1, keepdims=True), sums[span, :].shape)
         gains[0:1, own_half] += jnp.sum(dn * v * r, axis=0, keepdims=True)
 
     swap = remote(sums, other, (s_send, s_recv), 0, {"m": 1 - m})
@@ -1376,7 +1419,7 @@
     def _(span):
         r = stats[span, heads:heads + 1]
         factor = r * r * r * ((sums[span, :] + other[span, :]) / wide)[:, :1]
-        d = kept[1][span, :] + r * (d_input[span, :] * gain[...])
+        d = kept[1][span, :] + r * (d_input[span, :] * gain)
         d_input[span, :] = d - hidden[span, :].astype(F32) * factor
 
     give(1)
@@ -1440,7 +1483,7 @@
         self.length, self.part, self.halves, self.inner, self.groups, self.hd = length, part, halves, inner, groups, hd
         self.nq, self.shard, self.heads, self.kv = nq, shard, nq // hd, nq + 2 * hd
         self.width, self.tokens = part * halves, length * inner
-        self.unit, self.block, self.cols = hidden_units // 4, part * halves // groups, nq + 2 * hd + nq + 128
+        self.unit, self.block, self.cols = hidden_units // 4, part * halves // groups, nq + 2 * hd + nq
 
     def values(self):
         return (self.length, self.part, self.halves, self.inner, self.groups, self.hd, self.nq, self.shard,
@@ -1451,16 +1494,18 @@
     (length, part, halves, inner, groups, hd, nq, shard, heads, kv, width, tokens, unit, block, cols) = dims.values()
     fold_scratch = tp_fold_scratch(length, part, halves)
     return comm_call(
-        partial(fore_kernel, groups, heads, hd), [SMEM] + [VMEM] * 8,
-        [(shape((width, cols), BF), ANY), (shape((2, width, 3 * unit), BF), ANY), (shape((2, block, 3 * unit), BF), ANY),
+        partial(fore_kernel, groups, heads, hd), [SMEM] + [VMEM] * 13,
+        [(shape((tokens, 2 * hd), F32), VMEM), (shape((width, cols), BF), ANY), (shape((2, width, 3 * unit), BF), ANY), (shape((2, block, 3 * unit), BF), ANY),
          (shape((2, block, 3 * unit), BF), ANY),
          (shape((tokens, width), BF), ANY), (shape((tokens, kv), F32), VMEM), (shape((tokens, kv), BF), VMEM),
          (shape((tokens, 128), F32), VMEM), (shape((tokens, nq), BF), VMEM), (shape((length, part), F32), VMEM),
          (shape((length, 128), F32), VMEM), (shape((tokens, width), BF), ANY), (shape((tokens, width), BF), ANY),
          (shape((8, width), F32), VMEM)],
         fold_scratch + [
-            pltpu.VMEM((tokens, width), BF), pltpu.VMEM((width, cols), BF), pltpu.VMEM((length, part), BF),
-            pltpu.VMEM((length, 128), F32), DMA((2,)),
+            pltpu.VMEM((tokens, width), BF), pltpu.VMEM((width, cols), BF), pltpu.VMEM((inner, shard, cols), BF),
+            pltpu.VMEM((shard, 4 * inner * unit), BF), pltpu.VMEM((inner * groups, 16, shard), BF),
+            pltpu.VMEM((length, part), BF),
+            pltpu.VMEM((length, 128), F32), DMA((2,)), DMA((16,)), DMA((16,)),
             DMA((39,)), DMA((39,)), DMA((13,)), DMA((20,)), DMA((20,)),
             DMA((24,)), DMA((24,)), DMA((3,)), DMA((1,)), DMA((1,))], 0,
     )(*args)
@@ -1488,7 +1533,7 @@
     (length, part, halves, inner, groups, hd, nq, shard, heads, kv, width, tokens, unit, block, cols) = dims.values()
     fold_scratch = tp_fold_scratch(length, part, halves)
     return comm_call(
-        partial(aft_kernel, groups, heads, hd), [SMEM] + [ANY] * 14 + [VMEM] * 4,
+        partial(aft_kernel, groups, heads, hd), [SMEM] + [ANY] * 14 + [VMEM] * 5,
         [(shape((length, part), F32), VMEM), (shape((length, part), BF), VMEM),
          (shape((inner, nq + kv, block // inner), BF), ANY), (shape((8, width), F32), VMEM),
          (shape((2, 3, 3 * unit, block), BF), ANY), (shape((2, 3, 3 * unit, block), BF), ANY),
@@ -1522,31 +1567,21 @@
     heads = w_query.shape[1] // inner // hd
     nq, kv = heads * hd, (heads + 2) * hd
     hidden_units = w_gate.shape[1] // inner
-    t_index, i_index, m_index = lax.axis_index("t"), lax.axis_index("i"), lax.axis_index("m")
-    cuts = lax.dynamic_slice_in_dim(doc_starts, t_index * inner, inner, 0)
-    cosine, sine_table, _ = jax.vmap(partial(tables, length=length, head_dim=hd))(cuts)
-    table = jnp.concatenate([cosine.reshape(tokens, hd), sine_table.reshape(tokens, hd)], axis=1)
-    qk_gain = jnp.zeros((8, hd), F32).at[0].set(query_gain.astype(F32)).at[1].set(key_gain.astype(F32))
-
-    def by_rank(w):
-        return jnp.moveaxis(w.reshape(shard, inner, w.shape[1] // inner), 1, 0)
-
-    gains = jnp.zeros((shard, 128), BF).at[:, 0].set(attn_gain).at[:, 1].set(mlp_gain)
-    pack = jnp.concatenate(
-        [by_rank(w_query), by_rank(w_key), by_rank(w_value), by_rank(w_out.T),
-         jnp.broadcast_to(gains[None], (inner, shard, 128))], 2)
+    t_index, i_index = lax.axis_index("t"), lax.axis_index("i")
+    gain_q, gain_k = query_gain[None], key_gain[None]
     dims = Dims(length, part, halves, inner, groups, hd, nq, shard, hidden_units)
     unit = dims.unit
-    (attn_w, first_w, other_w, near_w, normed_one, pre, qkv, stats, mixed, middle, r_two, two_full, grad_full, gain_rows) = call_fore(
-        dims, cuts, pack, w_gate, w_up, w_down.T, hidden_in, cotangent, qk_gain, table)
-
-    own_gains = lax.dynamic_slice(gain_rows, (0, m_index * part), (2, part))
+    (table, attn_w, first_w, other_w, near_w, normed_one, pre, qkv, stats, mixed, middle, r_two, two_full, grad_full,
+     gain_rows) = call_fore(
+        dims, doc_starts, w_query, w_key, w_value, w_out, attn_gain[None], mlp_gain[None], w_gate, w_up, w_down,
+        hidden_in, cotangent, gain_q, gain_k)
 
     (_, mlp_grads, _, _, next_up, next_down, mlp_back, out_parts, d_middle, d_gain_two, d_low) = call_mlp(
-        dims, two_full, grad_full, first_w, other_w, near_w, middle, r_two, cotangent, own_gains[1:2])
+        dims, two_full, grad_full, first_w, other_w, near_w, middle, r_two, cotangent, gain_rows)
 
     d_input, block_out, attn_back, gains_out, _, _, last_back = call_aft(
-        dims, cuts, d_low, normed_one, out_parts, attn_w, pre, middle, d_middle, qkv, stats, mixed, table, mlp_grads, next_up, next_down, qk_gain, hidden_in, own_gains[0:1], d_gain_two)
+        dims, doc_starts, d_low, normed_one, out_parts, attn_w, pre, middle, d_middle, qkv, stats, mixed, table, mlp_grads, next_up, next_down, gain_q, gain_k,
+        hidden_in, gain_rows, d_gain_two)
 
     all_back = jnp.concatenate([mlp_back, last_back], axis=0)
 

time: 651 us -> 619 us (0.951)
  Pallas kernels: 604 us -> 590 us
  other arithmetic: 15.8 us -> 3.7 us
    pallas_call x1, Pallas kernels: 197 us -> 180 us  [call_mlp(): comm_call(partial(mlp_kernel, groups), [ANY] * 5 + [VMEM] * 4, [(shape((2...]
    unnamed x38 -> x17, local copies, waits for them, and re-layouts: 14.8 us -> 12.5 us
where the time goes in v5:
time: 619 us; the launch traced here: 615 us
  Pallas kernels  590 us (95%)
  local copies, waits for them, and re-layouts  20.3 us (3%)
    pallas_call x1, Pallas kernels, call_aft(): comm_call(partial(aft_kernel, groups, heads, hd), [SMEM] + [ANY] * 14 + [...  210 us
    pallas_call x1, Pallas kernels, call_fore(): comm_call(partial(fore_kernel, groups, heads, hd), [SMEM] + [VMEM] * 13,...  201 us
    pallas_call x1, Pallas kernels, call_mlp(): comm_call(partial(mlp_kernel, groups), [ANY] * 5 + [VMEM] * 4, [(shape((2...  180 us
    unnamed x17, local copies, waits for them, and re-layouts  12.5 us

profile of v5, /device:TPU:0, one launch (start us, length us, event | category | flops | bytes accessed | tf_op | source)
XLA Modules:
  0.0 615.1 jit_solution(470329332068446621)
XLA Ops:
  0.6 1.4 copy.33.cuts
  2.0 200.8 %shard_map.237 = (f32[2048,128]{1,0:T(8,128)}, bf16[2048,640]{1,0:T(8,128)(2,1)}, bf16[2,2048,768]{2,1,0:T(8,128)(2,1)}, bf16[2,512,768]{2,1,0:T(8,128)(2,1)}, b...) custom-call(s32[16,2]{1,0:T(8,128)} %copy.33.cuts, ...), custom_call_target="tpu_custom_call" | custom-call | tf_op jit(solution)/shard_map/pallas_call | solution.py:1496
  202.8 179.5 %shard_map.238 = (bf16[2,2048,768]{2,1,0:T(8,128)(2,1)}, bf16[4,4,768,512]{3,2,1,0:T(8,128)(2,1)}, bf16[2,3,768,512]{3,2,1,0:T(8,128)(2,1)}, bf16[2,3,768,512]{3...) custom-call(bf16[2048,2048]{1,0:T(8,128)(2,1)} %get-tuple-element.41, ...), custom_call_target="tpu_custom_call" | custom-call | tf_op jit(solution)/shard_map/pallas_call | solution.py:1516
  382.3 0.0 copy-start.1
  382.3 209.9 %shard_map.239 = (f32[512,1024]{1,0:T(8,128)}, bf16[512,1024]{1,0:T(8,128)(2,1)}, bf16[4,640,128]{2,1,0:T(8,128)(2,1)}, f32[8,2048]{1,0:T(8,128)}, bf16[2,3,768,...) custom-call(s32[16,2]{1,0:T(8,128)} %copy.33.cuts, ...), custom_call_target="tpu_custom_call" | custom-call | tf_op jit(solution)/shard_map/pallas_call | solution.py:1535
  592.3 0.0 copy-start.2
  592.3 0.0 copy-done.1
  592.3 0.1 constant_dynamic-update-slice_fusion.1
  592.4 1.3 copy-done.2
  593.7 0.2 constant_dynamic-update-slice_fusion
  593.9 2.8 convert_bitcast_fusion
  596.7 0.1 copy.34
  596.8 1.8 copy.40
  598.6 1.7 copy.35
  600.4 1.8 copy.41
  602.2 0.0 copy-start.3
  602.2 3.2 copy.36
  605.4 0.0 copy-done.3
  605.4 0.1 fusion
  605.4 0.8 bitcast_convert_fusion
  606.3 0.0 copy-start
  606.3 1.0 copy.37
  607.3 0.8 copy.38
  608.0 0.8 copy.39
  608.8 0.7 constant_dynamic-slice_fusion
  609.5 0.5 slice_bitcast_fusion
  610.0 1.3 slice_bitcast_fusion.1
  611.3 2.3 copy.45
  613.6 0.0 copy-done
  613.6 1.3 copy.46
  (1 shorter events, 0.0 us)
Async XLA Ops:
  382.3 210.0 %copy-start.1 = (bf16[2,4,768,128]{3,2,1,0:T(8,128)(2,1)S(1)}, bf16[2,4,768,128]{3,2,1,0:T(8,128)(2,1)}, u32[]{:S(2)}) copy-start(bf16[2,4,768,128]{3,2,1,0:T(8,128)(2,1)} %get-tuple-element.67) | copy-start | bytes 4718596
  592.3 1.4 copy-start.2
  602.2 3.2 copy-start.3
  606.3 7.3 %copy-start = (f32[512,1024]{1,0:T(8,128)S(1)}, f32[512,1024]{1,0:T(8,128)}, u32[]{:S(2)}) copy-start(f32[512,1024]{1,0:T(8,128)} %get-tuple-element.120) | copy-start | bytes 6291460
